TPU v7x, 32 devices: a whole 2x2x4 slice. The times are simulated.
32 devices in a mesh: dp: 8 (over z, x), space: 4 (over y, core).
Axes of the slice: x: 2, y: 2, z: 4, core: 2. Of those that a mesh axis runs over, the one named last changes fastest.
Arguments:
- images: bfloat16 [256, 24, 24, 384], P('dp', 'space'), may hold values from -6 to 6
- cotangent: bfloat16 [256, 24, 24, 384], P('dp', 'space'), may hold values from -6 to 6
- image_sides: int32 [256], P('dp'), may hold values from 14 to 24, as said below
- keep_flags: int32 [256], P('dp'), may hold values 0 or 1
- depth_kernel: float32 [49, 384], P(None, ('dp', 'space')), may hold values from -0.875 to 0.875
- kernel_moment: float32 [49, 384], P(None, ('dp', 'space')), may hold values from -0.00061035156 to 0.00061035156
- kernel_square: float32 [49, 384], P(None, ('dp', 'space')), may hold values from 4.1600107e-10 to 6.656017e-09
- block_vectors: float32 [5, 384], P(None, ('dp', 'space')), may hold values from -1.5 to 1.5
- vector_moment: float32 [5, 384], P(None, ('dp', 'space')), may hold values from -0.00061035156 to 0.00061035156
- vector_square: float32 [5, 384], P(None, ('dp', 'space')), may hold values from 4.1600107e-10 to 6.656017e-09
- up_weight: float32 [384, 1536], P(None, ('dp', 'space')), may hold values from -0.3125 to 0.3125
- up_moment: float32 [384, 1536], P(None, ('dp', 'space')), may hold values from -0.00061035156 to 0.00061035156
- up_square: float32 [384, 1536], P(None, ('dp', 'space')), may hold values from 4.1600107e-10 to 6.656017e-09
- up_bias: float32 [1536], P(('dp', 'space')), may hold values from -3 to 3
- bias_moment: float32 [1536], P(('dp', 'space')), may hold values from -0.00061035156 to 0.00061035156
- bias_square: float32 [1536], P(('dp', 'space')), may hold values from 4.1600107e-10 to 6.656017e-09
- down_weight: float32 [1536, 384], P(('dp', 'space')), may hold values from -0.15625 to 0.15625
- down_moment: float32 [1536, 384], P(('dp', 'space')), may hold values from -0.00061035156 to 0.00061035156
- down_square: float32 [1536, 384], P(('dp', 'space')), may hold values from 4.1600107e-10 to 6.656017e-09
Outputs:
- out_images: bfloat16 [256, 24, 24, 384], P('dp', 'space')
- grad_images: bfloat16 [256, 24, 24, 384], P('dp', 'space')
- new_kernel: float32 [49, 384], P(None, ('dp', 'space'))
- new_kernel_moment: float32 [49, 384], P(None, ('dp', 'space'))
- new_kernel_square: float32 [49, 384], P(None, ('dp', 'space'))
- new_vectors: float32 [5, 384], P(None, ('dp', 'space'))
- new_vector_moment: float32 [5, 384], P(None, ('dp', 'space'))
- new_vector_square: float32 [5, 384], P(None, ('dp', 'space'))
- new_up: float32 [384, 1536], P(None, ('dp', 'space'))
- new_up_moment: float32 [384, 1536], P(None, ('dp', 'space'))
- new_up_square: float32 [384, 1536], P(None, ('dp', 'space'))
- new_bias: float32 [1536], P(('dp', 'space'))
- new_bias_moment: float32 [1536], P(('dp', 'space'))
- new_bias_square: float32 [1536], P(('dp', 'space'))
- new_down: float32 [1536, 384], P(('dp', 'space'))
- new_down_moment: float32 [1536, 384], P(('dp', 'space'))
- new_down_square: float32 [1536, 384], P(('dp', 'space'))
- grad_norm: float32 [], replicated
Inputs may be any that keep to these rules, and one draw needn't show every extreme that they name: `image_sides`: each image's valid square has one of the sides 24, 18, 14.
All inputs are finite; a program needn't handle non-finite values. No bound on the sum of `keep_flags` on one device may be relied on, other than what follows from the above.
Results may differ from a plain program's by a relative error of at most 0.0055.
Values may be sent and summed in bfloat16 or wider, within the bound.
No kernel may reach another device: no remote copies, remote signals or barrier semaphores. Data moves between devices by JAX's collectives and lax.ppermute only.
A program may use at most 192 MiB of HBM per device.

v0:
```python
import jax
import jax.numpy as jnp
from jax import lax
from jax.sharding import PartitionSpec as P

STEP = 5


keep_scale = 4.0 / 3.0
norm_eps = 1e-06
clip_limit = 1.0
beta_one = 0.9
beta_two = 0.999
adam_eps = 1e-08
decay_rate = 0.05
step_rates = (0.15, 0.5, 0.05, 0.2, 0.025)
inv_root_two = 0.7071067811865476
inv_root_tau = 0.3989422804014327


def conv_rows(padded, kernel, out_rows, out_cols):
    wide = jnp.pad(padded, ((0, 0), (0, 0), (3, 3), (0, 0)))
    running = jnp.zeros((padded.shape[0], out_rows, out_cols, padded.shape[3]), jnp.float32)
    for row_off in range(7):
        for col_off in range(7):
            running = (
                running
                + kernel[row_off * 7 + col_off]
                * wide[:, row_off : row_off + out_rows, col_off : col_off + out_cols, :]
            )
    return running


def kernel_grad(padded, grad_conv):
    wide = jnp.pad(padded, ((0, 0), (0, 0), (3, 3), (0, 0)))
    out_rows = grad_conv.shape[1]
    out_cols = grad_conv.shape[2]
    pieces = [
        jnp.sum(
            wide[:, row_off : row_off + out_rows, col_off : col_off + out_cols, :] * grad_conv,
            axis=(0, 1, 2),
        )
        for row_off in range(7)
        for col_off in range(7)
    ]
    return jnp.stack(pieces)


def adam_update(weight, moment, square, grad_part, factor, step_rate):
    scaled = grad_part * factor
    new_moment = beta_one * moment + (1.0 - beta_one) * scaled
    new_square = beta_two * square + (1.0 - beta_two) * scaled * scaled
    corrected = new_moment / (1.0 - beta_one**STEP)
    spread = jnp.sqrt(new_square / (1.0 - beta_two**STEP))
    new_weight = weight - step_rate * (corrected / (spread + adam_eps) + decay_rate * weight)
    return (new_weight, new_moment, new_square)


def body(
    images,
    cotangent,
    image_sides,
    keep_flags,
    depth_kernel,
    kernel_moment,
    kernel_square,
    block_vectors,
    vector_moment,
    vector_square,
    up_weight,
    up_moment,
    up_square,
    up_bias,
    bias_moment,
    bias_square,
    down_weight,
    down_moment,
    down_square,
):
    up_full, down_full = (
        lax.all_gather(up_weight.astype(jnp.bfloat16), ("dp", "space"), axis=1, tiled=True),
        lax.all_gather(down_weight.astype(jnp.bfloat16), ("dp", "space"), axis=0, tiled=True),
    )
    kernel_full, vector_full, bias_full = (
        lax.all_gather(depth_kernel, ("dp", "space"), axis=1, tiled=True),
        lax.all_gather(block_vectors, ("dp", "space"), axis=1, tiled=True),
        lax.all_gather(up_bias, ("dp", "space"), axis=0, tiled=True),
    )
    map_side = images.shape[2]
    local_images, local_cot = (
        lax.all_to_all(images, "space", split_axis=0, concat_axis=1, tiled=True),
        lax.all_to_all(cotangent, "space", split_axis=0, concat_axis=1, tiled=True),
    )
    img_count = local_images.shape[0]
    first_image = lax.axis_index("space") * img_count
    local_sides = lax.dynamic_slice_in_dim(image_sides, first_image, img_count)
    local_keep = lax.dynamic_slice_in_dim(keep_flags, first_image, img_count)
    row_ids = jnp.arange(map_side, dtype=jnp.int32)
    col_ids = jnp.arange(map_side, dtype=jnp.int32)
    rows_in = row_ids[None, :] < local_sides[:, None]
    cols_in = col_ids[None, :] < local_sides[:, None]
    pixel_mask = (rows_in[:, :, None] & cols_in[:, None, :]).astype(jnp.float32)
    branch_scale = pixel_mask * (local_keep.astype(jnp.float32) * keep_scale)[:, None, None]
    masked = local_images * pixel_mask.astype(jnp.bfloat16)[..., None]
    padded = jnp.pad(masked, ((0, 0), (3, 3), (0, 0), (0, 0)))
    out_rows = local_images.shape[1]
    conv = conv_rows(padded, kernel_full, out_rows, map_side) + vector_full[0]
    chan_mean = jnp.mean(conv, axis=-1, keepdims=True)
    centred = conv - chan_mean
    chan_var = jnp.mean(centred * centred, axis=-1, keepdims=True)
    inv_std = lax.rsqrt(chan_var + norm_eps)
    unit_norm = centred * inv_std
    normed = (unit_norm * vector_full[1] + vector_full[2]).astype(jnp.bfloat16)
    hidden = (
        jnp.einsum("nijc,ch->nijh", normed, up_full, preferred_element_type=jnp.float32) + bias_full
    )
    normal_cdf = 0.5 * (1.0 + lax.erf(hidden * inv_root_two))
    active = (hidden * normal_cdf).astype(jnp.bfloat16)
    branch = (
        jnp.einsum("nijh,hc->nijc", active, down_full, preferred_element_type=jnp.float32)
        + vector_full[3]
    )
    out_images = (
        local_images.astype(jnp.float32) + branch_scale[..., None] * vector_full[4] * branch
    ).astype(jnp.bfloat16)
    grad_out = local_cot.astype(jnp.float32)
    grad_branch = (grad_out * branch_scale[..., None] * vector_full[4]).astype(jnp.bfloat16)
    grad_scale = jnp.sum(grad_out * branch_scale[..., None] * branch, axis=(0, 1, 2))
    grad_outbias = jnp.sum(grad_branch.astype(jnp.float32), axis=(0, 1, 2))
    grad_down = jnp.einsum("nijh,nijc->hc", active, grad_branch, preferred_element_type=jnp.float32)
    grad_active = jnp.einsum(
        "nijc,hc->nijh", grad_branch, down_full, preferred_element_type=jnp.float32
    )
    slope = normal_cdf + hidden * inv_root_tau * jnp.exp(-0.5 * hidden * hidden)
    grad_hidden = (grad_active * slope).astype(jnp.bfloat16)
    grad_up = jnp.einsum("nijc,nijh->ch", normed, grad_hidden, preferred_element_type=jnp.float32)
    grad_upbias = jnp.sum(grad_hidden.astype(jnp.float32), axis=(0, 1, 2))
    grad_normed = jnp.einsum(
        "nijh,ch->nijc", grad_hidden, up_full, preferred_element_type=jnp.float32
    )
    grad_gain = jnp.sum(grad_normed * unit_norm, axis=(0, 1, 2))
    grad_shift = jnp.sum(grad_normed, axis=(0, 1, 2))
    scaled_dn = grad_normed * vector_full[1]
    grad_conv = inv_std * (
        scaled_dn
        - jnp.mean(scaled_dn, axis=-1, keepdims=True)
        - unit_norm * jnp.mean(scaled_dn * unit_norm, axis=-1, keepdims=True)
    )
    grad_convbias = jnp.sum(grad_conv, axis=(0, 1, 2))
    grad_rows = jnp.pad(grad_conv, ((0, 0), (3, 3), (0, 0), (0, 0)))
    grad_u = conv_rows(grad_rows, kernel_full[::-1], out_rows, map_side)
    grad_local = (grad_out + pixel_mask[..., None] * grad_u).astype(jnp.bfloat16)
    grad_kernel = kernel_grad(padded, grad_conv)
    grad_vectors = jnp.stack([grad_convbias, grad_gain, grad_shift, grad_outbias, grad_scale])
    out_tiles, grad_tiles = (
        lax.all_to_all(out_images, "space", split_axis=1, concat_axis=0, tiled=True),
        lax.all_to_all(grad_local, "space", split_axis=1, concat_axis=0, tiled=True),
    )
    local_grads = (grad_kernel, grad_vectors, grad_up, grad_upbias, grad_down)
    summed = lax.psum(
        (local_grads[0], local_grads[1], local_grads[2], local_grads[3], local_grads[4]),
        ("dp", "space"),
    )
    total_squares = sum((jnp.sum(g * g) for g in summed))
    owner = lax.axis_index(("dp", "space"))
    shard_grads = (
        lax.dynamic_slice_in_dim(
            summed[0], owner * depth_kernel.shape[1], depth_kernel.shape[1], 1
        ),
        lax.dynamic_slice_in_dim(
            summed[1], owner * block_vectors.shape[1], block_vectors.shape[1], 1
        ),
        lax.dynamic_slice_in_dim(summed[2], owner * up_weight.shape[1], up_weight.shape[1], 1),
        lax.dynamic_slice_in_dim(summed[3], owner * up_bias.shape[0], up_bias.shape[0], 0),
        lax.dynamic_slice_in_dim(summed[4], owner * down_weight.shape[0], down_weight.shape[0], 0),
    )
    grad_norm = jnp.sqrt(total_squares)
    factor = clip_limit / jnp.maximum(grad_norm, clip_limit)
    states = (
        (depth_kernel, kernel_moment, kernel_square),
        (block_vectors, vector_moment, vector_square),
        (up_weight, up_moment, up_square),
        (up_bias, bias_moment, bias_square),
        (down_weight, down_moment, down_square),
    )
    results = []
    for (weight, moment, square), grad_part, step_rate in zip(states, shard_grads, step_rates):
        results.extend(adam_update(weight, moment, square, grad_part, factor, step_rate))
    return (
        out_tiles,
        grad_tiles,
        results[0],
        results[1],
        results[2],
        results[3],
        results[4],
        results[5],
        results[6],
        results[7],
        results[8],
        results[9],
        results[10],
        results[11],
        results[12],
        results[13],
        results[14],
        grad_norm,
    )


def solution(mesh):
    in_specs = (
        P("dp", "space", None, None),
        P("dp", "space", None, None),
        P("dp"),
        P("dp"),
        P(None, ("dp", "space")),
        P(None, ("dp", "space")),
        P(None, ("dp", "space")),
        P(None, ("dp", "space")),
        P(None, ("dp", "space")),
        P(None, ("dp", "space")),
        P(None, ("dp", "space")),
        P(None, ("dp", "space")),
        P(None, ("dp", "space")),
        P(("dp", "space")),
        P(("dp", "space")),
        P(("dp", "space")),
        P(("dp", "space"), None),
        P(("dp", "space"), None),
        P(("dp", "space"), None),
    )
    out_specs = (
        P("dp", "space", None, None),
        P("dp", "space", None, None),
        P(None, ("dp", "space")),
        P(None, ("dp", "space")),
        P(None, ("dp", "space")),
        P(None, ("dp", "space")),
        P(None, ("dp", "space")),
        P(None, ("dp", "space")),
        P(None, ("dp", "space")),
        P(None, ("dp", "space")),
        P(None, ("dp", "space")),
        P(("dp", "space")),
        P(("dp", "space")),
        P(("dp", "space")),
        P(("dp", "space"), None),
        P(("dp", "space"), None),
        P(("dp", "space"), None),
        P(),
    )
    return jax.shard_map(body, mesh=mesh, in_specs=in_specs, out_specs=out_specs, check_vma=False)
```

profile of v0, /device:TPU:0, one launch (start us, length us, event | category | flops | bytes accessed | tf_op | source)
XLA Modules:
  0.0 850.2 jit_solution(6092713917045323219)
XLA Ops:
  7.2 4.4 all-to-all-start
  11.6 1.5 convert_element_type.333
  13.1 40.5 %all-to-all-done = bf16[32,6,24,384]{3,2,1,0:T(8,128)(2,1)S(1)} async-done(((bf16[32,6,24,384]{3,2,1,0:T(8,128)(2,1)}), bf16[32,6,24,384]{3,2,1,0:T(8,128)(2,1)S(1)}, u32[]{:S(2)}, u32[]{:S(2)}) %all-to-all-start) | async-done | bytes 3538976 | tf_op jit(solution)/shard_map/all_to_all | solution.py:91
  53.6 4.7 all-to-all-start.2
  58.4 1.5 convert_element_type.335
  60.0 75.1 %all-gather = f32[32,12,5]{1,2,0:T(8,128)S(1)} all-gather(f32[1,12,5]{1,2,0:T(8,128)S(1)} %bitcast.83), channel_id=1, replica_groups=mesh['dp'=8,'space'=4] {'dp','space'}, dimensions={0}, use_global_device_ids=true | all-gather | bytes 7920 | tf_op jit(solution)/shard_map/all_gather | solution.py:86
  135.7 1.6 reshape.229
  137.3 40.0 %all-gather.1 = f32[32,12,49]{2,1,0:T(8,128)} all-gather(f32[1,12,49]{2,1,0:T(8,128)S(1)} %bitcast.81), channel_id=1, replica_groups=mesh['dp'=8,'space'=4] {'dp','space'}, dimensions={0}, use_global_device_ids=true | all-gather | bytes 77616 | tf_op jit(solution)/shard_map/all_gather | solution.py:85
  177.3 1.0 reshape.231
  178.3 0.7 dynamic_slice.21
  179.2 37.0 %all-reduce.4 = f32[1536]{0:T(1024)} all-reduce(f32[1536]{0:T(1024)S(1)} %dynamic-update-slice), channel_id=1, replica_groups=mesh['dp'=8,'space'=4] {'dp','space'}, use_global_device_ids=true, to_apply=%add.4 | all-reduce | flops 1536 | bytes 12288
  216.3 0.9 convert_multiply_fusion.98
  217.1 1.6 slice_reduce_fusion.53
  218.7 1.8 slice_reduce_fusion.46
  220.5 2.6 slice_reduce_fusion.47
  223.1 2.6 slice_reduce_fusion.48
  225.9 0.7 and_select_fusion.1
  226.6 0.8 and_select_fusion
  227.4 0.7 and_convert_fusion
  228.6 5.5 copy.165
  234.4 0.8 broadcast_multiply_fusion
  235.7 1.3 copy-done.2
  237.4 59.4 %fusion.231 = (f32[8,24,24]{2,1,0:T(8,128)S(1)}, f32[8,24,24,384]{3,2,1,0:T(8,128)S(1)}) fusion(f32[384]{0:T(512)} %get-tuple-element.179, f32[384]{0:T(512)S(1)} %copy-done.48, f32[384]{0:T(512)S(1)} %copy-done.49, f32[384]{0:T(512)S(1)} %copy-done.50, bf16[8,30,24,384]{3,2,1,0:T(8,128)(2,1)S(1)} %pad.17, f32[384]{0:T(512)S(1)} %copy-done.51, ...), kind=kLoop, calls=%fused_computation.507 | loop fusion | flops 267185664 | bytes 36440576 | tf_op jit(solution)/shard_map/reduce_sum | solution.py:108
  296.9 2.8 copy-done.1
  299.7 1.6 multiply_reduce_fusion.3
  302.0 18.7 %multiply_convert_fusion = (bf16[8,24,24,1536]{3,2,1,0:T(8,128)(2,1)}, f32[8,24,24,1536]{3,2,1,0:T(8,128)}) fusion(f32[1536]{0:T(1024)S(1)} %copy-done.85, bf16[384,1536]{0,1:T(8,128)(2,1)} %all-gather.5.cloned.1.call-done, f32[8,24,24,384]{3,2,1,0:T(8,128)} %copy-done.1, f32[384]{0:T(512)} %get-tuple-element.177, f32[384]{0:T(512)S(1)} %copy-done.64, ...), kind=kOutput, calls=%fused_computation.49 | convolution fusion | flops 5487132672 | bytes 50770944 | tf_op jit(solution)/shard_map/nijc,ch->nijh/dot_general | solution.py:115
  320.7 16.5 %multiply_reduce_fusion = (f32[384]{0:T(512)}, bf16[8,24,24,384]{3,2,1,0:T(8,128)(2,1)}, bf16[8,24,24,384]{3,2,1,0:T(8,128)(2,1)S(1)}) fusion(f32[8,24,24,384]{3,2,1,0:T(8,128)} %bitcast.75, f32[384]{0:T(512)} %get-tuple-element.176, f32[8,24,24]{2,1,0:T(8,128)} %and_select_fusion.1, f32[384]{0:T(512)S(1)} %copy-done.62, ...), kind=kOutput, calls=%fused_computation.387 | convolution fusion | flops 5455281664 | bytes 33053184 | tf_op jit(solution)/shard_map/nijh,hc->nijc/dot_general | solution.py:120
  337.2 11.9 %fusion.203 = f32[1536,384]{1,0:T(8,128)} fusion(bf16[8,24,24,384]{3,2,1,0:T(8,128)(2,1)S(1)} %get-tuple-element.205, bf16[8,24,24,1536]{3,2,1,0:T(8,128)(2,1)} %get-tuple-element.208), kind=kOutput, calls=%fused_computation.401 | convolution fusion | flops 5435817984 | bytes 20054016 | tf_op jit(solution)/shard_map/nijh,nijc->hc/dot_general | solution.py:130
  349.0 21.6 %convert_reduce_fusion = (f32[1536]{0:T(1024)}, bf16[8,24,24,1536]{3,2,1,0:T(8,128)(2,1)}) fusion(f32[8,24,24,1536]{3,2,1,0:T(8,128)} %get-tuple-element.209, f32[1536]{0:T(1024)S(1)} %copy-done.85, bf16[8,24,24,384]{3,2,1,0:T(8,128)(2,1)S(1)} %get-tuple-element.205, bf16[1536,384]{1,0:T(8,128)(2,1)S(1)} %copy-done.112), kind=kOutput, calls=%fused_computation.48 | convolution fusion | flops 5527828992 | bytes 47198208 | tf_op jit(solution)/shard_map/nijc,hc->nijh/dot_general | solution.py:131
  370.7 16.5 %fusion.208 = f32[384,1536]{0,1:T(8,128)} fusion(bf16[8,24,24,1536]{3,2,1,0:T(8,128)(2,1)} %get-tuple-element.212, f32[8,24,24,384]{3,2,1,0:T(8,128)} %copy-done.1, f32[384]{0:T(512)S(1)} %copy-done.106, f32[384]{0:T(512)S(1)} %copy-done.64, f32[8,24,24]{2,1,0:T(8,128)S(1)} %copy-done.11, f32[8,24,24]{2,1,0:T(8,128)S(1)} %copy-done.8), kind=kOutput, calls=%fused_computation.402 | convolution fusion | flops 5444665344 | bytes 23632896 | tf_op jit(solution)/shard_map/nijc,nijh->ch/dot_general | solution.py:136
  387.2 15.5 %multiply_reduce_fusion.1 = (f32[384]{0:T(512)}, f32[8,24,24]{2,1,0:T(8,128)S(1)}, f32[8,24,24]{2,1,0:T(8,128)S(1)}, f32[384]{0:T(512)}, f32[8,24,24,384]{3,2,1,0:T(8,128)}) fusion(f32[8,24,24,384]{3,2,1,0:T(8,128)} %copy-done.1, f32[8,24,24]{2,1,0:T(8,128)S(1)} %copy-done.11, f32[8,24,24]{2,1,0:T(8,128)S(1)} %copy-done.8, f32[384]{0:T(512)S(1)} %copy-done.64, ...), kind=kOutput, calls=%fused_computation.389 | convolution fusion | flops 5451732992 | bytes 29569536 | tf_op jit(solution)/shard_map/nijh,ch->nijc/dot_general | solution.py:138
  403.4 36.5 %fusion.105 = (f32[384]{0:T(512)}, f32[384]{0:T(512)}, f32[384]{0:T(512)}, f32[384]{0:T(512)}, f32[384]{0:T(512)}, /*index=5*/f32[384]{0:T(512)}, f32[384]{0:T(5...) fusion(bf16[8,30,24,384]{3,2,1,0:T(8,128)(2,1)} %copy-done, ...), kind=kLoop, calls=%fused_computation.291 | loop fusion | flops 107930880 | bytes 25760256 | tf_op jit(solution)/shard_map/reduce_sum | solution.py:39
  439.9 8.9 %fusion.102 = (f32[384]{0:T(512)}, f32[384]{0:T(512)}, f32[384]{0:T(512)}, f32[384]{0:T(512)}, f32[384]{0:T(512)}, /*index=5*/f32[384]{0:T(512)}, f32[384]{0:T(512)}, f32[384]{0:T(512)}) fusion(f32[8,24,24,384]{3,2,1,0:T(8,128)} %get-tuple-element.200, bf16[8,24,24,384]{3,2,1,0:T(8,128)(2,1)S(1)} %copy-done.3), kind=kLoop, calls=%fused_computation.288 | loop fusion | flops 38925312 | bytes 10629120 | tf_op jit(solution)/shard_map/reduce_sum | solution.py:39
  448.8 8.6 %fusion.40 = (f32[384]{0:T(512)}, f32[384]{0:T(512)}, f32[384]{0:T(512)}, f32[384]{0:T(512)S(1)}, f32[384]{0:T(512)S(1)}, /*index=5*/f32[384]{0:T(512)S(1)}) fusion(f32[8,24,24,384]{3,2,1,0:T(8,128)} %get-tuple-element.200, bf16[8,30,24,384]{3,2,1,0:T(8,128)(2,1)S(1)} %bitcast.71), kind=kLoop, calls=%fused_computation.226 | loop fusion | flops 31848192 | bytes 11510784 | tf_op jit(solution)/shard_map/reduce_sum | solution.py:39
  457.4 33.2 %fusion.84 = (f32[384]{0:T(512)}, f32[384]{0:T(512)}, f32[384]{0:T(512)}, f32[384]{0:T(512)}, f32[384]{0:T(512)}, /*index=5*/f32[384]{0:T(512)}, f32[384]{0:T(51...) fusion(f32[8,24,24,384]{3,2,1,0:T(8,128)} %get-tuple-element.20, ...), kind=kLoop, calls=%fused_computation.270 | loop fusion | flops 95544576 | bytes 11529216 | tf_op jit(solution)/shard_map/reduce_sum | solution.py:39
  490.9 7.1 pad.19
  498.1 1.3 stack.213
  510.5 1.2 stack.199
  511.7 1.3 stack.192
  513.0 1.3 stack.185
  515.4 1.3 stack.195
  528.3 9.3 %stack.217 = f32[49,384]{1,0:T(8,128)} concatenate(f32[1,384]{1,0:T(1,128)S(1)} %stack.168, f32[1,384]{1,0:T(1,128)S(1)} %stack.169, f32[1,384]{1,0:T(1,128)} %stack.170, f32[1,384]{1,0:T(1,128)} %stack.171, f32[1,384]{1,0:T(1,128)} %stack.172, f32[1,384]{1,0:T(1,128)} %stack.173, f32[1,384]{1,0:T(1,128)} %stack.174, f32[1,384]{1,0:T(1,128)} %stack.175, f32[1,384]{1,0:T(1,128)} %stack.176, ...), dimensions={0} | concatenate | bytes 150528 | tf_op jit(solution)/shard_map/stack | solution.py:46
  537.6 1.7 copy.168
  539.3 2.4 copy.163
  541.8 3.9 all-to-all-start.1
  546.4 184.0 %fusion.195 = bf16[8,24,24,384]{3,2,1,0:T(8,128)(2,1)} fusion(f32[8,24,24,384]{3,2,1,0:T(8,128)} %bitcast.76, f32[8,30,24,384]{3,2,1,0:T(8,128)} %pad.19, f32[8,24,24,384]{3,2,1,0:T(8,128)} %get-tuple-element.200, f32[8,24,24]{2,1,0:T(8,128)} %get-tuple-element.206, f32[384]{0:T(512)} %get-tuple-element.127, f32[384]{0:T(512)} %get-tuple-element.128, ...), kind=kLoop, calls=%fused_computation.381 | loop fusion | flops 176947200 | bytes 69206016 | tf_op jit(solution)/shard_map/convert_element_type | solution.py:152
  730.4 4.5 copy.166
  734.9 4.7 all-to-all-start.3
  739.7 2.6 bitcast_convert_fusion
  742.3 0.9 convert_reduce_fusion.1
  746.0 0.8 stack.223
  746.8 68.2 %all-reduce.5 = (f32[5,384]{1,0:T(8,128)}, f32[1536]{0:T(1024)}) all-reduce(f32[5,384]{1,0:T(8,128)S(1)} %stack.223, f32[1536]{0:T(1024)} %get-tuple-element.211), channel_id=1, replica_groups=mesh['dp'=8,'space'=4] {'dp','space'}, use_global_device_ids=true, to_apply=%region_60.61 | all-reduce | flops 3456 | bytes 27648 | tf_op jit(solution)/shard_map/psum | solution.py:160
  815.0 1.3 multiply_reduce_fusion.9
  816.3 1.3 multiply_reduce_fusion.8
  817.6 1.6 multiply_reduce_fusion.7
  820.5 2.9 multiply_reduce_fusion.6
  824.7 2.9 multiply_reduce_fusion.5
  828.3 1.3 multiply_subtract_fusion.4
  829.6 1.4 multiply_subtract_fusion.3
  831.0 1.4 multiply_subtract_fusion.2
  832.4 1.7 multiply_subtract_fusion
  834.1 1.7 multiply_subtract_fusion.1
  835.8 2.2 copy.164
  838.0 4.1 copy.167
  (301 shorter events, 31.1 us)
Async XLA Ops:
  7.2 52.8 %copy-start.60 = (f32[5,12]{1,0:T(8,128)S(1)}, f32[5,12]{1,0:T(8,128)}, u32[]{:S(2)}) copy-start(f32[5,12]{1,0:T(8,128)} %param.26) | copy-start | bytes 724
  7.2 130.1 %copy-start.12 = (f32[49,12]{0,1:T(8,128)S(1)}, f32[49,12]{0,1:T(8,128)}, u32[]{:S(2)}) copy-start(f32[49,12]{0,1:T(8,128)} %param.23) | copy-start | bytes 7060
  7.2 171.8 %copy-start.110 = (f32[48]{0:T(128)S(1)}, f32[48]{0:T(128)}, u32[]{:S(2)}) copy-start(f32[48]{0:T(128)} %param.32) | copy-start | bytes 580
  7.2 46.4 %all-to-all-start = ((bf16[32,6,24,384]{3,2,1,0:T(8,128)(2,1)}), bf16[32,6,24,384]{3,2,1,0:T(8,128)(2,1)S(1)}, u32[]{:S(2)}, u32[]{:S(2)}) async-start(bf16[32,6,24,384]{3,2,1,0:T(8,128)(2,1)} %param.19), calls=%async_computation | async-start | bytes 7077888 | tf_op jit(solution)/shard_map/all_to_all | solution.py:91
  11.6 290.4 %all-gather.5.cloned.1.call-start = ((), (), s32[]{:S(2)}) async-start(), calls=%async_computation.4 | async-start | bytes 1216512 | tf_op jit(solution)/shard_map/all_gather | solution.py:81
  53.6 83.7 %copy-start.4 = (bf16[32,6,24,384]{3,2,1,0:T(8,128)(2,1)}, bf16[32,6,24,384]{3,2,1,0:T(8,128)(2,1)S(1)}, u32[]{:S(2)}) copy-start(bf16[32,6,24,384]{3,2,1,0:T(8,128)(2,1)S(1)} %all-to-all-done) | copy-start | bytes 10616836
  53.6 174.9 %all-to-all-start.2 = ((bf16[32,6,24,384]{3,2,1,0:T(8,128)(2,1)}), bf16[32,6,24,384]{3,2,1,0:T(8,128)(2,1)}, u32[]{:S(2)}, u32[]{:S(2)}) async-start(bf16[32,6,24,384]{3,2,1,0:T(8,128)(2,1)} %param.20), calls=%async_computation.2 | async-start | bytes 7077888 | tf_op jit(solution)/shard_map/all_to_all | solution.py:92
  58.4 262.3 %all-gather.7.cloned.1.call-start = ((), (), s32[]{:S(2)}) async-start(), calls=%async_computation.5 | async-start | bytes 1216512 | tf_op jit(solution)/shard_map/all_gather | solution.py:82
  216.2 11.9 %copy-start.5 = (bf16[32,6,24,384]{3,2,1,0:T(8,128)(2,1)S(1)}, bf16[32,6,24,384]{3,2,1,0:T(8,128)(2,1)}, u32[]{:S(2)}) copy-start(bf16[32,6,24,384]{3,2,1,0:T(8,128)(2,1)} %copy-done.4) | copy-start | bytes 10616836
  220.5 16.5 %copy-start.13 = (f32[384]{0:T(512)}, f32[384]{0:T(512)S(1)}, u32[]{:S(2)}) copy-start(f32[384]{0:T(512)S(1)} %get-tuple-element.164) | copy-start | bytes 4612
  220.5 16.5 %copy-start.15 = (f32[384]{0:T(512)}, f32[384]{0:T(512)S(1)}, u32[]{:S(2)}) copy-start(f32[384]{0:T(512)S(1)} %get-tuple-element.165) | copy-start | bytes 4612
  220.5 16.5 %copy-start.17 = (f32[384]{0:T(512)}, f32[384]{0:T(512)S(1)}, u32[]{:S(2)}) copy-start(f32[384]{0:T(512)S(1)} %get-tuple-element.166) | copy-start | bytes 4612
  220.5 16.5 %copy-start.19 = (f32[384]{0:T(512)}, f32[384]{0:T(512)S(1)}, u32[]{:S(2)}) copy-start(f32[384]{0:T(512)S(1)} %get-tuple-element.167) | copy-start | bytes 4612
  235.7 61.2 %copy-start = (bf16[8,30,24,384]{3,2,1,0:T(8,128)(2,1)}, bf16[8,30,24,384]{3,2,1,0:T(8,128)(2,1)S(1)}, u32[]{:S(2)}) copy-start(bf16[8,30,24,384]{3,2,1,0:T(8,128)(2,1)S(1)} %pad.17) | copy-start | bytes 13271044
  302.0 18.7 %copy-start.62 = (f32[384]{0:T(512)S(1)}, f32[384]{0:T(512)}, u32[]{:S(2)}) copy-start(f32[384]{0:T(512)} %get-tuple-element.175) | copy-start | bytes 4612
  337.2 11.9 %copy-start.112 = (bf16[1536,384]{1,0:T(8,128)(2,1)S(1)}, bf16[1536,384]{1,0:T(8,128)(2,1)}, u32[]{:S(2)}) copy-start(bf16[1536,384]{1,0:T(8,128)(2,1)} %all-gather.7.cloned.1.call-done) | copy-start | bytes 3538948
  349.0 21.6 %copy-start.8 = (f32[8,24,24]{2,1,0:T(8,128)S(1)}, f32[8,24,24]{2,1,0:T(8,128)}, u32[]{:S(2)}) copy-start(f32[8,24,24]{2,1,0:T(8,128)} %copy-done.7) | copy-start | bytes 55300
  349.0 21.6 %copy-start.11 = (f32[8,24,24]{2,1,0:T(8,128)S(1)}, f32[8,24,24]{2,1,0:T(8,128)}, u32[]{:S(2)}) copy-start(f32[8,24,24]{2,1,0:T(8,128)} %add_rsqrt_fusion) | copy-start | bytes 55300
  349.0 21.6 %copy-start.106 = (f32[384]{0:T(512)S(1)}, f32[384]{0:T(512)}, u32[]{:S(2)}) copy-start(f32[384]{0:T(512)} %get-tuple-element.177) | copy-start | bytes 4612
  370.6 16.5 %copy-start.111 = (bf16[384,1536]{0,1:T(8,128)(2,1)S(1)}, bf16[384,1536]{0,1:T(8,128)(2,1)}, u32[]{:S(2)}) copy-start(bf16[384,1536]{0,1:T(8,128)(2,1)} %all-gather.5.cloned.1.call-done) | copy-start | bytes 3538948
  403.4 36.5 %copy-start.3 = (bf16[8,24,24,384]{3,2,1,0:T(8,128)(2,1)S(1)}, bf16[8,24,24,384]{3,2,1,0:T(8,128)(2,1)}, u32[]{:S(2)}) copy-start(bf16[8,24,24,384]{3,2,1,0:T(8,128)(2,1)} %copy-done.2) | copy-start | bytes 10616836
  490.6 9.4 %copy-start.83 = (f32[384]{0:T(512)S(1)}, f32[384]{0:T(512)}, u32[]{:S(2)}) copy-start(f32[384]{0:T(512)} %get-tuple-element.75) | copy-start | bytes 4612
  490.6 9.9 %copy-start.82 = (f32[384]{0:T(512)S(1)}, f32[384]{0:T(512)}, u32[]{:S(2)}) copy-start(f32[384]{0:T(512)} %get-tuple-element.76) | copy-start | bytes 4612
  490.6 10.5 %copy-start.81 = (f32[384]{0:T(512)S(1)}, f32[384]{0:T(512)}, u32[]{:S(2)}) copy-start(f32[384]{0:T(512)} %get-tuple-element.77) | copy-start | bytes 4612
  490.6 11.1 %copy-start.80 = (f32[384]{0:T(512)S(1)}, f32[384]{0:T(512)}, u32[]{:S(2)}) copy-start(f32[384]{0:T(512)} %get-tuple-element.78) | copy-start | bytes 4612
  490.6 11.7 %copy-start.79 = (f32[384]{0:T(512)S(1)}, f32[384]{0:T(512)}, u32[]{:S(2)}) copy-start(f32[384]{0:T(512)} %get-tuple-element.79) | copy-start | bytes 4612
  490.6 12.2 %copy-start.78 = (f32[384]{0:T(512)S(1)}, f32[384]{0:T(512)}, u32[]{:S(2)}) copy-start(f32[384]{0:T(512)} %get-tuple-element.80) | copy-start | bytes 4612
  490.6 12.8 %copy-start.77 = (f32[384]{0:T(512)S(1)}, f32[384]{0:T(512)}, u32[]{:S(2)}) copy-start(f32[384]{0:T(512)} %get-tuple-element.81) | copy-start | bytes 4612
  490.6 13.3 %copy-start.76 = (f32[384]{0:T(512)S(1)}, f32[384]{0:T(512)}, u32[]{:S(2)}) copy-start(f32[384]{0:T(512)} %get-tuple-element.82) | copy-start | bytes 4612
  490.6 13.9 %copy-start.75 = (f32[384]{0:T(512)S(1)}, f32[384]{0:T(512)}, u32[]{:S(2)}) copy-start(f32[384]{0:T(512)} %get-tuple-element.83) | copy-start | bytes 4612
  490.6 14.5 %copy-start.74 = (f32[384]{0:T(512)S(1)}, f32[384]{0:T(512)}, u32[]{:S(2)}) copy-start(f32[384]{0:T(512)} %get-tuple-element.84) | copy-start | bytes 4612
  490.6 15.0 %copy-start.73 = (f32[384]{0:T(512)S(1)}, f32[384]{0:T(512)}, u32[]{:S(2)}) copy-start(f32[384]{0:T(512)} %get-tuple-element.85) | copy-start | bytes 4612
  490.7 15.6 %copy-start.72 = (f32[384]{0:T(512)S(1)}, f32[384]{0:T(512)}, u32[]{:S(2)}) copy-start(f32[384]{0:T(512)} %get-tuple-element.86) | copy-start | bytes 4612
  490.7 16.2 %copy-start.71 = (f32[384]{0:T(512)S(1)}, f32[384]{0:T(512)}, u32[]{:S(2)}) copy-start(f32[384]{0:T(512)} %get-tuple-element.87) | copy-start | bytes 4612
  490.7 16.8 %copy-start.69 = (f32[384]{0:T(512)S(1)}, f32[384]{0:T(512)}, u32[]{:S(2)}) copy-start(f32[384]{0:T(512)} %get-tuple-element.88) | copy-start | bytes 4612
  490.7 17.3 %copy-start.67 = (f32[384]{0:T(512)S(1)}, f32[384]{0:T(512)}, u32[]{:S(2)}) copy-start(f32[384]{0:T(512)} %get-tuple-element.89) | copy-start | bytes 4612
  490.7 17.9 %copy-start.65 = (f32[384]{0:T(512)S(1)}, f32[384]{0:T(512)}, u32[]{:S(2)}) copy-start(f32[384]{0:T(512)} %get-tuple-element.90) | copy-start | bytes 4612
  490.7 23.5 %copy-start.105 = (f32[384]{0:T(512)S(1)}, f32[384]{0:T(512)}, u32[]{:S(2)}) copy-start(f32[384]{0:T(512)} %get-tuple-element.121) | copy-start | bytes 4612
  490.7 24.1 %copy-start.104 = (f32[384]{0:T(512)S(1)}, f32[384]{0:T(512)}, u32[]{:S(2)}) copy-start(f32[384]{0:T(512)} %get-tuple-element.122) | copy-start | bytes 4612
  490.7 25.9 %copy-start.70 = (f32[384]{0:T(512)S(1)}, f32[384]{0:T(512)}, u32[]{:S(2)}) copy-start(f32[384]{0:T(512)} %get-tuple-element.110) | copy-start | bytes 4612
  490.7 26.5 %copy-start.68 = (f32[384]{0:T(512)S(1)}, f32[384]{0:T(512)}, u32[]{:S(2)}) copy-start(f32[384]{0:T(512)} %get-tuple-element.111) | copy-start | bytes 4612
  490.7 27.1 %copy-start.66 = (f32[384]{0:T(512)S(1)}, f32[384]{0:T(512)}, u32[]{:S(2)}) copy-start(f32[384]{0:T(512)} %get-tuple-element.112) | copy-start | bytes 4612
  490.8 28.2 %copy-start.103 = (f32[384]{0:T(512)S(1)}, f32[384]{0:T(512)}, u32[]{:S(2)}) copy-start(f32[384]{0:T(512)} %get-tuple-element.93) | copy-start | bytes 4612
  490.8 28.2 %copy-start.102 = (f32[384]{0:T(512)S(1)}, f32[384]{0:T(512)}, u32[]{:S(2)}) copy-start(f32[384]{0:T(512)} %get-tuple-element.94) | copy-start | bytes 4612
  490.8 28.8 %copy-start.101 = (f32[384]{0:T(512)S(1)}, f32[384]{0:T(512)}, u32[]{:S(2)}) copy-start(f32[384]{0:T(512)} %get-tuple-element.95) | copy-start | bytes 4612
  490.8 29.4 %copy-start.100 = (f32[384]{0:T(512)S(1)}, f32[384]{0:T(512)}, u32[]{:S(2)}) copy-start(f32[384]{0:T(512)} %get-tuple-element.96) | copy-start | bytes 4612
  490.8 29.9 %copy-start.99 = (f32[384]{0:T(512)S(1)}, f32[384]{0:T(512)}, u32[]{:S(2)}) copy-start(f32[384]{0:T(512)} %get-tuple-element.97) | copy-start | bytes 4612
  490.8 30.5 %copy-start.98 = (f32[384]{0:T(512)S(1)}, f32[384]{0:T(512)}, u32[]{:S(2)}) copy-start(f32[384]{0:T(512)} %get-tuple-element.98) | copy-start | bytes 4612
  490.8 31.1 %copy-start.97 = (f32[384]{0:T(512)S(1)}, f32[384]{0:T(512)}, u32[]{:S(2)}) copy-start(f32[384]{0:T(512)} %get-tuple-element.99) | copy-start | bytes 4612
  490.8 31.7 %copy-start.96 = (f32[384]{0:T(512)S(1)}, f32[384]{0:T(512)}, u32[]{:S(2)}) copy-start(f32[384]{0:T(512)} %get-tuple-element.100) | copy-start | bytes 4612
  490.8 32.3 %copy-start.95 = (f32[384]{0:T(512)S(1)}, f32[384]{0:T(512)}, u32[]{:S(2)}) copy-start(f32[384]{0:T(512)} %get-tuple-element.101) | copy-start | bytes 4612
  490.8 32.9 %copy-start.94 = (f32[384]{0:T(512)S(1)}, f32[384]{0:T(512)}, u32[]{:S(2)}) copy-start(f32[384]{0:T(512)} %get-tuple-element.102) | copy-start | bytes 4612
  490.9 33.4 %copy-start.93 = (f32[384]{0:T(512)S(1)}, f32[384]{0:T(512)}, u32[]{:S(2)}) copy-start(f32[384]{0:T(512)} %get-tuple-element.103) | copy-start | bytes 4612
  490.9 34.0 %copy-start.92 = (f32[384]{0:T(512)S(1)}, f32[384]{0:T(512)}, u32[]{:S(2)}) copy-start(f32[384]{0:T(512)} %get-tuple-element.104) | copy-start | bytes 4612
  490.9 34.5 %copy-start.91 = (f32[384]{0:T(512)S(1)}, f32[384]{0:T(512)}, u32[]{:S(2)}) copy-start(f32[384]{0:T(512)} %get-tuple-element.105) | copy-start | bytes 4612
  490.9 35.1 %copy-start.90 = (f32[384]{0:T(512)S(1)}, f32[384]{0:T(512)}, u32[]{:S(2)}) copy-start(f32[384]{0:T(512)} %get-tuple-element.106) | copy-start | bytes 4612
  490.9 35.7 %copy-start.89 = (f32[384]{0:T(512)S(1)}, f32[384]{0:T(512)}, u32[]{:S(2)}) copy-start(f32[384]{0:T(512)} %get-tuple-element.107) | copy-start | bytes 4612
  490.9 36.2 %copy-start.88 = (f32[384]{0:T(512)S(1)}, f32[384]{0:T(512)}, u32[]{:S(2)}) copy-start(f32[384]{0:T(512)} %get-tuple-element.108) | copy-start | bytes 4612
  490.9 36.8 %copy-start.87 = (f32[384]{0:T(512)S(1)}, f32[384]{0:T(512)}, u32[]{:S(2)}) copy-start(f32[384]{0:T(512)} %get-tuple-element.109) | copy-start | bytes 4612
  490.9 48.4 %copy-start.6 = (bf16[8,24,24,384]{3,2,1,0:T(8,128)(2,1)S(1)}, bf16[8,24,24,384]{3,2,1,0:T(8,128)(2,1)}, u32[]{:S(2)}) copy-start(bf16[8,24,24,384]{3,2,1,0:T(8,128)(2,1)} %get-tuple-element.204) | copy-start | bytes 10616836
  541.8 193.1 %all-to-all-start.1 = ((bf16[8,24,24,384]{3,2,0,1:T(8,128)(2,1)}), bf16[8,24,24,384]{3,2,0,1:T(8,128)(2,1)S(1)}, u32[]{:S(2)}, u32[]{:S(2)}) async-start(bf16[8,24,24,384]{3,2,0,1:T(8,128)(2,1)} %copy.163), calls=%async_computation.1 | async-start | bytes 7077888 | tf_op jit(solution)/shard_map/all_to_all | solution.py:156
  545.6 272.0 %all-reduce.9.cloned.1.call-start = ((), (), s32[]{:S(2)}) async-start(), calls=%async_computation.6 | async-start | bytes 9830400 | tf_op jit(solution)/shard_map/psum | solution.py:160
  734.9 103.1 %all-to-all-start.3 = ((bf16[8,24,24,384]{3,2,0,1:T(8,128)(2,1)}), bf16[8,24,24,384]{3,2,0,1:T(8,128)(2,1)}, u32[]{:S(2)}, u32[]{:S(2)}) async-start(bf16[8,24,24,384]{3,2,0,1:T(8,128)(2,1)} %copy.166), calls=%async_computation.3 | async-start | bytes 7077888 | tf_op jit(solution)/shard_map/all_to_all | solution.py:157
  742.3 87.3 %copy-start.61 = (f32[5,12]{1,0:T(8,128)S(1)}, f32[5,12]{1,0:T(8,128)}, u32[]{:S(2)}) copy-start(f32[5,12]{1,0:T(8,128)} %param.26) | copy-start | bytes 724
  (58 other events, 212.3 us)
Sparse Core Ops, SparseCore 0:
  15.9 57.4 all-gather.4
  76.8 53.5 all-gather.6
  552.6 150.6 all-reduce.8
where the time goes:
time: 862 us; the launch traced here: 850 us
  other arithmetic  362 us (42%)
  blocking collectives  220 us (26%)
  matrix products  101 us (12%)
  local copies, waits for them, and re-layouts  88.7 us (10%)
  waiting for transfers between devices  41.3 us (5%)
  between operations  19.9 us (2%)
  starting transfers between devices  17.8 us (2%)
    convert_element_type x1, other arithmetic, body(): (grad_out + pixel_mask[..., None] * grad_u).astype(jnp.bfloat16)  184 us
    reduce_sum x4, other arithmetic, kernel_grad(): jnp.sum(wide[:, row_off:row_off + out_rows, col_off:col_off + out_cols, :...  87.2 us
    all_gather x1, blocking collectives, body(): lax.all_gather(block_vectors, ('dp', 'space'), axis=1, tiled=True)  75.1 us
    psum x1, blocking collectives, body(): lax.psum((local_grads[0], local_grads[1], local_grads[2], local_grads[3],...  68.2 us
    reduce_sum x1, other arithmetic, body(): chan_mean = jnp.mean(conv, axis=-1, keepdims=True)  59.4 us
    another operation x51, local copies, waits for them, and re-layouts, kernel_grad(): return jnp.stack(pieces)  41.1 us
    all_to_all x1, waiting for transfers between devices, body(): lax.all_to_all(images, 'space', split_axis=0, concat_axis=1, tiled=True)  40.5 us
    all_gather x1, blocking collectives, body(): lax.all_gather(depth_kernel, ('dp', 'space'), axis=1, tiled=True)  40 us
  transfers between devices with their start and end apart: 7, of which 1 were waited for; matrix products, arithmetic and copies ran while one was open for 38% of the time, Pallas kernels for 0%

commit v1 on v0

v1 whole, which is shorter than its diff:
```python
import functools

import jax
import jax.numpy as jnp
from jax import lax
from jax.experimental import pallas as pl
from jax.experimental.pallas import tpu as pltpu
from jax.sharding import PartitionSpec as P

STEP = 5

keep_scale = 4.0 / 3.0
norm_eps = 1e-06
clip_limit = 1.0
beta_one = 0.9
beta_two = 0.999
adam_eps = 1e-08
decay_rate = 0.05
step_rates = (0.15, 0.5, 0.05, 0.2, 0.025)
inv_root_two = 0.7071067811865476
inv_root_tau = 0.3989422804014327
f32 = jnp.float32
bf16 = jnp.bfloat16
AXES = ("dp", "space")
LANES = 128
REACH = 3
TAPS = 7
EDGE = 8
MLP_ROWS = 512
MLP_COLS = 256
MIB = 1 << 20


def clear_edges(pad_ref, cols):
    tiles, rows, width, lanes = pad_ref.shape
    for tile in range(tiles):
        for row in range(rows):
            pad_ref[tile, row, 0:EDGE, :] = jnp.zeros((EDGE, lanes), f32)
            pad_ref[tile, row, EDGE + cols : width, :] = jnp.zeros((width - EDGE - cols, lanes), f32)


def fill_rows(pad_ref, first, block, limit=None, row_start=None):
    rows, cols, channels = block.shape
    for row in range(rows):
        line = block[row].astype(f32)
        if limit is not None:
            reach = jnp.where(row_start + row < limit, limit, 0)
            inside = lax.broadcasted_iota(jnp.int32, (cols, channels), 0) < reach
            line = jnp.where(inside, line, 0.0)
        for tile in range(channels // LANES):
            pad_ref[tile, first + row, EDGE : EDGE + cols, :] = line[:, tile * LANES : (tile + 1) * LANES]


def conv_tile(pad_ref, tile, taps_ref, out_rows, cols, flip):
    lanes = slice(tile * LANES, (tile + 1) * LANES)
    sums = [None] * out_rows
    for col_off in range(TAPS):
        weights = []
        for row_off in range(TAPS):
            index = row_off * TAPS + col_off
            if flip:
                index = TAPS * TAPS - 1 - index
            weights.append(taps_ref[index : index + 1, lanes])
        for row in range(out_rows + 2 * REACH):
            start = EDGE - REACH + col_off
            line = pad_ref[tile, row, start : start + cols, :]
            for row_off in range(TAPS):
                out = row - row_off
                if 0 <= out < out_rows:
                    term = weights[row_off] * line
                    sums[out] = term if sums[out] is None else sums[out] + term
    return sums


def conv_norm_kernel(
    keep_ref, slot_ref, side_ref, row_ref, above_ref, own_ref, below_ref, cot_ref, taps_ref, vec_ref,
    unit_ref, inv_ref, cotm_ref, pad_ref, conv_ref,
):
    image = pl.program_id(0)
    rows, cols, channels = own_ref.shape[1:]

    @pl.when(image == 0)
    def _():
        clear_edges(pad_ref, cols)

    @pl.when(keep_ref[image] > 0)
    def _():
        side = side_ref[image]
        start = row_ref[0]
        fill_rows(pad_ref, 0, above_ref[0], side, start - REACH)
        fill_rows(pad_ref, REACH, own_ref[0], side, start)
        fill_rows(pad_ref, REACH + rows, below_ref[0], side, start + rows)
        for tile in range(channels // LANES):
            lanes = slice(tile * LANES, (tile + 1) * LANES)
            sums = conv_tile(pad_ref, tile, taps_ref, rows, cols, False)
            for row in range(rows):
                conv_ref[row * cols : (row + 1) * cols, lanes] = sums[row] + vec_ref[0:1, lanes]
        conv = conv_ref[...]
        mean = jnp.mean(conv, axis=-1, keepdims=True)
        centred = conv - mean
        var = jnp.mean(centred * centred, axis=-1, keepdims=True)
        inv_std = lax.rsqrt(var + norm_eps)
        unit_ref[...] = centred * inv_std
        inv_ref[...] = jnp.broadcast_to(inv_std, inv_ref.shape)
        for row in range(rows):
            line = cot_ref[0, row].astype(f32)
            reach = jnp.where(start + row < side, side, 0)
            inside = lax.broadcasted_iota(jnp.int32, (cols, channels), 0) < reach
            conv_ref[row * cols : (row + 1) * cols, :] = jnp.where(inside, line, 0.0)
        cotm_ref[...] = conv_ref[...].astype(bf16)


def dot_nn(a, b):
    return lax.dot_general(a, b, (((1,), (0,)), ((), ())), preferred_element_type=f32)


def dot_nt(a, b):
    return lax.dot_general(a, b, (((1,), (1,)), ((), ())), preferred_element_type=f32)


def fold(value):
    rows, channels = value.shape
    return jnp.sum(value.reshape(rows // 8, 8, channels), axis=0)


def mlp_kernel(
    count_ref, unit_ref, inv_ref, cotm_ref, near_ref, far_ref, bias_ref, vec_ref,
    branch_ref, gc_ref, grad_ref, bsum_ref, vsum_ref, up_acc, down_acc, scaled_ref, bias_acc, vec_acc,
):
    step = pl.program_id(0)
    rows, channels = unit_ref.shape
    half = near_ref.shape[0]
    hidden_size = 2 * half
    used = count_ref[0]
    gamma = vec_ref[4:5, :] * keep_scale

    def weights(start):
        ref = near_ref if start < half else far_ref
        base = start % half
        return ref, slice(base, base + MLP_COLS)

    @pl.when(step == 0)
    def _():
        up_acc[...] = jnp.zeros_like(up_acc)
        down_acc[...] = jnp.zeros_like(down_acc)
        bias_acc[...] = jnp.zeros_like(bias_acc)
        vec_acc[...] = jnp.zeros_like(vec_acc)
        for start in range(0, hidden_size, MLP_COLS):
            ref, part = weights(start)
            down = ref[part, channels : 2 * channels].astype(f32)
            scaled_ref[start : start + MLP_COLS, :] = (down * gamma).astype(bf16)

    @pl.when(step * rows < used)
    def _():
        inside = lax.broadcasted_iota(jnp.int32, (rows, channels), 0) < used - step * rows
        unit = jnp.where(inside, unit_ref[...], 0.0)
        cotm32 = jnp.where(inside, cotm_ref[...].astype(f32), 0.0)
        cotm = cotm32.astype(bf16)
        normed = (unit * vec_ref[1:2, :] + vec_ref[2:3, :]).astype(bf16)
        normed_t = normed.T
        cotm_t = cotm.T
        branch = None
        grad_normed = None
        for start in range(0, hidden_size, MLP_COLS):
            ref, part = weights(start)
            cols = slice(start, start + MLP_COLS)
            up = ref[part, 0:channels]
            down = ref[part, channels : 2 * channels]
            hidden = dot_nt(normed, up) + bias_ref[0:1, cols]
            cdf = 0.5 + 0.5 * lax.erf(hidden * inv_root_two)
            active = (hidden * cdf).astype(bf16)
            slope = cdf + hidden * (inv_root_tau * jnp.exp(-0.5 * hidden * hidden))
            part_branch = dot_nn(active, down)
            branch = part_branch if branch is None else branch + part_branch
            grad_hidden32 = dot_nt(cotm, scaled_ref[cols, :]) * slope
            bias_acc[:, cols] += fold(grad_hidden32)
            grad_hidden = grad_hidden32.astype(bf16)
            part_grad = dot_nn(grad_hidden, up)
            grad_normed = part_grad if grad_normed is None else grad_normed + part_grad
            up_acc[:, cols] += dot_nn(normed_t, grad_hidden)
            down_acc[:, cols] += dot_nn(cotm_t, active)
        branch = branch + vec_ref[3:4, :]
        branch_ref[...] = branch.astype(bf16)
        inv_std = inv_ref[:, 0:1]
        scaled = grad_normed * vec_ref[1:2, :]
        mean_a = jnp.mean(scaled, axis=-1, keepdims=True)
        mean_b = jnp.mean(scaled * unit, axis=-1, keepdims=True)
        grad_conv = inv_std * (scaled - mean_a - unit * mean_b)
        grad_conv = jnp.where(inside, grad_conv, 0.0)
        gc_ref[...] = grad_conv.astype(bf16)
        vec_acc[0:8, :] += fold(grad_conv)
        vec_acc[8:16, :] += fold(grad_normed * unit)
        vec_acc[16:24, :] += fold(grad_normed)
        vec_acc[24:32, :] += fold(cotm32)
        vec_acc[32:40, :] += fold(cotm32 * branch)

    @pl.when(step == pl.num_programs(0) - 1)
    def _():
        for start in range(0, hidden_size, MLP_COLS):
            cols = slice(start, start + MLP_COLS)
            grad_ref[cols, 0:channels] = up_acc[:, cols].T.astype(bf16)
            grad_ref[cols, channels : 2 * channels] = (down_acc[:, cols].T * gamma).astype(bf16)
        bsum_ref[...] = jnp.sum(bias_acc[...], axis=0, keepdims=True)
        vsum_ref[...] = jnp.zeros_like(vsum_ref)
        for row in range(5):
            total = jnp.sum(vec_acc[8 * row : 8 * row + 8, :], axis=0, keepdims=True)
            if row == 3:
                total = total * gamma
            if row == 4:
                total = total * keep_scale
            vsum_ref[row : row + 1, :] = total


def taps_grad_kernel(
    keep_ref, slot_ref, side_ref, row_ref, above_ref, own_ref, below_ref, gc_ref,
    out_ref, pad_ref, acc_ref, grad_ref,
):
    image = pl.program_id(0)
    rows, cols, channels = own_ref.shape[1:]

    @pl.when(image == 0)
    def _():
        clear_edges(pad_ref, cols)
        acc_ref[...] = jnp.zeros_like(acc_ref)

    @pl.when(keep_ref[image] > 0)
    def _():
        side = side_ref[image]
        start = row_ref[0]
        fill_rows(pad_ref, 0, above_ref[0], side, start - REACH)
        fill_rows(pad_ref, REACH, own_ref[0], side, start)
        fill_rows(pad_ref, REACH + rows, below_ref[0], side, start + rows)
        grad_ref[...] = gc_ref[...].astype(f32)
        for tile in range(channels // LANES):
            lanes = slice(tile * LANES, (tile + 1) * LANES)
            lines = [grad_ref[row * cols : (row + 1) * cols, lanes] for row in range(rows)]
            for col_off in range(TAPS):
                sums = [None] * TAPS
                for row in range(rows + 2 * REACH):
                    at = EDGE - REACH + col_off
                    line = pad_ref[tile, row, at : at + cols, :]
                    for row_off in range(TAPS):
                        out = row - row_off
                        if 0 <= out < rows:
                            term = line * lines[out]
                            sums[row_off] = term if sums[row_off] is None else sums[row_off] + term
                for row_off in range(TAPS):
                    index = row_off * TAPS + col_off
                    acc_ref[index, :, lanes] += fold(sums[row_off])

    @pl.when(image == pl.num_programs(0) - 1)
    def _():
        out_ref[...] = jnp.sum(acc_ref[...], axis=1)


def finish_kernel(
    keep_ref, slot_ref, side_ref, row_ref, above_ref, own_ref, below_ref, branch_ref, image_ref, cot_ref, taps_ref, vec_ref,
    out_ref, gim_ref, pad_ref,
):
    image = pl.program_id(0)
    rows, cols, channels = image_ref.shape[1:]

    @pl.when(image == 0)
    def _():
        clear_edges(pad_ref, cols)

    @pl.when(keep_ref[image] > 0)
    def _():
        side = side_ref[image]
        start = row_ref[0]
        fill_rows(pad_ref, 0, above_ref[0])
        fill_rows(pad_ref, REACH, own_ref[...].astype(f32).reshape(rows, cols, channels))
        fill_rows(pad_ref, REACH + rows, below_ref[0])
        branch = branch_ref[...].astype(f32).reshape(rows, cols, channels)
        scale = vec_ref[4:5, :] * keep_scale
        for tile in range(channels // LANES):
            lanes = slice(tile * LANES, (tile + 1) * LANES)
            sums = conv_tile(pad_ref, tile, taps_ref, rows, cols, True)
            for row in range(rows):
                reach = jnp.where(start + row < side, side, 0)
                inside = lax.broadcasted_iota(jnp.int32, (cols, LANES), 0) < reach
                grad = cot_ref[0, row, :, lanes].astype(f32) + jnp.where(inside, sums[row], 0.0)
                gim_ref[0, row, :, lanes] = grad.astype(bf16)
                extra = jnp.where(inside, branch[row, :, lanes] * scale[:, lanes], 0.0)
                out = image_ref[0, row, :, lanes].astype(f32) + extra
                out_ref[0, row, :, lanes] = out.astype(bf16)

    @pl.when(keep_ref[image] == 0)
    def _():
        out_ref[...] = image_ref[...]
        gim_ref[...] = cot_ref[...]


def params(mib):
    return pltpu.CompilerParams(dimension_semantics=("arbitrary",), vmem_limit_bytes=mib * MIB)


def conv_norm(scalars, above, own, below, cot, taps, vecs):
    count, rows, cols, channels = own.shape
    pixels = rows * cols
    image_map = lambda i, k, s, d, r: (i, 0, 0, 0)
    whole = lambda i, k, s, d, r: (0, 0)
    slot_map = lambda i, k, s, d, r: (s[i], 0)
    return pl.pallas_call(
        conv_norm_kernel,
        grid_spec=pltpu.PrefetchScalarGridSpec(
            num_scalar_prefetch=4,
            grid=(count,),
            in_specs=[
                pl.BlockSpec((1, REACH, cols, channels), image_map),
                pl.BlockSpec((1, rows, cols, channels), image_map),
                pl.BlockSpec((1, REACH, cols, channels), image_map),
                pl.BlockSpec((1, rows, cols, channels), image_map),
                pl.BlockSpec(taps.shape, whole),
                pl.BlockSpec(vecs.shape, whole),
            ],
            out_specs=[
                pl.BlockSpec((pixels, channels), slot_map),
                pl.BlockSpec((pixels, LANES), slot_map),
                pl.BlockSpec((pixels, channels), slot_map),
            ],
            scratch_shapes=[
                pltpu.VMEM((channels // LANES, rows + 2 * REACH, cols + 2 * EDGE, LANES), f32),
                pltpu.VMEM((pixels, channels), f32),
            ],
        ),
        out_shape=[
            jax.ShapeDtypeStruct((count * pixels, channels), f32),
            jax.ShapeDtypeStruct((count * pixels, LANES), f32),
            jax.ShapeDtypeStruct((count * pixels, channels), bf16),
        ],
        compiler_params=params(40),
        name="conv_norm",
    )(*scalars, above, own, below, cot, taps, vecs)


def mlp(used, unit, inv_std, cotm, near, far, bias, vecs):
    total, channels = unit.shape
    hidden_size = bias.shape[1]
    steps = total // MLP_ROWS

    def tile_map(i, n):
        return (jnp.minimum(i, jnp.maximum((n[0] + MLP_ROWS - 1) // MLP_ROWS - 1, 0)), 0)

    whole = lambda i, n: (0, 0)
    return pl.pallas_call(
        mlp_kernel,
        grid_spec=pltpu.PrefetchScalarGridSpec(
            num_scalar_prefetch=1,
            grid=(steps,),
            in_specs=[
                pl.BlockSpec((MLP_ROWS, channels), tile_map),
                pl.BlockSpec((MLP_ROWS, LANES), tile_map),
                pl.BlockSpec((MLP_ROWS, channels), tile_map),
                pl.BlockSpec(near.shape, whole),
                pl.BlockSpec(far.shape, whole),
                pl.BlockSpec(bias.shape, whole),
                pl.BlockSpec(vecs.shape, whole),
            ],
            out_specs=[
                pl.BlockSpec((MLP_ROWS, channels), tile_map),
                pl.BlockSpec((MLP_ROWS, channels), tile_map),
                pl.BlockSpec((hidden_size, 2 * channels), whole),
                pl.BlockSpec((1, hidden_size), whole),
                pl.BlockSpec((8, channels), whole),
            ],
            scratch_shapes=[
                pltpu.VMEM((channels, hidden_size), f32),
                pltpu.VMEM((channels, hidden_size), f32),
                pltpu.VMEM((hidden_size, channels), bf16),
                pltpu.VMEM((8, hidden_size), f32),
                pltpu.VMEM((40, channels), f32),
            ],
        ),
        out_shape=[
            jax.ShapeDtypeStruct((total, channels), bf16),
            jax.ShapeDtypeStruct((total, channels), bf16),
            jax.ShapeDtypeStruct((hidden_size, 2 * channels), bf16),
            jax.ShapeDtypeStruct((1, hidden_size), f32),
            jax.ShapeDtypeStruct((8, channels), f32),
        ],
        compiler_params=params(56),
        name="mlp",
    )(used, unit, inv_std, cotm, near, far, bias, vecs)


def taps_grad(scalars, above, own, below, gc):
    count, rows, cols, channels = own.shape
    pixels = rows * cols
    image_map = lambda i, k, s, d, r: (i, 0, 0, 0)
    return pl.pallas_call(
        taps_grad_kernel,
        grid_spec=pltpu.PrefetchScalarGridSpec(
            num_scalar_prefetch=4,
            grid=(count,),
            in_specs=[
                pl.BlockSpec((1, REACH, cols, channels), image_map),
                pl.BlockSpec((1, rows, cols, channels), image_map),
                pl.BlockSpec((1, REACH, cols, channels), image_map),
                pl.BlockSpec((pixels, channels), lambda i, k, s, d, r: (s[i], 0)),
            ],
            out_specs=pl.BlockSpec((TAPS * TAPS, channels), lambda i, k, s, d, r: (0, 0)),
            scratch_shapes=[
                pltpu.VMEM((channels // LANES, rows + 2 * REACH, cols + 2 * EDGE, LANES), f32),
                pltpu.VMEM((TAPS * TAPS, 8, channels), f32),
                pltpu.VMEM((pixels, channels), f32),
            ],
        ),
        out_shape=jax.ShapeDtypeStruct((TAPS * TAPS, channels), f32),
        compiler_params=params(40),
        name="taps_grad",
    )(*scalars, above, own, below, gc)


def finish(scalars, above, gc, below, branch, images, cot, taps, vecs):
    count, rows, cols, channels = images.shape
    pixels = rows * cols
    image_map = lambda i, k, s, d, r: (i, 0, 0, 0)
    slot_map = lambda i, k, s, d, r: (s[i], 0)
    slot_halo = lambda i, k, s, d, r: (s[i], 0, 0, 0)
    whole = lambda i, k, s, d, r: (0, 0)
    return pl.pallas_call(
        finish_kernel,
        grid_spec=pltpu.PrefetchScalarGridSpec(
            num_scalar_prefetch=4,
            grid=(count,),
            in_specs=[
                pl.BlockSpec((1, REACH, cols, channels), slot_halo),
                pl.BlockSpec((pixels, channels), slot_map),
                pl.BlockSpec((1, REACH, cols, channels), slot_halo),
                pl.BlockSpec((pixels, channels), slot_map),
                pl.BlockSpec((1, rows, cols, channels), image_map),
                pl.BlockSpec((1, rows, cols, channels), image_map),
                pl.BlockSpec(taps.shape, whole),
                pl.BlockSpec(vecs.shape, whole),
            ],
            out_specs=[
                pl.BlockSpec((1, rows, cols, channels), image_map),
                pl.BlockSpec((1, rows, cols, channels), image_map),
            ],
            scratch_shapes=[
                pltpu.VMEM((channels // LANES, rows + 2 * REACH, cols + 2 * EDGE, LANES), f32),
            ],
        ),
        out_shape=[
            jax.ShapeDtypeStruct(images.shape, bf16),
            jax.ShapeDtypeStruct(images.shape, bf16),
        ],
        compiler_params=params(40),
        name="finish",
    )(*scalars, above, gc, below, branch, images, cot, taps, vecs)


def neighbour_rows(value, places):
    above = lax.ppermute(value[:, -REACH:], "space", [(i, i + 1) for i in range(places - 1)])
    below = lax.ppermute(value[:, :REACH], "space", [(i + 1, i) for i in range(places - 1)])
    return above, below


def spread(value, devices):
    sent = jnp.broadcast_to(value[None], (devices,) + value.shape)
    return lax.all_to_all(sent, AXES, 0, 0, tiled=True)


def flip_perm(size, bit):
    return [(i, i ^ bit) for i in range(size)]


def swap(value, bits):
    axis, bit, size = ("dp", bits[0], 8) if bits[0] else ("space", bits[1], 4)
    return lax.ppermute(value, axis, flip_perm(size, bit))


X, Y, CORE = (1, 0), (0, 2), (0, 1)
Z1, Z2, Z3 = (2, 0), (4, 0), (6, 0)


def cube_order():
    first = [0, 2 * 4]
    last = [4 * 4, 6 * 4]
    first = first + [v ^ 4 for v in first]
    last = last + [v ^ 2 for v in last]
    first = first + [v ^ 2 for v in first]
    last = last + [v ^ 4 for v in last]
    near = first + last
    return near + [v ^ 1 for v in near]


def join(*parts):
    return jnp.concatenate(parts, axis=0)


def gather_cube(piece):
    first = join(piece, swap(piece, Z1))
    last = join(swap(piece, Z2), swap(piece, Z3))
    first = join(first, swap(first, X))
    last = join(last, swap(last, Y))
    near = join(first, swap(first, Y), last, swap(last, X))
    return near, swap(near, CORE)


def scatter_cube(value):
    half = value.shape[0] // 2
    near = value[:half].astype(f32) + swap(value[half:], CORE).astype(f32)
    first, last = near[: half // 2], near[half // 2 :]
    rows = half // 4
    got_first = swap(first[rows:].astype(bf16), Y)
    got_last = swap(last[rows:].astype(bf16), X)
    first = first[:rows] + got_first.astype(f32)
    last = last[:rows] + got_last.astype(f32)
    rows = rows // 2
    got_first = swap(first[rows:].astype(bf16), X)
    got_last = swap(last[rows:].astype(bf16), Y)
    first = first[:rows] + got_first.astype(f32)
    last = last[:rows] + got_last.astype(f32)
    rows = rows // 2
    one = swap(first[rows:].astype(bf16), Z1)
    two = swap(last[:rows].astype(bf16), Z2)
    three = swap(last[rows:].astype(bf16), Z3)
    return first[:rows] + one.astype(f32) + two.astype(f32) + three.astype(f32)


def by_owner(value, devices):
    rows, width = value.shape
    return value.reshape(rows, devices, width // devices).transpose(1, 0, 2).reshape(devices, -1)


def from_owner(value, rows):
    devices = value.shape[0]
    return value.reshape(devices, rows, -1).transpose(1, 0, 2).reshape(rows, -1)


def pack_lanes(value):
    devices, size = value.shape
    padded = -(-size // (8 * LANES)) * 8 * LANES
    return jnp.pad(value, ((0, 0), (0, padded - size))).reshape(devices, padded // LANES, LANES)


def adam_update(weight, moment, square, grad_part, factor, step_rate):
    scaled = grad_part * factor
    new_moment = beta_one * moment + (1.0 - beta_one) * scaled
    new_square = beta_two * square + (1.0 - beta_two) * scaled * scaled
    corrected = new_moment / (1.0 - beta_one**STEP)
    spread_ = jnp.sqrt(new_square / (1.0 - beta_two**STEP))
    new_weight = weight - step_rate * (corrected / (spread_ + adam_eps) + decay_rate * weight)
    return (new_weight, new_moment, new_square)


def body(
    dp_size, space_size,
    images, cotangent, image_sides, keep_flags,
    depth_kernel, kernel_moment, kernel_square,
    block_vectors, vector_moment, vector_square,
    up_weight, up_moment, up_square,
    up_bias, bias_moment, bias_square,
    down_weight, down_moment, down_square,
):
    devices = dp_size * space_size
    count, rows, cols, channels = images.shape
    pixels = rows * cols
    part = up_weight.shape[1]
    width = depth_kernel.shape[1]
    taps_n, vecs_n = depth_kernel.shape[0], block_vectors.shape[0]
    place = lax.axis_index("space")
    me = lax.axis_index(AXES)
    cube = dp_size == 8 and space_size == 4

    above, below = neighbour_rows(images, space_size)
    small = jnp.concatenate([depth_kernel.reshape(-1), block_vectors.reshape(-1), up_bias])
    small_all = spread(pack_lanes(small[None])[0], devices).reshape(devices, -1)
    piece = jnp.concatenate([up_weight.astype(bf16).T, down_weight.astype(bf16)], axis=1)
    if cube:
        near, far = gather_cube(piece)
        order = me ^ jnp.array(cube_order(), jnp.int32)
    else:
        whole = lax.all_gather(piece, AXES, axis=0, tiled=True)
        near, far = whole[: whole.shape[0] // 2], whole[whole.shape[0] // 2 :]
        order = jnp.arange(devices, dtype=jnp.int32)
    cut_a, cut_b = taps_n * width, (taps_n + vecs_n) * width
    taps = from_owner(small_all[:, :cut_a], taps_n)
    vecs = jnp.pad(from_owner(small_all[:, cut_a:cut_b], vecs_n), ((0, 3), (0, 0)))
    bias_own = small_all[:, cut_b : cut_b + part]
    hits = (order[:, None] == jnp.arange(devices, dtype=jnp.int32)[None, :])
    bias = jnp.sum(jnp.where(hits[:, :, None], bias_own[None], 0.0), axis=1).reshape(1, -1)

    keep = (keep_flags > 0).astype(jnp.int32)
    ids = jnp.arange(count, dtype=jnp.int32)
    before = jnp.sum(jnp.where(ids[None, :] <= ids[:, None], keep[None, :], 0), axis=1)
    slot = jnp.maximum(before - 1, 0)
    used = (jnp.sum(keep) * pixels).reshape(1)
    first_row = (place * rows).astype(jnp.int32).reshape(1)
    scalars = (keep, slot, image_sides, first_row)

    unit, inv_std, cotm = conv_norm(scalars, above, images, below, cotangent, taps, vecs)
    branch, gc, grads, bias_sum, vec_sum = mlp(used, unit, inv_std, cotm, near, far, bias, vecs)
    gc_above, gc_below = neighbour_rows(gc.reshape(count, rows, cols, channels), space_size)
    taps_sum = taps_grad(scalars, above, images, below, gc)
    if cube:
        own = scatter_cube(grads)
    else:
        own = lax.psum_scatter(grads.astype(f32), AXES, scatter_dimension=0, tiled=True)
    bias_rows = bias_sum.reshape(devices, part)
    bias_true = jnp.sum(jnp.where(hits[:, :, None], bias_rows[:, None], 0.0), axis=0)
    mine = jnp.concatenate([by_owner(taps_sum, devices), by_owner(vec_sum[:vecs_n], devices), bias_true], axis=1)
    got = jnp.sum(lax.all_to_all(pack_lanes(mine), AXES, 0, 0, tiled=True), axis=0).reshape(-1)
    grad_kernel = got[:cut_a].reshape(taps_n, width)
    grad_vectors = got[cut_a:cut_b].reshape(vecs_n, width)
    grad_bias = got[cut_b : cut_b + part]
    grad_up = own[:, :channels].T
    grad_down = own[:, channels:]
    local = jnp.sum(own * own) + jnp.sum(got * got)
    total = jnp.sum(spread(jnp.broadcast_to(local, (8, LANES)), devices)[:, 0, 0] if False else spread(jnp.broadcast_to(local, (8, LANES)), devices).reshape(devices, 8, LANES)[:, 0, 0])
    out_images, grad_images = finish(scalars, gc_above, gc, gc_below, branch, images, cotangent, taps, vecs)
    grad_norm = jnp.sqrt(total)
    factor = clip_limit / jnp.maximum(grad_norm, clip_limit)
    states = (
        (depth_kernel, kernel_moment, kernel_square),
        (block_vectors, vector_moment, vector_square),
        (up_weight, up_moment, up_square),
        (up_bias, bias_moment, bias_square),
        (down_weight, down_moment, down_square),
    )
    shards = (grad_kernel, grad_vectors, grad_up, grad_bias, grad_down)
    results = []
    for (weight, moment, square), grad_part, step_rate in zip(states, shards, step_rates):
        results.extend(adam_update(weight, moment, square, grad_part, factor, step_rate))
    return (out_images, grad_images, *results, grad_norm)


def solution(mesh):
    lanes = P(None, AXES)
    flat = P(AXES)
    tall = P(AXES, None)
    maps = P("dp", "space", None, None)
    in_specs = (maps, maps, P("dp"), P("dp")) + (lanes,) * 9 + (flat,) * 3 + (tall,) * 3
    out_specs = (maps, maps) + (lanes,) * 9 + (flat,) * 3 + (tall,) * 3 + (P(),)
    run = functools.partial(body, mesh.shape["dp"], mesh.shape["space"])
    return jax.shard_map(run, mesh=mesh, in_specs=in_specs, out_specs=out_specs, check_vma=False)
```

time: 862 us -> 347 us (0.40)
  other arithmetic: 362 us -> 27.5 us
  blocking collectives: 220 us -> 0 us
  Pallas kernels: 0 us -> 152 us
  matrix products: 101 us -> 0 us
  local copies, waits for them, and re-layouts: 88.7 us -> 65.8 us
  starting transfers between devices: 17.8 us -> 40 us
  between operations: 19.9 us -> 4.87 us
  waiting for transfers between devices: 41.3 us -> 51 us
    convert_element_type x5 -> x2, other arithmetic: 190 us -> 0.89 us  [the longest x1 0.89 us: body(): down_weight.astype(bf16)]
    pallas_call x0 -> x4, Pallas kernels: none -> 152 us  [the longest x1 55 us: mlp(): pl.pallas_call(mlp_kernel, grid_spec=pltpu.PrefetchScalarGridSpec(num_sca...]
    reduce_sum x12 -> x8, other arithmetic: 159 us -> 8.16 us  [the longest x2 1.89 us: body(): local = jnp.sum(own * own) + jnp.sum(got * got)]
    all_gather x2 -> x0, blocking collectives: 115 us -> none  [the longest x1 75.1 us: body(): lax.all_gather(block_vectors, ('dp', 'space'), axis=1, tiled=True)]
    dot_general x6 -> x0, matrix products: 101 us -> none  [the longest x1 21.6 us: body(): jnp.einsum('nijc,hc->nijh', grad_branch, down_full, preferred_element_typ...]
    psum x1 -> x0, blocking collectives: 68.2 us -> none  [body(): lax.psum((local_grads[0], local_grads[1], local_grads[2], local_grads[3],...]
    another operation x57 -> x1, local copies, waits for them, and re-layouts: 44.7 us -> 0.66 us  [spread(): sent = jnp.broadcast_to(value[None], (devices,) + value.shape)]
    ppermute x0 -> x20, waiting for transfers between devices: none -> 40.6 us  [the longest x16 40.6 us: swap(): return lax.ppermute(value, axis, flip_perm(size, bit))]
  transfers between devices with their start and end apart: 7 -> 23, of which waited for: 1 -> 8; matrix products, arithmetic and copies ran while one was open for 38% -> 18% of each run, Pallas kernels for 0% -> 28%
where the time goes in v1:
time: 347 us; the launch traced here: 341 us
  Pallas kernels  152 us (44%)
  local copies, waits for them, and re-layouts  65.8 us (19%)
  waiting for transfers between devices  51 us (15%)
  starting transfers between devices  40 us (12%)
  other arithmetic  27.5 us (8%)
  between operations  4.87 us (1%)
    pallas_call x1, Pallas kernels, mlp(): pl.pallas_call(mlp_kernel, grid_spec=pltpu.PrefetchScalarGridSpec(num_sca...  55 us
    ppermute x16, waiting for transfers between devices, swap(): return lax.ppermute(value, axis, flip_perm(size, bit))  40.6 us
    pallas_call x1, Pallas kernels, conv_norm(): pl.pallas_call(conv_norm_kernel, grid_spec=pltpu.PrefetchScalarGridSpec(n...  38.7 us
    pallas_call x1, Pallas kernels, finish(): pl.pallas_call(finish_kernel, grid_spec=pltpu.PrefetchScalarGridSpec(num_...  31.8 us
    pallas_call x1, Pallas kernels, taps_grad(): pl.pallas_call(taps_grad_kernel, grid_spec=pltpu.PrefetchScalarGridSpec(n...  26.5 us
    unnamed x73, local copies, waits for them, and re-layouts  21.7 us
    ppermute x16, starting transfers between devices, swap(): return lax.ppermute(value, axis, flip_perm(size, bit))  15.4 us
    all_to_all x1, waiting for transfers between devices, body(): lax.all_to_all(pack_lanes(mine), AXES, 0, 0, tiled=True)  10.4 us
  transfers between devices with their start and end apart: 23, of which 8 were waited for; matrix products, arithmetic and copies ran while one was open for 18% of the time, Pallas kernels for 28%

profile of v1, /device:TPU:0, one launch (start us, length us, event | category | flops | bytes accessed | tf_op | source)
XLA Modules:
  0.0 341.2 jit_solution(557560551131528691)
XLA Ops:
  2.5 4.1 %collective-permute-start.5 = (bf16[48,768]{1,0:T(8,128)(2,1)S(1)}, bf16[48,768]{1,0:T(8,128)(2,1)S(1)}, u32[]{:S(2)}, u32[]{:S(2)}) collective-permute-start(bf16[48,768]{1,0:T(8,128)(2,1)S(1)} %get-tuple-element.139), channel_id=1, source_target_pairs={{0,16},{4,20},{8,24},{12,28},{16,0},{20,4},{24,8},{28,12},{1,17},{... | collective-permute-start | bytes 221192 | tf_op jit(solution)/shard_map/ppermute | solution.py:471
  6.6 1.6 collective-permute-start.2
  11.2 6.2 %all-to-all-start = ((f32[32,8,128]{2,1,0:T(8,128)}), f32[32,8,128]{2,1,0:T(8,128)}, u32[]{:S(2)}, u32[]{:S(2)}) async-start(f32[32,8,128]{2,1,0:T(8,128)} %broadcast_in_dim.72), calls=%async_computation | async-start | bytes 262144 | tf_op jit(solution)/shard_map/all_to_all | solution.py:462
  17.4 1.8 collective-permute-start.3
  19.2 4.2 %fusion.19 = (bf16[32,3,24,384]{3,2,1,0:T(8,128)(2,1)}, bf16[32,3,24,384]{3,2,1,0:T(8,128)(2,1)}) fusion(bf16[32,6,24,384]{3,2,1,0:T(8,128)(2,1)} %own_ref.3), kind=kLoop, calls=%fused_computation.72 | loop fusion | bytes 7077888 | tf_op jit(solution)/shard_map/slice | solution.py:456
  23.4 1.3 collective-permute-start.1
  24.7 4.2 %collective-permute-start = (bf16[32,3,24,384]{3,2,1,0:T(8,128)(2,1)}, bf16[32,3,24,384]{3,2,1,0:T(8,128)(2,1)}, u32[]{:S(2)}, u32[]{:S(2)}) collective-permute-start(bf16[32,3,24,384]{3,2,1,0:T(8,128)(2,1)} %get-tuple-element.132), channel_id=1, source_target_pairs={{0,1},{1,2},{2,3},{4,5},{5,6},{6,7},{8,9},{9,10},{10,11},{12,13},{... | collective-permute-start | bytes 5308424 | tf_op jit(solution)/shard_map/ppermute | solution.py:455
  28.9 1.6 collective-permute-start.7
  31.1 22.7 %collective-permute-done.7 = bf16[96,768]{1,0:T(8,128)(2,1)S(1)} collective-permute-done((bf16[96,768]{1,0:T(8,128)(2,1)S(1)}, bf16[96,768]{1,0:T(8,128)(2,1)S(1)}, u32[]{:S(2)}, u32[]{:S(2)}) %collective-permute-start.7) | collective-permute-done | bytes 147488 | tf_op jit(solution)/shard_map/ppermute | solution.py:471
  54.4 2.5 collective-permute-done.4
  58.0 5.7 %collective-permute-done.8 = bf16[192,768]{1,0:T(8,128)(2,1)S(1)} collective-permute-done((bf16[192,768]{1,0:T(8,128)(2,1)S(1)}, bf16[192,768]{1,0:T(8,128)(2,1)S(1)}, u32[]{:S(2)}, u32[]{:S(2)}) %collective-permute-start.8) | collective-permute-done | bytes 294944 | tf_op jit(solution)/shard_map/ppermute | solution.py:471
  69.4 1.5 select_reduce_fusion.1
  71.0 1.4 reshape.127.bias_ref
  73.0 1.4 reshape.125
  74.4 1.5 copy.116
  75.9 1.6 reshape.126
  78.2 1.8 copy.129
  80.0 1.7 reshape.123
  81.8 1.9 copy.114
  83.7 1.6 reshape.124
  85.3 1.7 copy.117.taps_ref
  89.3 38.7 %conv_norm.1 = (f32[4608,384]{1,0:T(8,128)}, f32[4608,128]{1,0:T(8,128)S(1)}, bf16[4608,384]{1,0:T(8,128)(2,1)S(1)}) custom-call(s32[32]{0:T(128)S(1)} %copy-done.14, s32[32]{0:T(128)S(1)} %copy-done.17, s32[32]{0:T(128)S(1)} %copy-done.12, s32[1]{0:T(128)} %bitcast.row_ref, bf16[32,3,24,384]{3,2,1,0:T(8,128)(2,1)} %collective-permute-done.above_ref, ...), custom_call_target="tpu_custom_call" | custom-call | tf_op jit(solution)/shard_map/conv_norm/pallas_call | solution.py:304
  128.0 1.8 copy-done.5
  129.8 1.5 copy-done.6
  131.3 55.0 %mlp.1 = (bf16[4608,384]{1,0:T(8,128)(2,1)}, bf16[4608,384]{1,0:T(8,128)(2,1)}, bf16[1536,768]{1,0:T(8,128)(2,1)}, f32[1,1536]{1,0:T(1,128)}, f32[8,384]{1,0:T(8,128)}) custom-call(s32[1]{0:T(128)} %bitcast.1.count_ref, f32[4608,384]{1,0:T(8,128)} %get-tuple-element.28.unit_ref, f32[4608,128]{1,0:T(8,128)} %copy-done.6, bf16[4608,384]{1,0:T(8,128)(2,1)} %copy-done.5, ...), custom_call_target="tpu_custom_call" | custom-call | tf_op jit(solution)/shard_map/mlp/pallas_call | solution.py:346
  186.3 1.5 slice.107
  188.2 2.5 collective-permute-done.12
  190.7 1.8 fusion.11
  193.8 2.2 fusion.18
  196.0 1.3 reduce.2
  197.3 1.4 broadcast_in_dim.76
  198.7 1.4 reshape.131
  200.1 1.6 copy.121
  201.7 1.4 reshape.132
  203.1 1.4 copy.123
  204.6 2.0 copy-done.2
  206.6 26.5 %taps_grad.1 = f32[49,384]{1,0:T(8,128)S(1)} custom-call(s32[32]{0:T(128)S(1)} %copy-done.15, s32[32]{0:T(128)S(1)} %copy-done.18, s32[32]{0:T(128)S(1)} %copy-done.12, s32[1]{0:T(128)} %bitcast.row_ref, bf16[32,3,24,384]{3,2,1,0:T(8,128)(2,1)} %collective-permute-done.above_ref, bf16[32,6,24,384]{3,2,1,0:T(8,128)(2,1)S(1)} %copy-done, ...), custom_call_target="tpu_custom_call" | custom-call | tf_op jit(solution)/shard_map/taps_grad/pallas_call | solution.py:391
  233.7 1.7 copy.119
  235.4 1.6 reshape.129
  237.1 1.9 copy.120
  239.0 1.8 reshape.130
  240.8 1.7 copy.122
  242.5 1.3 collective-permute-start.11
  243.8 4.3 %collective-permute-start.10 = (bf16[32,3,24,384]{3,2,1,0:T(8,128)(2,1)}, bf16[32,3,24,384]{3,2,1,0:T(8,128)(2,1)}, u32[]{:S(2)}, u32[]{:S(2)}) collective-permute-start(bf16[32,3,24,384]{3,2,1,0:T(8,128)(2,1)} %get-tuple-element.130), channel_id=1, source_target_pairs={{0,1},{1,2},{2,3},{4,5},{5,6},{6,7},{8,9},{9,10},{10,11},{12,13},{... | collective-permute-start | bytes 5308424 | tf_op jit(solution)/shard_map/ppermute | solution.py:455
  250.7 3.7 %all-to-all-start.1 = ((f32[32,8,128]{2,1,0:T(8,128)}), f32[32,8,128]{2,1,0:T(8,128)}, u32[]{:S(2)}, u32[]{:S(2)}) async-start(f32[32,8,128]{2,1,0:T(8,128)} %bitcast.42), calls=%async_computation.1 | async-start | bytes 262144 | tf_op jit(solution)/shard_map/all_to_all | solution.py:605
  254.4 2.3 slice_add_fusion.1
  258.3 1.5 collective-permute-start.17
  259.8 10.4 %all-to-all-done.1 = f32[32,8,128]{2,1,0:T(8,128)} async-done(((f32[32,8,128]{2,1,0:T(8,128)}), f32[32,8,128]{2,1,0:T(8,128)}, u32[]{:S(2)}, u32[]{:S(2)}) %all-to-all-start.1) | async-done | bytes 131104 | tf_op jit(solution)/shard_map/all_to_all | solution.py:605
  270.2 1.5 reduce_sum.76
  271.7 1.0 slice.183
  272.8 1.7 collective-permute-start.14
  276.5 3.0 collective-permute-done.14
  280.3 2.9 collective-permute-done.18
  283.2 1.3 collective-permute-done.15
  284.5 1.3 multiply_reduce_fusion
  287.7 3.6 %all-to-all-start.2 = ((f32[32,8,128]{2,1,0:T(8,128)}), f32[32,8,128]{2,1,0:T(8,128)}, u32[]{:S(2)}, u32[]{:S(2)}) async-start(f32[32,8,128]{2,1,0:T(8,128)} %broadcast_in_dim_broadcast_in_dim_broadcast_in_dim.3), calls=%async_computation.2 | async-start | bytes 262144 | tf_op jit(solution)/shard_map/all_to_all | solution.py:462
  291.4 2.0 copy-done.3
  293.4 2.0 copy-done.4
  297.6 31.8 %finish.1 = (bf16[32,6,24,384]{3,2,1,0:T(8,128)(2,1)}, bf16[32,6,24,384]{3,2,1,0:T(8,128)(2,1)}) custom-call(s32[32]{0:T(128)S(1)} %copy-done.16, s32[32]{0:T(128)S(1)} %copy-done.19, s32[32]{0:T(128)S(1)} %copy-done.12, s32[1]{0:T(128)} %bitcast.row_ref, bf16[32,3,24,384]{3,2,1,0:T(8,128)(2,1)} %collective-permute-done.10.above_ref, ...), custom_call_target="tpu_custom_call" | custom-call | tf_op jit(solution)/shard_map/finish/pallas_call | solution.py:422
  329.4 1.6 slice_reduce_fusion
  333.4 1.3 multiply_subtract_fusion.4
  334.7 1.7 multiply_subtract_fusion
  336.4 1.7 multiply_subtract_fusion.1
  338.1 1.3 multiply_subtract_fusion.3
  (132 shorter events, 30.3 us)
Async XLA Ops:
  2.5 26.4 %collective-permute-start.5 = (bf16[48,768]{1,0:T(8,128)(2,1)S(1)}, bf16[48,768]{1,0:T(8,128)(2,1)S(1)}, u32[]{:S(2)}, u32[]{:S(2)}) collective-permute-start(bf16[48,768]{1,0:T(8,128)(2,1)S(1)} %get-tuple-element.139), channel_id=1, source_target_pairs={{0,16},{4,20},{8,24},{12,28},{16,0},{20,4},{24,8},{28,12},{1,17},{... | collective-permute-start | bytes 221192 | tf_op jit(solution)/shard_map/ppermute | solution.py:471
  6.6 10.9 %collective-permute-start.2 = (bf16[48,768]{1,0:T(8,128)(2,1)S(1)}, bf16[48,768]{1,0:T(8,128)(2,1)S(1)}, u32[]{:S(2)}, u32[]{:S(2)}) collective-permute-start(bf16[48,768]{1,0:T(8,128)(2,1)S(1)} %get-tuple-element.139), channel_id=1, source_target_pairs={{0,8},{4,12},{8,0},{12,4},{16,24},{20,28},{24,16},{28,20},{1,9},{5... | collective-permute-start | bytes 221192 | tf_op jit(solution)/shard_map/ppermute | solution.py:471
  8.1 20.8 %collective-permute-start.6 = (bf16[48,768]{1,0:T(8,128)(2,1)S(1)}, bf16[48,768]{1,0:T(8,128)(2,1)S(1)}, u32[]{:S(2)}, u32[]{:S(2)}) collective-permute-start(bf16[48,768]{1,0:T(8,128)(2,1)S(1)} %get-tuple-element.139), channel_id=1, source_target_pairs={{0,24},{4,28},{8,16},{12,20},{16,8},{20,12},{24,0},{28,4},{1,25},{... | collective-permute-start | bytes 221192 | tf_op jit(solution)/shard_map/ppermute | solution.py:471
  11.2 56.5 %all-to-all-start = ((f32[32,8,128]{2,1,0:T(8,128)}), f32[32,8,128]{2,1,0:T(8,128)}, u32[]{:S(2)}, u32[]{:S(2)}) async-start(f32[32,8,128]{2,1,0:T(8,128)} %broadcast_in_dim.72), calls=%async_computation | async-start | bytes 262144 | tf_op jit(solution)/shard_map/all_to_all | solution.py:462
  17.4 13.1 %collective-permute-start.3 = (bf16[96,768]{1,0:T(8,128)(2,1)S(1)}, bf16[96,768]{1,0:T(8,128)(2,1)S(1)}, u32[]{:S(2)}, u32[]{:S(2)}) collective-permute-start(bf16[96,768]{1,0:T(8,128)(2,1)S(1)} %pad_maximum_fusion.2), channel_id=1, source_target_pairs={{0,4},{4,0},{8,12},{12,8},{16,20},{20,16},{24,28},{28,24},{1,5},{5... | collective-permute-start | bytes 442376 | tf_op jit(solution)/shard_map/ppermute | solution.py:471
  23.4 63.7 %collective-permute-start.1 = (bf16[32,3,24,384]{3,2,1,0:T(8,128)(2,1)}, bf16[32,3,24,384]{3,2,1,0:T(8,128)(2,1)}, u32[]{:S(2)}, u32[]{:S(2)}) collective-permute-start(bf16[32,3,24,384]{3,2,1,0:T(8,128)(2,1)} %get-tuple-element.131), channel_id=1, source_target_pairs={{1,0},{2,1},{3,2},{5,4},{6,5},{7,6},{9,8},{10,9},{11,10},{13,12},{... | collective-permute-start | bytes 5308424 | tf_op jit(solution)/shard_map/ppermute | solution.py:456
  24.7 62.4 %collective-permute-start = (bf16[32,3,24,384]{3,2,1,0:T(8,128)(2,1)}, bf16[32,3,24,384]{3,2,1,0:T(8,128)(2,1)}, u32[]{:S(2)}, u32[]{:S(2)}) collective-permute-start(bf16[32,3,24,384]{3,2,1,0:T(8,128)(2,1)} %get-tuple-element.132), channel_id=1, source_target_pairs={{0,1},{1,2},{2,3},{4,5},{5,6},{6,7},{8,9},{9,10},{10,11},{12,13},{... | collective-permute-start | bytes 5308424 | tf_op jit(solution)/shard_map/ppermute | solution.py:455
  28.9 24.9 %collective-permute-start.7 = (bf16[96,768]{1,0:T(8,128)(2,1)S(1)}, bf16[96,768]{1,0:T(8,128)(2,1)S(1)}, u32[]{:S(2)}, u32[]{:S(2)}) collective-permute-start(bf16[96,768]{1,0:T(8,128)(2,1)S(1)} %pad_maximum_fusion.3), channel_id=1, source_target_pairs={{0,2},{1,3},{2,0},{3,1},{4,6},{5,7},{6,4},{7,5},{8,10},{9,11},{10,... | collective-permute-start | bytes 442376 | tf_op jit(solution)/shard_map/ppermute | solution.py:471
  30.5 26.4 %collective-permute-start.4 = (bf16[192,768]{1,0:T(8,128)(2,1)S(1)}, bf16[192,768]{1,0:T(8,128)(2,1)S(1)}, u32[]{:S(2)}, u32[]{:S(2)}) collective-permute-start(bf16[192,768]{1,0:T(8,128)(2,1)S(1)} %pad_maximum_fusion), channel_id=1, source_target_pairs={{0,2},{1,3},{2,0},{3,1},{4,6},{5,7},{6,4},{7,5},{8,10},{9,11},{10,... | collective-permute-start | bytes 884744 | tf_op jit(solution)/shard_map/ppermute | solution.py:471
  53.8 10.8 %copy-start.29 = (s32[32]{0:T(128)S(1)}, s32[32]{0:T(128)}, u32[]{:S(2)}) copy-start(s32[32]{0:T(128)} %param.23) | copy-start | bytes 388
  53.8 12.0 %copy-start.30 = (s32[32]{0:T(128)S(1)}, s32[32]{0:T(128)}, u32[]{:S(2)}) copy-start(s32[32]{0:T(128)} %constant.45.clone) | copy-start | bytes 388
  53.8 9.9 %collective-permute-start.8 = (bf16[192,768]{1,0:T(8,128)(2,1)S(1)}, bf16[192,768]{1,0:T(8,128)(2,1)S(1)}, u32[]{:S(2)}, u32[]{:S(2)}) collective-permute-start(bf16[192,768]{1,0:T(8,128)(2,1)S(1)} %pad_maximum_fusion.1), channel_id=1, source_target_pairs={{0,4},{4,0},{8,12},{12,8},{16,20},{20,16},{24,28},{28,24},{1,5},{5... | collective-permute-start | bytes 884744 | tf_op jit(solution)/shard_map/ppermute | solution.py:471
  57.0 1.0 copy-start.23
  63.7 23.3 %copy-start = (bf16[32,6,24,384]{3,2,1,0:T(8,128)(2,1)S(1)}, bf16[32,6,24,384]{3,2,1,0:T(8,128)(2,1)}, u32[]{:S(2)}) copy-start(bf16[32,6,24,384]{3,2,1,0:T(8,128)(2,1)} %own_ref.3) | copy-start | bytes 10616836
  64.5 66.8 %collective-permute-start.9 = (bf16[768,768]{1,0:T(8,128)(2,1)}, bf16[768,768]{1,0:T(8,128)(2,1)}, u32[]{:S(2)}, u32[]{:S(2)}) collective-permute-start(bf16[768,768]{1,0:T(8,128)(2,1)} %constant_dynamic-update-slice_fusion.near_ref), channel_id=1, source_target_pairs={{0,1},{1,0},{2,3},{3,2},{4,5},{5,4},{6,7},{7,6},{8,9},{9,8},{10,11... | collective-permute-start | bytes 3538952 | tf_op jit(solution)/shard_map/ppermute | solution.py:471
  64.7 0.5 copy-start.13
  78.2 8.8 %copy-start.10 = (f32[8,384]{1,0:T(8,128)}, f32[8,384]{1,0:T(8,128)S(1)}, u32[]{:S(2)}) copy-start(f32[8,384]{1,0:T(8,128)S(1)} %pad.13.vec_ref) | copy-start | bytes 36868
  78.2 8.8 %copy-start.12 = (s32[32]{0:T(128)S(1)}, s32[32]{0:T(128)}, u32[]{:S(2)}) copy-start(s32[32]{0:T(128)} %side_ref.5) | copy-start | bytes 388
  87.1 0.9 copy-start.7
  88.0 0.7 copy-start.14
  88.6 0.7 copy-start.17
  128.0 1.8 copy-start.5
  129.8 1.5 copy-start.6
  186.3 4.4 %copy-start.20 = (bf16[1536,768]{1,0:T(8,128)(2,1)S(1)}, bf16[1536,768]{1,0:T(8,128)(2,1)}, u32[]{:S(2)}) copy-start(bf16[1536,768]{1,0:T(8,128)(2,1)} %get-tuple-element.37) | copy-start | bytes 7077892
  187.8 2.9 collective-permute-start.12
  190.7 3.1 copy-start.1
  193.4 61.0 %collective-permute-start.13 = (bf16[192,768]{1,0:T(8,128)(2,1)}, bf16[192,768]{1,0:T(8,128)(2,1)}, u32[]{:S(2)}, u32[]{:S(2)}) collective-permute-start(bf16[192,768]{1,0:T(8,128)(2,1)} %get-tuple-element.135), channel_id=1, source_target_pairs={{0,2},{1,3},{2,0},{3,1},{4,6},{5,7},{6,4},{7,5},{8,10},{9,11},{10,... | collective-permute-start | bytes 884744 | tf_op jit(solution)/shard_map/ppermute | solution.py:471
  193.4 61.1 %collective-permute-start.16 = (bf16[192,768]{1,0:T(8,128)(2,1)}, bf16[192,768]{1,0:T(8,128)(2,1)}, u32[]{:S(2)}, u32[]{:S(2)}) collective-permute-start(bf16[192,768]{1,0:T(8,128)(2,1)} %get-tuple-element.136), channel_id=1, source_target_pairs={{0,4},{4,0},{8,12},{12,8},{16,20},{20,16},{24,28},{28,24},{1,5},{5... | collective-permute-start | bytes 884744 | tf_op jit(solution)/shard_map/ppermute | solution.py:471
  193.8 10.8 %copy-start.15 = (s32[32]{0:T(128)S(1)}, s32[32]{0:T(128)}, u32[]{:S(2)}) copy-start(s32[32]{0:T(128)} %copy-done.13) | copy-start | bytes 388
  193.8 10.8 %copy-start.18 = (s32[32]{0:T(128)S(1)}, s32[32]{0:T(128)}, u32[]{:S(2)}) copy-start(s32[32]{0:T(128)} %add_maximum_fusion.slot_ref) | copy-start | bytes 388
  204.6 2.0 copy-start.2
  233.1 0.6 copy-start.9
  233.7 14.3 %copy-start.25 = (pred[32,32]{1,0:T(8,128)(4,1)S(1)}, pred[32,32]{1,0:T(8,128)(4,1)}, u32[]{:S(2)}) copy-start(pred[32,32]{1,0:T(8,128)(4,1)} %iota_compare_fusion.1) | copy-start | bytes 3076
  242.5 48.8 %collective-permute-start.11 = (bf16[32,3,24,384]{3,2,1,0:T(8,128)(2,1)}, bf16[32,3,24,384]{3,2,1,0:T(8,128)(2,1)}, u32[]{:S(2)}, u32[]{:S(2)}) collective-permute-start(bf16[32,3,24,384]{3,2,1,0:T(8,128)(2,1)} %get-tuple-element.129), channel_id=1, source_target_pairs={{1,0},{2,1},{3,2},{5,4},{6,5},{7,6},{9,8},{10,9},{11,10},{13,12},{... | collective-permute-start | bytes 5308424 | tf_op jit(solution)/shard_map/ppermute | solution.py:456
  243.8 47.5 %collective-permute-start.10 = (bf16[32,3,24,384]{3,2,1,0:T(8,128)(2,1)}, bf16[32,3,24,384]{3,2,1,0:T(8,128)(2,1)}, u32[]{:S(2)}, u32[]{:S(2)}) collective-permute-start(bf16[32,3,24,384]{3,2,1,0:T(8,128)(2,1)} %get-tuple-element.130), channel_id=1, source_target_pairs={{0,1},{1,2},{2,3},{4,5},{5,6},{6,7},{8,9},{9,10},{10,11},{12,13},{... | collective-permute-start | bytes 5308424 | tf_op jit(solution)/shard_map/ppermute | solution.py:455
  250.7 19.5 %all-to-all-start.1 = ((f32[32,8,128]{2,1,0:T(8,128)}), f32[32,8,128]{2,1,0:T(8,128)}, u32[]{:S(2)}, u32[]{:S(2)}) async-start(f32[32,8,128]{2,1,0:T(8,128)} %bitcast.42), calls=%async_computation.1 | async-start | bytes 262144 | tf_op jit(solution)/shard_map/all_to_all | solution.py:605
  256.8 0.8 copy-start.21
  258.3 16.2 %collective-permute-start.17 = (bf16[96,768]{1,0:T(8,128)(2,1)}, bf16[96,768]{1,0:T(8,128)(2,1)}, u32[]{:S(2)}, u32[]{:S(2)}) collective-permute-start(bf16[96,768]{1,0:T(8,128)(2,1)} %slice.182), channel_id=1, source_target_pairs={{0,2},{1,3},{2,0},{3,1},{4,6},{5,7},{6,4},{7,5},{8,10},{9,11},{10,... | collective-permute-start | bytes 442376 | tf_op jit(solution)/shard_map/ppermute | solution.py:471
  271.7 7.8 %copy-start.22 = (f32[192,768]{1,0:T(8,128)S(1)}, f32[192,768]{1,0:T(8,128)}, u32[]{:S(2)}) copy-start(f32[192,768]{1,0:T(8,128)} %get-tuple-element.133) | copy-start | bytes 1769476
  271.7 8.0 %copy-start.24 = (f32[8,128]{1,0:T(8,128)S(1)}, f32[8,128]{1,0:T(8,128)}, u32[]{:S(2)}) copy-start(f32[8,128]{1,0:T(8,128)} %reduce_sum.76) | copy-start | bytes 12292
  272.8 6.8 %collective-permute-start.14 = (bf16[96,768]{1,0:T(8,128)(2,1)S(1)}, bf16[96,768]{1,0:T(8,128)(2,1)S(1)}, u32[]{:S(2)}, u32[]{:S(2)}) collective-permute-start(bf16[96,768]{1,0:T(8,128)(2,1)S(1)} %slice.183), channel_id=1, source_target_pairs={{0,4},{4,0},{8,12},{12,8},{16,20},{20,16},{24,28},{28,24},{1,5},{5... | collective-permute-start | bytes 442376 | tf_op jit(solution)/shard_map/ppermute | solution.py:471
  275.5 15.9 %copy-start.11 = (f32[8,384]{1,0:T(8,128)S(1)}, f32[8,384]{1,0:T(8,128)}, u32[]{:S(2)}) copy-start(f32[8,384]{1,0:T(8,128)} %copy-done.10) | copy-start | bytes 36868
  275.5 7.7 %collective-permute-start.18 = (bf16[48,768]{1,0:T(8,128)(2,1)S(1)}, bf16[48,768]{1,0:T(8,128)(2,1)S(1)}, u32[]{:S(2)}, u32[]{:S(2)}) collective-permute-start(bf16[48,768]{1,0:T(8,128)(2,1)S(1)} %get-tuple-element.137), channel_id=1, source_target_pairs={{0,16},{4,20},{8,24},{12,28},{16,0},{20,4},{24,8},{28,12},{1,17},{... | collective-permute-start | bytes 221192 | tf_op jit(solution)/shard_map/ppermute | solution.py:471
  275.6 7.6 %collective-permute-start.19 = (bf16[48,768]{1,0:T(8,128)(2,1)S(1)}, bf16[48,768]{1,0:T(8,128)(2,1)S(1)}, u32[]{:S(2)}, u32[]{:S(2)}) collective-permute-start(bf16[48,768]{1,0:T(8,128)(2,1)S(1)} %get-tuple-element.138), channel_id=1, source_target_pairs={{0,24},{4,28},{8,16},{12,20},{16,8},{20,12},{24,0},{28,4},{1,25},{... | collective-permute-start | bytes 221192 | tf_op jit(solution)/shard_map/ppermute | solution.py:471
  279.6 4.9 %collective-permute-start.15 = (bf16[48,768]{1,0:T(8,128)(2,1)S(1)}, bf16[48,768]{1,0:T(8,128)(2,1)S(1)}, u32[]{:S(2)}, u32[]{:S(2)}) collective-permute-start(bf16[48,768]{1,0:T(8,128)(2,1)S(1)} %slice.184), channel_id=1, source_target_pairs={{0,8},{4,12},{8,0},{12,4},{16,24},{20,28},{24,16},{28,20},{1,9},{5... | collective-permute-start | bytes 221192 | tf_op jit(solution)/shard_map/ppermute | solution.py:471
  287.7 41.6 %all-to-all-start.2 = ((f32[32,8,128]{2,1,0:T(8,128)}), f32[32,8,128]{2,1,0:T(8,128)}, u32[]{:S(2)}, u32[]{:S(2)}) async-start(f32[32,8,128]{2,1,0:T(8,128)} %broadcast_in_dim_broadcast_in_dim_broadcast_in_dim.3), calls=%async_computation.2 | async-start | bytes 262144 | tf_op jit(solution)/shard_map/all_to_all | solution.py:462
  291.4 2.0 copy-start.3
  293.4 2.0 copy-start.4
  295.4 0.9 copy-start.8
  296.3 0.7 copy-start.16
  296.9 0.7 copy-start.19
  329.3 10.1 %copy-start.26 = (f32[49,12]{0,1:T(8,128)S(1)}, f32[49,12]{0,1:T(8,128)}, u32[]{:S(2)}) copy-start(f32[49,12]{0,1:T(8,128)} %param.24) | copy-start | bytes 7060
  329.3 10.1 %copy-start.27 = (f32[49,12]{0,1:T(8,128)S(1)}, f32[49,12]{0,1:T(8,128)}, u32[]{:S(2)}) copy-start(f32[49,12]{0,1:T(8,128)} %param.25) | copy-start | bytes 7060
  329.3 10.1 %copy-start.28 = (f32[49,12]{0,1:T(8,128)S(1)}, f32[49,12]{0,1:T(8,128)}, u32[]{:S(2)}) copy-start(f32[49,12]{0,1:T(8,128)} %param.26) | copy-start | bytes 7060

commit v2 on v0

v2 whole, which is shorter than its diff:
```python
import functools

import jax
import jax.numpy as jnp
from jax import lax
from jax.experimental import pallas as pl
from jax.experimental.pallas import tpu as pltpu
from jax.sharding import PartitionSpec as P

STEP = 5

keep_scale = 4.0 / 3.0
norm_eps = 1e-06
clip_limit = 1.0
beta_one = 0.9
beta_two = 0.999
adam_eps = 1e-08
decay_rate = 0.05
step_rates = (0.15, 0.5, 0.05, 0.2, 0.025)
inv_root_two = 0.7071067811865476
inv_root_tau = 0.3989422804014327
f32 = jnp.float32
bf16 = jnp.bfloat16
AXES = ("dp", "space")
LANES = 128
REACH = 3
TAPS = 7
VEC = TAPS * TAPS
ROWS = 64
EDGE = 8
MLP_SLOTS = 4
VMEM_MIB = 60
DEPTH = 5
AHEAD = DEPTH - 2
MLP_COLS = 768
MIB = 1 << 20


def dot_nn(a, b):
    return lax.dot_general(a, b, (((1,), (0,)), ((), ())), preferred_element_type=f32)


def dot_nt(a, b):
    return lax.dot_general(a, b, (((1,), (1,)), ((), ())), preferred_element_type=f32)


def fold(value):
    rows, channels = value.shape
    return jnp.sum(value.reshape(rows // 8, 8, channels), axis=0)


def mlp_kernel(
    count_ref, unit_ref, stat_ref, cot_ref, bias_ref, par_ref, *refs
):
    step = pl.program_id(0)
    rows, channels = unit_ref.shape
    pieces = refs[:-14]
    (branch_ref, gc_ref, top_ref, low_ref, grad_near_ref, grad_far_ref, bsum_ref, vsum_ref,
     up_acc, down_acc, scaled_ref, both_ref, bias_acc, vec_acc) = refs[-14:]
    hidden_size = both_ref.shape[0]
    half = hidden_size // 2
    pixels = rows // MLP_SLOTS
    used = count_ref[0] * pixels
    gamma = par_ref[VEC + 4 : VEC + 5, :] * keep_scale

    @pl.when(step == 0)
    def _():
        up_acc[...] = jnp.zeros_like(up_acc)
        down_acc[...] = jnp.zeros_like(down_acc)
        bias_acc[...] = jnp.zeros_like(bias_acc)
        vec_acc[...] = jnp.zeros_like(vec_acc)
        at = 0
        for ref in pieces:
            size = ref.shape[0]
            both_ref[at : at + size, :] = ref[...]
            down = ref[:, channels : 2 * channels].astype(f32)
            scaled_ref[at : at + size, :] = (down * gamma).astype(bf16)
            at += size

    @pl.when(step * rows < used)
    def _():
        inside = lax.broadcasted_iota(jnp.int32, (rows, channels), 0) < used - step * rows
        unit = jnp.where(inside, unit_ref[...], 0.0)
        valid = stat_ref[:, LANES // 2 : LANES // 2 + 1]
        cotm32 = jnp.where(inside, cot_ref[...].astype(f32) * valid, 0.0)
        cotm = cotm32.astype(bf16)
        normed = (unit * par_ref[VEC + 1 : VEC + 2, :] + par_ref[VEC + 2 : VEC + 3, :]).astype(bf16)
        normed_t = normed.T
        cotm_t = cotm.T
        branch = None
        grad_normed = None
        for start in range(0, hidden_size, MLP_COLS):
            cols = slice(start, start + MLP_COLS)
            up = both_ref[cols, 0:channels]
            down = both_ref[cols, channels : 2 * channels]
            hidden = dot_nt(normed, up) + bias_ref[0:1, cols]
            cdf = 0.5 + 0.5 * lax.erf(hidden * inv_root_two)
            active = (hidden * cdf).astype(bf16)
            slope = cdf + hidden * (inv_root_tau * jnp.exp(-0.5 * hidden * hidden))
            part_branch = dot_nn(active, down)
            branch = part_branch if branch is None else branch + part_branch
            grad_hidden32 = dot_nt(cotm, scaled_ref[cols, :]) * slope
            bias_acc[:, cols] += fold(grad_hidden32)
            grad_hidden = grad_hidden32.astype(bf16)
            part_grad = dot_nn(grad_hidden, up)
            grad_normed = part_grad if grad_normed is None else grad_normed + part_grad
            up_acc[:, cols] += dot_nn(normed_t, grad_hidden)
            down_acc[:, cols] += dot_nn(cotm_t, active)
        branch = branch + par_ref[VEC + 3 : VEC + 4, :]
        branch_ref[...] = branch.astype(bf16).reshape(branch_ref.shape)
        inv_std = stat_ref[:, 0:1]
        scaled = grad_normed * par_ref[VEC + 1 : VEC + 2, :]
        mean_a = jnp.mean(scaled, axis=-1, keepdims=True)
        mean_b = jnp.mean(scaled * unit, axis=-1, keepdims=True)
        grad_conv = inv_std * (scaled - mean_a - unit * mean_b)
        grad_conv = jnp.where(inside, grad_conv, 0.0)
        maps = grad_conv.reshape(gc_ref.shape).astype(bf16)
        gc_ref[...] = maps
        top_ref[...] = maps[:, :REACH]
        low_ref[...] = maps[:, -REACH:]
        vec_acc[0:8, :] += fold(grad_conv)
        vec_acc[8:16, :] += fold(grad_normed * unit)
        vec_acc[16:24, :] += fold(grad_normed)
        vec_acc[24:32, :] += fold(cotm32)
        vec_acc[32:40, :] += fold(cotm32 * branch)

    @pl.when(step == pl.num_programs(0) - 1)
    def _():
        for start in range(0, hidden_size, MLP_COLS):
            cols = slice(start, start + MLP_COLS)
            ref = grad_near_ref if start < half else grad_far_ref
            part = slice(start % half, start % half + MLP_COLS)
            ref[part, 0:channels] = up_acc[:, cols].T.astype(bf16)
            ref[part, channels : 2 * channels] = (down_acc[:, cols].T * gamma).astype(bf16)
        bsum_ref[...] = jnp.sum(bias_acc[...], axis=0, keepdims=True)
        vsum_ref[...] = jnp.zeros_like(vsum_ref)
        for row in range(5):
            total = jnp.sum(vec_acc[8 * row : 8 * row + 8, :], axis=0, keepdims=True)
            if row == 3:
                total = total * gamma
            if row == 4:
                total = total * keep_scale
            vsum_ref[row : row + 1, :] = total


def walk(low, high, fetch, compute, store, load, prepare):
    def begin(i, carry):
        for copy in fetch(i, lax.rem(i - low, DEPTH)):
            copy.start()
        return carry

    def end(i, carry):
        for copy in store(i, lax.rem(i - low, DEPTH)):
            copy.wait()
        return carry

    if load is not None:
        load.start()
    lax.fori_loop(low, jnp.minimum(high, low + AHEAD), begin, 0)
    prepare()
    if load is not None:
        load.wait()

    def step(i, carry):
        buf = lax.rem(i - low, DEPTH)
        for copy in fetch(i, buf):
            copy.wait()

        @pl.when(i - low >= 2)
        def _():
            end(i - 2, 0)

        @pl.when(i + AHEAD < high)
        def _():
            begin(i + AHEAD, 0)

        compute(i, buf)
        for copy in store(i, buf):
            copy.start()
        return carry

    lax.fori_loop(low, high, step, 0)
    lax.fori_loop(jnp.maximum(low, high - 2), high, end, 0)


def copies(pairs, sems, buf):
    return [pltpu.make_async_copy(src, dst, sems.at[buf, at]) for at, (src, dst) in enumerate(pairs)]


def clear_edges(pad_ref, cols):
    tiles, rows, width, lanes = pad_ref.shape
    for tile in range(tiles):
        for row in range(rows):
            pad_ref[tile, row, 0:EDGE, :] = jnp.zeros((EDGE, lanes), f32)
            pad_ref[tile, row, EDGE + cols : width, :] = jnp.zeros((width - EDGE - cols, lanes), f32)


def inside_cols(cols, row, side):
    reach = jnp.where(row < side, side, 0)
    return lax.broadcasted_iota(jnp.int32, (cols, LANES), 0) < reach


def fill_rows(pad_ref, win_ref, side=None, first_row=None):
    rows, cols, channels = win_ref.shape
    for row in range(rows):
        inside = None if side is None else inside_cols(cols, first_row + row, side)
        for tile in range(channels // LANES):
            line = win_ref[row, :, tile * LANES : (tile + 1) * LANES].astype(f32)
            if side is not None:
                line = jnp.where(inside, line, 0.0)
            pad_ref[tile, row, EDGE : EDGE + cols, :] = line


def conv_tile(pad_ref, tile, par_ref, out_rows, cols, flip):
    lanes = slice(tile * LANES, (tile + 1) * LANES)
    sums = [None] * out_rows
    for col_off in range(TAPS):
        weights = []
        for row_off in range(TAPS):
            index = row_off * TAPS + col_off
            if flip:
                index = TAPS * TAPS - 1 - index
            weights.append(par_ref[index : index + 1, lanes])
        for row in range(out_rows + 2 * REACH):
            start = EDGE - REACH + col_off
            line = pad_ref[tile, row, start : start + cols, :]
            for row_off in range(TAPS):
                out = row - row_off
                if 0 <= out < out_rows:
                    term = weights[row_off] * line
                    sums[out] = term if sums[out] is None else sums[out] + term
    return sums


def conv_norm_kernel(
    which, first, order_ref, range_ref, side_ref, above_ref, own_ref, below_ref, cot_ref, pars_ref, *rest
):
    (unit_ref, stat_ref, cots_ref, win_ref, unit_buf, stat_buf, cot_buf, pad_ref, conv_ref, par_ref,
     in_sems, out_sems, par_sem) = rest[-13:]
    rows, cols, channels = own_ref.shape[1:]
    low, high, start = range_ref[which, 0], range_ref[which, 1], range_ref[which, 2]

    def fetch(i, buf):
        image = order_ref[i]
        win = win_ref.at[buf]
        return copies(
            [
                (above_ref.at[image - first], win.at[0:REACH]),
                (own_ref.at[image], win.at[REACH : REACH + rows]),
                (below_ref.at[image - first], win.at[REACH + rows : 2 * REACH + rows]),
                (cot_ref.at[image], cot_buf.at[buf]),
            ],
            in_sems,
            buf,
        )

    def store(i, buf):
        pairs = [(unit_buf, unit_ref), (stat_buf, stat_ref), (cot_buf, cots_ref)]
        return copies([(mine.at[buf], ref.at[i]) for mine, ref in pairs], out_sems, buf)

    def compute(i, buf):
        side = side_ref[order_ref[i]]
        fill_rows(pad_ref, win_ref.at[buf], side, start - REACH)
        for tile in range(channels // LANES):
            lanes = slice(tile * LANES, (tile + 1) * LANES)
            sums = conv_tile(pad_ref, tile, par_ref, rows, cols, False)
            for row in range(rows):
                conv_ref[row * cols : (row + 1) * cols, lanes] = sums[row] + par_ref[VEC : VEC + 1, lanes]

        @pl.when(i < high)
        def _():
            conv = conv_ref[...]
            mean = jnp.mean(conv, axis=-1, keepdims=True)
            centred = conv - mean
            var = jnp.mean(centred * centred, axis=-1, keepdims=True)
            inv_std = lax.rsqrt(var + norm_eps)
            unit_buf[buf] = centred * inv_std
            left = lax.broadcasted_iota(jnp.int32, (cols, LANES), 1) < LANES // 2
            for row in range(rows):
                inside = inside_cols(cols, start + row, side)
                spread_inv = jnp.broadcast_to(inv_std[row * cols : (row + 1) * cols], (cols, LANES))
                lines = slice(row * cols, (row + 1) * cols)
                stat_buf[buf, lines, :] = jnp.where(left, spread_inv, jnp.where(inside, 1.0, 0.0))

    load = pltpu.make_async_copy(pars_ref, par_ref, par_sem)
    walk(low, high, fetch, compute, store, load, lambda: clear_edges(pad_ref, cols))


def fill_pairs(pair_ref, win_ref, side=None, first_row=None):
    tiles, pairs = pair_ref.shape[:2]
    rows, cols, channels = win_ref.shape
    apart = rows - pairs
    for row in range(rows):
        if side is not None:
            mask = jnp.where(inside_cols(cols, first_row + row, side), 1.0, 0.0).astype(bf16)
        for tile in range(tiles):
            line = win_ref[row, :, tile * LANES : (tile + 1) * LANES]
            if side is not None:
                line = line * mask
            if row < pairs:
                pair_ref[tile, row, 0:cols, :] = line
            if row >= apart:
                pair_ref[tile, row - apart, cols : 2 * cols, :] = line


def taps_grad_kernel(
    which, split, order_ref, range_ref, side_ref, above_ref, own_ref, below_ref, far_above_ref, far_below_ref, gc_ref,
    out_ref, win_ref, gc_buf, pair_ref, acc_ref, grad_ref, in_sems,
):
    rows, cols, channels = own_ref.shape[1:]
    half = rows // 2
    low, high, start = range_ref[which, 0], range_ref[which, 1], range_ref[which, 2]

    def halo_copies(above, below, image, buf):
        win = win_ref.at[buf]
        return [
            pltpu.make_async_copy(above.at[image], win.at[0:REACH], in_sems.at[buf, 2]),
            pltpu.make_async_copy(below.at[image], win.at[REACH + rows : 2 * REACH + rows], in_sems.at[buf, 3]),
        ]

    class Halo:
        def __init__(self, image, buf):
            self.image, self.buf = image, buf

        def start(self):
            @pl.when(self.image < split)
            def _():
                for copy in halo_copies(above_ref, below_ref, self.image, self.buf):
                    copy.start()

            @pl.when(self.image >= split)
            def _():
                for copy in halo_copies(far_above_ref, far_below_ref, self.image - split, self.buf):
                    copy.start()

        def wait(self):
            for copy in halo_copies(above_ref, below_ref, 0, self.buf):
                copy.wait()

    def fetch(i, buf):
        image = order_ref[i]
        win = win_ref.at[buf]
        near = copies([(own_ref.at[image], win.at[REACH : REACH + rows]), (gc_ref.at[i], gc_buf.at[buf])], in_sems, buf)
        return near + [Halo(image, buf)]

    def compute(i, buf):
        fill_pairs(pair_ref, win_ref.at[buf], side_ref[order_ref[i]], start - REACH)
        for row in range(rows):
            for tile in range(channels // LANES):
                line = gc_buf[buf, row, :, tile * LANES : (tile + 1) * LANES]
                grad_ref[tile, row, EDGE : EDGE + cols, :] = line.astype(f32)
        for tile in range(channels // LANES):
            lanes = slice(tile * LANES, (tile + 1) * LANES)
            for col_off in range(TAPS):
                at = EDGE + REACH - col_off
                grads = []
                for row in range(half):
                    two = [grad_ref[tile, row, at : at + cols, :], grad_ref[tile, row + half, at : at + cols, :]]
                    grads.append(jnp.concatenate(two, axis=0).astype(bf16))
                for row_off in range(TAPS):
                    total = grads[0] * pair_ref[tile, row_off]
                    for row in range(1, half):
                        total = total + grads[row] * pair_ref[tile, row_off + row]
                    total = total[0:16] + total[16:32] + total[32:48]
                    acc_ref[row_off * TAPS + col_off, :, lanes] += fold(total.astype(f32))

    def prepare():
        acc_ref[...] = jnp.zeros_like(acc_ref)
        clear_edges(grad_ref, cols)

    walk(low, high, fetch, compute, lambda i, buf: [], None, prepare)
    out_ref[...] = jnp.sum(acc_ref[...], axis=1)


def finish_kernel(
    which, order_ref, range_ref, side_ref, above_ref, gc_ref, below_ref, branch_ref, image_ref, cot_ref, pars_ref, *rest
):
    (out_ref, gim_ref, win_ref, branch_buf, image_buf, cot_buf, out_buf, gim_buf, pair_ref, part_ref, sum_ref, par_ref,
     in_sems, out_sems, par_sem) = rest[-15:]
    rows, cols, channels = image_ref.shape[1:]
    half = rows // 2
    low, high, start = range_ref[which, 0], range_ref[which, 1], range_ref[which, 2]
    plain_low, plain_high = range_ref[which, 3], range_ref[which, 4]

    def fetch(i, buf):
        image = order_ref[i]
        win = win_ref.at[buf]
        return copies(
            [
                (above_ref.at[i], win.at[0:REACH]),
                (gc_ref.at[i], win.at[REACH : REACH + rows]),
                (below_ref.at[i], win.at[REACH + rows : 2 * REACH + rows]),
                (branch_ref.at[i], branch_buf.at[buf]),
                (image_ref.at[image], image_buf.at[buf]),
                (cot_ref.at[image], cot_buf.at[buf]),
            ],
            in_sems,
            buf,
        )

    def store(i, buf):
        image = order_ref[i]
        return copies([(out_buf.at[buf], out_ref.at[image]), (gim_buf.at[buf], gim_ref.at[image])], out_sems, buf)

    def pass_in(i, buf):
        image = order_ref[i]
        return copies([(image_ref.at[image], image_buf.at[buf]), (cot_ref.at[image], cot_buf.at[buf])], in_sems, buf)

    def pass_out(i, buf):
        image = order_ref[i]
        return copies([(image_buf.at[buf], out_ref.at[image]), (cot_buf.at[buf], gim_ref.at[image])], out_sems, buf)

    def compute(i, buf):
        side = side_ref[order_ref[i]]
        fill_pairs(pair_ref, win_ref.at[buf])
        for tile in range(channels // LANES):
            lanes = slice(tile * LANES, (tile + 1) * LANES)
            for col_off in range(TAPS):
                at = EDGE
                weights = []
                for row_off in range(TAPS):
                    index = TAPS * TAPS - 1 - row_off * TAPS - col_off
                    weights.append(par_ref[index : index + 1, lanes].astype(bf16))
                for row in range(half):
                    total = weights[0] * pair_ref[tile, row]
                    for row_off in range(1, TAPS):
                        total = total + weights[row_off] * pair_ref[tile, row + row_off]
                    total = total.astype(f32)
                    part_ref[col_off, row, at : at + cols, :] = total[0:cols]
                    part_ref[col_off, row + half, at : at + cols, :] = total[cols : 2 * cols]
            for row in range(rows):
                total = part_ref[REACH, row, EDGE : EDGE + cols, :]
                for col_off in range(TAPS):
                    if col_off != REACH:
                        at = EDGE - REACH + col_off
                        total = total + part_ref[col_off, row, at : at + cols, :]
                sum_ref[row, :, lanes] = total

        @pl.when(i < high)
        def _():
            scale = par_ref[VEC + 4 : VEC + 5, :] * keep_scale
            for row in range(rows):
                inside = inside_cols(cols, start + row, side)
                for tile in range(channels // LANES):
                    lanes = slice(tile * LANES, (tile + 1) * LANES)
                    grad = cot_buf[buf, row, :, lanes].astype(f32) + jnp.where(inside, sum_ref[row, :, lanes], 0.0)
                    gim_buf[buf, row, :, lanes] = grad.astype(bf16)
                    extra = branch_buf[buf, row, :, lanes].astype(f32) * scale[:, lanes]
                    out = image_buf[buf, row, :, lanes].astype(f32) + jnp.where(inside, extra, 0.0)
                    out_buf[buf, row, :, lanes] = out.astype(bf16)

    load = pltpu.make_async_copy(pars_ref, par_ref, par_sem)
    walk(low, high, fetch, compute, store, load, lambda: clear_edges(part_ref, cols))
    walk(plain_low, plain_high, pass_in, lambda i, buf: None, pass_out, None, lambda: None)


def lane_mask(low, high):
    lanes = lax.broadcasted_iota(jnp.int32, (8, LANES), 1)
    return (lanes >= low) & (lanes < high)


def pack_kernel(
    spans, codes, space_size, rows, keep_ref, kernel_ref, vectors_ref, bias_ref, up_ref, down_ref,
    small_ref, piece_ref, order_ref, range_ref, owner_ref, used_ref, rows_ref, seen_ref,
):
    part, channels = up_ref.shape
    width = kernel_ref.shape[0]
    count = keep_ref.shape[0]
    rows_ref[...] = jnp.zeros_like(rows_ref)
    rows_ref[0:width, 0:VEC] = kernel_ref[...]
    rows_ref[...] = rows_ref[...].T
    rows_ref[VEC : VEC + 5, 0:width] = vectors_ref[...]
    for at in range(part // width):
        rows_ref[VEC + 5 + at : VEC + 6 + at, 0:width] = bias_ref[0:1, at * width : (at + 1) * width]
    small = rows_ref[0:8, :]
    for group in range(1, ROWS // 8):
        small = small + pltpu.roll(rows_ref[8 * group : 8 * group + 8, :], group * width, 1)
    for device in range(small_ref.shape[0]):
        small_ref[device] = small
    piece_ref[:, 0:channels] = up_ref[...].astype(bf16)
    piece_ref[:, channels : 2 * channels] = down_ref[...].astype(bf16)

    def place(i, at):
        keep = keep_ref[i] > 0
        upper, lower = at
        seen_ref[i] = upper
        order_ref[jnp.where(keep, upper, lower)] = i
        return jnp.where(keep, upper + 1, upper), jnp.where(keep, lower, lower + 1)

    kept = lax.fori_loop(0, count, lambda i, at: at + jnp.where(keep_ref[i] > 0, 1, 0), 0)
    lax.fori_loop(0, count, place, (0, kept))
    seen_ref[count] = kept
    me_space = lax.axis_index("space")
    me = lax.axis_index("dp") * space_size + me_space
    for which, (low, high, plain) in enumerate(spans):
        range_ref[which, 0] = seen_ref[low]
        range_ref[which, 1] = seen_ref[high]
        range_ref[which, 2] = me_space * rows
        range_ref[which, 3] = jnp.maximum(kept, plain)
        range_ref[which, 4] = jnp.maximum(kept, count)
    for at, code in enumerate(codes):
        owner_ref[at] = code if space_size != 4 or len(codes) != 32 else me ^ code
    used_ref[0] = kept


def join_kernel(*refs):
    outs, pieces = refs[-2:], refs[:-2]
    each = len(pieces) // 2
    for out, group in zip(outs, (pieces[:each], pieces[each:])):
        size = group[0].shape[0]
        for at, ref in enumerate(group):
            out[at * size : (at + 1) * size, :] = ref[...]


def unpack_kernel(order_ref, small_ref, par_ref, bias_ref):
    devices = small_ref.shape[0]
    channels = par_ref.shape[1]
    width = channels // devices
    part = bias_ref.shape[1] // devices
    for group in range(ROWS // 8):
        tiles = [jnp.zeros((8, LANES), f32) for _ in range(channels // LANES)]
        for device in range(devices):
            start = device * width
            tile, low = start // LANES, start % LANES
            moved = pltpu.roll(small_ref[device], (start - group * width) % LANES, 1)
            tiles[tile] = jnp.where(lane_mask(low, low + width), moved, tiles[tile])
            if low + width > LANES:
                tiles[tile + 1] = jnp.where(lane_mask(0, low + width - LANES), moved, tiles[tile + 1])
        for tile, value in enumerate(tiles):
            par_ref[8 * group : 8 * group + 8, tile * LANES : (tile + 1) * LANES] = value
    bias_ref[...] = jnp.zeros_like(bias_ref)
    for place in range(devices):
        for at in range(part // width):
            row = VEC + 5 + at
            group, line = row // 8, row % 8
            start = place * part + at * width
            tile, low = start // LANES, start % LANES
            source = small_ref[order_ref[place], line : line + 1, :]
            moved = pltpu.roll(jnp.broadcast_to(source, (8, LANES)), (start - group * width) % LANES, 1)
            for where_, lower, upper in ((tile, low, low + width), (tile + 1, 0, low + width - LANES)):
                if upper > lower:
                    lanes = slice(where_ * LANES, (where_ + 1) * LANES)
                    kept = jnp.broadcast_to(bias_ref[0:1, lanes], (8, LANES))
                    bias_ref[0:1, lanes] = jnp.where(lane_mask(lower, upper), moved, kept)[0:1]


def pack_grads_kernel(order_ref, taps_ref, vec_ref, bias_ref, out_ref, rows_ref):
    devices = out_ref.shape[0]
    channels = taps_ref.shape[1]
    width = channels // devices
    part = bias_ref.shape[1] // devices
    rows_ref[...] = jnp.zeros_like(rows_ref)
    rows_ref[0:VEC, :] = taps_ref[...]
    rows_ref[VEC : VEC + 5, :] = vec_ref[0:5, :]

    def cut(row_slice, source, start, group):
        tile, low = start // LANES, start % LANES
        shift = (group * width - low) % LANES
        moved = pltpu.roll(source(row_slice, tile), shift, 1)
        if low + width > LANES:
            split = group * width + LANES - low
            moved = jnp.where(lane_mask(0, split), moved, pltpu.roll(source(row_slice, tile + 1), shift, 1))
        return moved

    def of_rows(rows, tile):
        return rows_ref[rows, tile * LANES : (tile + 1) * LANES]

    def of_bias(rows, tile):
        return jnp.broadcast_to(bias_ref[0:1, tile * LANES : (tile + 1) * LANES], (8, LANES))

    for device in range(devices):
        total = jnp.zeros((8, LANES), f32)
        for group in range(ROWS // 8):
            moved = cut(slice(8 * group, 8 * group + 8), of_rows, device * width, group)
            total = jnp.where(lane_mask(group * width, (group + 1) * width), moved, total)
        out_ref[device] = total
    for place in range(devices):
        device = order_ref[place]
        for at in range(part // width):
            row = VEC + 5 + at
            group, line = row // 8, row % 8
            moved = cut(None, of_bias, place * part + at * width, group)
            kept = jnp.broadcast_to(out_ref[device, line : line + 1, :], (8, LANES))
            mask = lane_mask(group * width, (group + 1) * width)
            out_ref[device, line : line + 1, :] = jnp.where(mask, moved, kept)[0:1]


def total_kernel(small_ref, *refs):
    count = (len(refs) - 5) // 2
    parts, (own_ref, sums_ref, norm_ref), bufs, (sems, small_buf) = refs[:count], refs[count : count + 3], refs[count + 3 : -2], refs[-2:]
    size = own_ref.shape[0]
    loads = [pltpu.make_async_copy(small_ref, small_buf, sems.at[count])]
    for at, (ref, buf) in enumerate(zip(parts, bufs)):
        loads.append(pltpu.make_async_copy(ref.at[0:size], buf, sems.at[at]))
    for load in loads:
        load.start()
    for load in loads:
        load.wait()
    own = bufs[0][...].astype(f32)
    for buf in bufs[1:]:
        own = own + buf[...].astype(f32)
    own_ref[...] = own
    sums = jnp.sum(small_buf[...], axis=0)
    sums_ref[...] = sums
    local = jnp.sum(own * own) + jnp.sum(sums * sums)
    norm_ref[...] = jnp.full_like(norm_ref, local)


def adam(weight, moment, square, grad, factor, rate):
    scaled = grad * factor
    new_moment = beta_one * moment + (1.0 - beta_one) * scaled
    new_square = beta_two * square + (1.0 - beta_two) * scaled * scaled
    corrected = new_moment / (1.0 - beta_one**STEP)
    spread = jnp.sqrt(new_square / (1.0 - beta_two**STEP))
    return weight - rate * (corrected / (spread + adam_eps) + decay_rate * weight), new_moment, new_square


def adam_kernel(own_ref, sums_ref, norms_ref, *refs):
    states, outs, norm_ref, rows_ref, flip_ref = refs[:15], refs[15:30], refs[30], refs[31], refs[32]
    part, channels = states[6].shape
    width = states[0].shape[0]
    total = jnp.sum(norms_ref[:, 0, 0:1])
    norm = jnp.sqrt(jnp.full((8, LANES), total, f32))
    norm_ref[...] = norm[0:1, 0:1]
    factor = (clip_limit / jnp.maximum(norm, clip_limit))[0:1, 0:1]
    sums = sums_ref[...]
    rows_ref[...] = jnp.zeros_like(rows_ref)
    for group in range(ROWS // 8):
        rows_ref[8 * group : 8 * group + 8, :] = pltpu.roll(sums, (-group * width) % LANES, 1)
    flip_ref[...] = rows_ref[...].T
    grads = [
        flip_ref[0:width, 0:VEC],
        rows_ref[VEC : VEC + 5, 0:width],
        own_ref[:, 0:channels],
        None,
        own_ref[:, channels : 2 * channels],
    ]
    for index, (grad, rate) in enumerate(zip(grads, step_rates)):
        if grad is None:
            continue
        results = adam(*(ref[...] for ref in states[3 * index : 3 * index + 3]), grad, factor, rate)
        for ref, value in zip(outs[3 * index : 3 * index + 3], results):
            ref[...] = value
    for at in range(part // width):
        lanes = slice(at * width, (at + 1) * width)
        row = VEC + 5 + at
        grad = rows_ref[row : row + 1, 0:width]
        results = adam(*(ref[0:1, lanes] for ref in states[9:12]), grad, factor, step_rates[3])
        for ref, value in zip(outs[9:12], results):
            ref[0:1, lanes] = value


def mlp(kept, unit, stat, cots, pieces, bias, pars, dims):
    count, rows, cols, channels = dims
    pixels = rows * cols
    total = count * pixels
    hidden_size = bias.shape[1]
    tall = MLP_SLOTS * pixels

    def last(i, n):
        return jnp.minimum(i, jnp.maximum((n[0] + MLP_SLOTS - 1) // MLP_SLOTS - 1, 0))

    tile_map = lambda i, n: (last(i, n), 0)
    slot_map = lambda i, n: (last(i, n), 0, 0, 0)
    whole = lambda i, n: (0, 0)
    grad = (hidden_size // 2, 2 * channels)
    halo = (count, REACH, cols, channels)
    once = pl.Buffered(1)
    return pl.pallas_call(
        mlp_kernel,
        grid_spec=pltpu.PrefetchScalarGridSpec(
            num_scalar_prefetch=1,
            grid=(-(-count // MLP_SLOTS),),
            in_specs=[
                pl.BlockSpec((tall, channels), tile_map),
                pl.BlockSpec((tall, LANES), tile_map),
                pl.BlockSpec((tall, channels), tile_map),
                pl.BlockSpec(bias.shape, whole),
                pl.BlockSpec(pars.shape, whole),
            ]
            + [pl.BlockSpec(value.shape, whole, pipeline_mode=once) for value in pieces],
            out_specs=[
                pl.BlockSpec((MLP_SLOTS, rows, cols, channels), slot_map),
                pl.BlockSpec((MLP_SLOTS, rows, cols, channels), slot_map),
                pl.BlockSpec((MLP_SLOTS, REACH, cols, channels), slot_map),
                pl.BlockSpec((MLP_SLOTS, REACH, cols, channels), slot_map),
                pl.BlockSpec(grad, whole),
                pl.BlockSpec(grad, whole),
                pl.BlockSpec((1, hidden_size), whole),
                pl.BlockSpec((8, channels), whole),
            ],
            scratch_shapes=[
                pltpu.VMEM((channels, hidden_size), f32),
                pltpu.VMEM((channels, hidden_size), f32),
                pltpu.VMEM((hidden_size, channels), bf16),
                pltpu.VMEM((hidden_size, 2 * channels), bf16),
                pltpu.VMEM((8, hidden_size), f32),
                pltpu.VMEM((40, channels), f32),
            ],
        ),
        out_shape=[
            shape(dims, bf16),
            shape(dims, bf16),
            shape(halo, bf16),
            shape(halo, bf16),
            shape(grad, bf16),
            shape(grad, bf16),
            shape((1, hidden_size), f32),
            shape((8, channels), f32),
        ],
        compiler_params=pltpu.CompilerParams(dimension_semantics=("arbitrary",), vmem_limit_bytes=VMEM_MIB * MIB),
        name="mlp",
    )(kept, unit.reshape(total, channels), stat.reshape(total, LANES), cots.reshape(total, channels), bias, pars, *pieces)


IN_PLACE = pl.BlockSpec(memory_space=pltpu.HBM)
SCALARS = pl.BlockSpec(memory_space=pltpu.SMEM)
LOADED = pl.BlockSpec(memory_space=pltpu.VMEM)


def call(kernel, in_specs, out_specs, out_shape, scratch, name, aliases=None):
    return pl.pallas_call(
        kernel,
        in_specs=in_specs,
        out_specs=out_specs,
        out_shape=out_shape,
        scratch_shapes=scratch,
        input_output_aliases=aliases or {},
        compiler_params=pltpu.CompilerParams(vmem_limit_bytes=VMEM_MIB * MIB),
        name=name,
    )


def shape(dims, kind):
    return jax.ShapeDtypeStruct(dims, kind)


def window(rows, cols, channels):
    return pltpu.VMEM((DEPTH, rows + 2 * REACH, cols, channels), bf16)


def padded(rows, cols, channels):
    return pltpu.VMEM((channels // LANES, rows + 2 * REACH, cols + 2 * EDGE, LANES), f32)


def paired(rows, cols, channels):
    return pltpu.VMEM((channels // LANES, rows // 2 + 2 * REACH, 2 * cols, LANES), bf16)


def conv_norm(which, first, order, ranges, sides, above, own, below, cot, pars, earlier):
    count, rows, cols, channels = own.shape
    pixels = rows * cols
    outs = [
        shape((count, pixels, channels), f32),
        shape((count, pixels, LANES), f32),
        shape((count, rows, cols, channels), bf16),
    ]
    run = call(
        functools.partial(conv_norm_kernel, which, first),
        [SCALARS] * 3 + [IN_PLACE] * (5 + len(earlier)),
        [IN_PLACE] * 3,
        outs,
        [
            window(rows, cols, channels),
            pltpu.VMEM((DEPTH, pixels, channels), f32),
            pltpu.VMEM((DEPTH, pixels, LANES), f32),
            pltpu.VMEM((DEPTH, rows, cols, channels), bf16),
            padded(rows, cols, channels),
            pltpu.VMEM((pixels, channels), f32),
            pltpu.VMEM(pars.shape, f32),
            pltpu.SemaphoreType.DMA((DEPTH, 4)),
            pltpu.SemaphoreType.DMA((DEPTH, 3)),
            pltpu.SemaphoreType.DMA,
        ],
        "conv_norm",
        {8 + at: at for at in range(len(earlier))},
    )
    return run(order, ranges, sides, above, own, below, cot, pars, *earlier)


def taps_grad(which, order, ranges, sides, halos, own, gc):
    count, rows, cols, channels = own.shape
    pixels = rows * cols
    run = call(
        functools.partial(taps_grad_kernel, which, halos[0].shape[0]),
        [SCALARS] * 3 + [IN_PLACE] * 6,
        LOADED,
        shape((TAPS * TAPS, channels), f32),
        [
            window(rows, cols, channels),
            pltpu.VMEM((DEPTH, rows, cols, channels), bf16),
            paired(rows, cols, channels),
            pltpu.VMEM((TAPS * TAPS, 8, channels), f32),
            pltpu.VMEM((channels // LANES, rows, cols + 2 * EDGE, LANES), f32),
            pltpu.SemaphoreType.DMA((DEPTH, 4)),
        ],
        "taps_grad",
    )
    return run(order, ranges, sides, halos[0], own, halos[1], halos[2], halos[3], gc.reshape(own.shape))


def finish(which, order, ranges, sides, above, gc, below, branch, images, cot, pars, earlier):
    count, rows, cols, channels = images.shape
    block = (DEPTH, rows, cols, channels)
    run = call(
        functools.partial(finish_kernel, which),
        [SCALARS] * 3 + [IN_PLACE] * (7 + len(earlier)),
        [IN_PLACE] * 2,
        [shape(images.shape, bf16)] * 2,
        [
            window(rows, cols, channels),
            pltpu.VMEM(block, bf16),
            pltpu.VMEM(block, bf16),
            pltpu.VMEM(block, bf16),
            pltpu.VMEM(block, bf16),
            pltpu.VMEM(block, bf16),
            paired(rows, cols, channels),
            pltpu.VMEM((TAPS, rows, cols + 2 * EDGE, LANES), f32),
            pltpu.VMEM((rows, cols, channels), f32),
            pltpu.VMEM(pars.shape, f32),
            pltpu.SemaphoreType.DMA((DEPTH, 6)),
            pltpu.SemaphoreType.DMA((DEPTH, 2)),
            pltpu.SemaphoreType.DMA,
        ],
        "finish",
        {10 + at: at for at in range(len(earlier))},
    )
    maps = (value.reshape(images.shape) for value in (gc, branch))
    gc, branch = maps
    return run(order, ranges, sides, above, gc, below, branch, images, cot, pars, *earlier)


def pack(spans, codes, space_size, rows, keep, kernel, vectors, bias, up, down):
    channels, part = up.shape
    return call(
        functools.partial(pack_kernel, spans, codes, space_size, rows),
        [SCALARS] + [LOADED] * 5,
        [LOADED] * 2 + [SCALARS] * 4,
        [
            shape((len(codes), 8, LANES), f32),
            shape((part, 2 * channels), bf16),
            shape(keep.shape, jnp.int32),
            shape((len(spans), 5), jnp.int32),
            shape((len(codes),), jnp.int32),
            shape((1,), jnp.int32),
        ],
        [pltpu.VMEM((LANES, LANES), f32), pltpu.SMEM((keep.shape[0] + 1,), jnp.int32)],
        "pack",
    )(keep, kernel.T, vectors, bias.reshape(1, -1), up.T, down)


def join_two(*pieces):
    size, width = pieces[0].shape
    each = len(pieces) // 2
    out = shape((each * size, width), pieces[0].dtype)
    return call(join_kernel, [LOADED] * len(pieces), [LOADED] * 2, [out, out], [], "join")(*pieces)


def unpack(order, small, channels, hidden_size):
    return call(
        unpack_kernel,
        [SCALARS, LOADED],
        [LOADED] * 2,
        [shape((ROWS, channels), f32), shape((1, hidden_size), f32)],
        [],
        "unpack",
    )(order, small)


def pack_grads(order, taps, vec, bias):
    return call(
        pack_grads_kernel,
        [SCALARS] + [LOADED] * 3,
        LOADED,
        shape((order.shape[0], 8, LANES), f32),
        [pltpu.VMEM((ROWS, taps.shape[1]), f32)],
        "pack_grads",
    )(order, taps, vec, bias)


def add_up(small, parts, size):
    devices = small.shape[0]
    width = parts[0].shape[1]
    return call(
        total_kernel,
        [IN_PLACE] * (1 + len(parts)),
        [LOADED] * 3,
        [shape((size, width), f32), shape((8, LANES), f32), shape((devices, 8, LANES), f32)],
        [pltpu.VMEM((size, width), value.dtype) for value in parts]
        + [pltpu.SemaphoreType.DMA((len(parts) + 1,)), pltpu.VMEM(small.shape, f32)],
        "add_up",
    )(small, *parts)


def update(own, sums, norms, states):
    def view(at, value):
        if at // 3 in (0, 2):
            return value.T
        return value.reshape(1, -1) if at // 3 == 3 else value

    def unview(at, value):
        return value.reshape(-1) if at // 3 == 3 else view(at, value)

    views = [view(at, value) for at, value in enumerate(states)]
    results = call(
        adam_kernel,
        [LOADED] * 18,
        [LOADED] * 16,
        [shape(value.shape, f32) for value in views] + [shape((1, 1), f32)],
        [pltpu.VMEM((LANES, LANES), f32), pltpu.VMEM((LANES, LANES), f32)],
        "update",
    )(own, sums, norms, *views)
    return [unview(at, value) for at, value in enumerate(results[:15])], results[15].reshape(())


def pass_rows(top, low, places):
    above = lax.ppermute(low, "space", [(i, i + 1) for i in range(places - 1)])
    below = lax.ppermute(top, "space", [(i + 1, i) for i in range(places - 1)])
    return above, below


def flip_perm(size, bit):
    return [(i, i ^ bit) for i in range(size)]


def swap(value, bits):
    axis, bit, size = ("dp", bits[0], 8) if bits[0] else ("space", bits[1], 4)
    return lax.ppermute(value, axis, flip_perm(size, bit))


X, Y, CORE = (1, 0), (0, 2), (0, 1)
Z1, Z2, Z3 = (2, 0), (4, 0), (6, 0)


def cube_order():
    first = [0, 2 * 4]
    last = [4 * 4, 6 * 4]
    first = first + [v ^ 4 for v in first]
    last = last + [v ^ 2 for v in last]
    first = first + [v ^ 2 for v in first]
    last = last + [v ^ 4 for v in last]
    near = first + last
    return near + [v ^ 1 for v in near]


def after(value, *others):
    return lax.optimization_barrier((value,) + others)[0]


def behind(values, token):
    return lax.optimization_barrier((*values, token))[:-1]


def total_of(*pieces):
    total = pieces[0].astype(f32)
    for piece in pieces[1:]:
        total = total + piece.astype(f32)
    return total.astype(bf16)


def exchange(value):
    return lax.all_to_all(value, AXES, 0, 0, tiled=True)


def body(dp_size, space_size, images, cotangent, image_sides, keep_flags, *states):
    devices = dp_size * space_size
    count, rows, cols, channels = images.shape
    depth_kernel, block_vectors, up_weight, up_bias, down_weight = states[0::3]
    part = up_weight.shape[1]
    hidden_size = part * devices
    cube = dp_size == 8 and space_size == 4

    cut, mid = 3 * count // 8, 11 * count // 16
    spans = ((0, cut, count), (cut, mid, count), (mid, count, count), (mid, count, 0), (0, count, count), (0, count, 0))
    codes = tuple(cube_order()) if cube else tuple(range(devices))
    small, piece, order, ranges, owners, kept = pack(
        spans, codes, space_size, rows, keep_flags, depth_kernel, block_vectors, up_bias, up_weight, down_weight
    )
    small_all = exchange(small)
    piece, maps = after((piece, images), small) if cube else (piece, images)
    halos = pass_rows(maps[:cut, :REACH], maps[:cut, -REACH:], space_size)
    pars, bias = unpack(owners, small_all, channels, hidden_size)

    def conv_part(which, earlier, *waits):
        above, below = halos[:2] if which == 0 else halos[2:]
        first = 0 if which == 0 else cut
        return conv_norm(
            which, first, after(order, *waits), ranges, image_sides, above, images, below, cotangent, pars, earlier
        )

    later = images
    if cube:
        first, last = join_two(*behind((piece, *(swap(piece, step) for step in (Z1, Z2, Z3))), small_all))
        later = after(images, first, last, *halos)
        got = (swap(first, X), swap(last, Y))
    halos += pass_rows(later[cut:, :REACH], later[cut:, -REACH:], space_size)
    if cube:
        made = conv_part(0, (), first, last)
        got = behind(got, made[1])
        first, last = join_two(first, got[0], last, got[1])
        got = (swap(first, Y), swap(last, X))
        made = conv_part(1, made, first, last)
        got = behind(got, made[1])
        pieces = [first, got[0], last, got[1]]
        far = [swap(value, CORE) for value in pieces]
        unit, stat, cots = conv_part(2, made, *pieces)
        pieces = pieces + list(behind(far, stat))
    else:
        pieces = [lax.all_gather(piece, AXES, axis=0, tiled=True)]
        made = conv_part(0, ())
        made = conv_part(1, made)
        unit, stat, cots = conv_part(2, made)
    branch, gc, top, low, grad_near, grad_far, bias_sum, vec_sum = mlp(
        kept, unit, stat, cots, pieces, bias, pars, images.shape
    )

    def taps_part(which, *waits):
        return taps_grad(which, after(order, *waits), ranges, image_sides, halos, images, gc)

    def finish_part(which, earlier, *waits):
        return finish(
            which, after(order, *waits), ranges, image_sides,
            gc_above, gc, gc_below, branch, images, cotangent, pars, earlier,
        )

    if cube:
        core = swap(grad_far, CORE)
        half = grad_near.shape[0] // 2
        quarter, eighth = half // 2, half // 4

        def kept_sum(which, low, high, *got):
            lines = slice(which * half + low, which * half + high)
            return total_of(grad_near[lines], core[lines], *(value[low:high] for value in got))

        gc_above, gc_below = pass_rows(top, low, space_size)
        send = [kept_sum(0, quarter, half), kept_sum(1, quarter, half)]
        two_a, two_b = swap(send[0], Y), swap(send[1], X)
        taps = taps_part(4, *send)
        two_a, two_b = behind((two_a, two_b), taps)
        got = exchange(pack_grads(owners, taps, vec_sum, bias_sum))
        send = [kept_sum(0, eighth, quarter, two_a), kept_sum(1, eighth, quarter, two_b)]
        three_a, three_b = swap(send[0], X), swap(send[1], Y)
        made = finish_part(0, (), *send)
        three_a, three_b, got = behind((three_a, three_b, got), made[0])
        send = [
            kept_sum(0, part, 2 * part, two_a, three_a),
            kept_sum(1, 0, part, two_b, three_b),
            kept_sum(1, part, 2 * part, two_b, three_b),
        ]
        z_got = [swap(value, step) for value, step in zip(send, (Z1, Z2, Z3))]
        made = finish_part(1, made, *send)
        z_got = behind(z_got, made[0])
        own, sums, norm = add_up(got, [grad_near, core, two_a, three_a, *z_got], part)
        norms = exchange(norm)
        out_images, grad_images = finish_part(3, made, norm)
        norms, grad_images = lax.optimization_barrier((norms, grad_images))
    else:
        gc_above, gc_below = pass_rows(top, low, space_size)
        grads = jnp.concatenate([grad_near, grad_far]).astype(f32)
        parts = [lax.psum_scatter(grads, AXES, scatter_dimension=0, tiled=True)]
        got = exchange(pack_grads(owners, taps_part(4), vec_sum, bias_sum))
        own, sums, norm = add_up(got, parts, part)
        norms = exchange(norm)
        out_images, grad_images = finish_part(5, ())
    results, grad_norm = update(own, sums, norms, states)
    return (out_images, grad_images, *results, grad_norm)


def solution(mesh):
    lanes = P(None, AXES)
    flat = P(AXES)
    tall = P(AXES, None)
    maps = P("dp", "space", None, None)
    in_specs = (maps, maps, P("dp"), P("dp")) + (lanes,) * 9 + (flat,) * 3 + (tall,) * 3
    out_specs = (maps, maps) + (lanes,) * 9 + (flat,) * 3 + (tall,) * 3 + (P(),)
    run = functools.partial(body, mesh.shape["dp"], mesh.shape["space"])
    return jax.shard_map(run, mesh=mesh, in_specs=in_specs, out_specs=out_specs, check_vma=False)
```

time: 862 us -> 222 us (0.26); the launches traced: 850 us -> 220 us
  other arithmetic: 362 us -> 5.42 us
  blocking collectives: 220 us -> 0 us
  Pallas kernels: 0 us -> 129 us
  matrix products: 101 us -> 0 us
  local copies, waits for them, and re-layouts: 88.7 us -> 12.8 us
  starting transfers between devices: 17.8 us -> 62.6 us
  waiting for transfers between devices: 41.3 us -> 8.56 us
  between operations: 19.9 us -> 1.32 us
    convert_element_type x5 -> x3, other arithmetic: 190 us -> 5.42 us  [total_of(): return total.astype(bf16)]
    reduce_sum x12 -> x0, other arithmetic: 159 us -> none  [the longest x4 87.2 us: kernel_grad(): jnp.sum(wide[:, row_off:row_off + out_rows, col_off:col_off + out_cols, :...]
    pallas_call x0 -> x15, Pallas kernels: none -> 129 us  [the longest x1 43.7 us: mlp(): pl.pallas_call(mlp_kernel, grid_spec=pltpu.PrefetchScalarGridSpec(num_sca...]
    all_gather x2 -> x0, blocking collectives: 115 us -> none  [the longest x1 75.1 us: body(): lax.all_gather(block_vectors, ('dp', 'space'), axis=1, tiled=True)]
    dot_general x6 -> x0, matrix products: 101 us -> none  [the longest x1 21.6 us: body(): jnp.einsum('nijc,hc->nijh', grad_branch, down_full, preferred_element_typ...]
    psum x1 -> x0, blocking collectives: 68.2 us -> none  [body(): lax.psum((local_grads[0], local_grads[1], local_grads[2], local_grads[3],...]
    another operation x57 -> x0, local copies, waits for them, and re-layouts: 44.7 us -> none  [the longest x51 41.1 us: kernel_grad(): return jnp.stack(pieces)]
    all_to_all x4 -> x3, waiting for transfers between devices: 40.5 us -> 0.01 us  [exchange(): return lax.all_to_all(value, AXES, 0, 0, tiled=True)]
  transfers between devices with their start and end apart: 7 -> 28, of which waited for: 1 -> 3; matrix products, arithmetic and copies ran while one was open for 38% -> 2% of each run, Pallas kernels for 0% -> 36%
where the time goes in v2:
time: 222 us; the launch traced here: 220 us
  Pallas kernels  129 us (58%)
  starting transfers between devices  62.6 us (28%)
  local copies, waits for them, and re-layouts  12.8 us (6%)
  waiting for transfers between devices  8.56 us (4%)
  other arithmetic  5.42 us (2%)
    pallas_call x1, Pallas kernels, mlp(): pl.pallas_call(mlp_kernel, grid_spec=pltpu.PrefetchScalarGridSpec(num_sca...  43.7 us
    pallas_call x3, Pallas kernels, conv_norm(): return run(order, ranges, sides, above, own, below, cot, pars, *earlier)  29.1 us
    all_to_all x3, starting transfers between devices, exchange(): return lax.all_to_all(value, AXES, 0, 0, tiled=True)  27.6 us
    pallas_call x3, Pallas kernels, finish(): run(order, ranges, sides, above, gc, below, branch, images, cot, pars, *e...  27.5 us
    ppermute x19, starting transfers between devices, swap(): return lax.ppermute(value, axis, flip_perm(size, bit))  22.7 us
    pallas_call x1, Pallas kernels, taps_grad(): run(order, ranges, sides, halos[0], own, halos[1], halos[2], halos[3], gc...  13.8 us
    ppermute x19, waiting for transfers between devices, swap(): return lax.ppermute(value, axis, flip_perm(size, bit))  8.54 us
    ppermute x3, starting transfers between devices, pass_rows(): above = lax.ppermute(low, 'space', [(i, i + 1) for i in range(places - 1)])  8.54 us
  transfers between devices with their start and end apart: 28, of which 3 were waited for; matrix products, arithmetic and copies ran while one was open for 2% of the time, Pallas kernels for 36%

profile of v2, /device:TPU:0, one launch (start us, length us, event | category | flops | bytes accessed | tf_op | source)
XLA Modules:
  0.0 219.6 jit_solution(11680075449447160811)
XLA Ops:
  0.7 2.5 %pack.1 = (f32[32,8,128]{2,1,0:T(8,128)}, bf16[48,768]{1,0:T(8,128)(2,1)}, s32[32]{0:T(128)}, s32[6,5]{1,0:T(8,128)}, s32[32]{0:T(128)}, /*index=5*/s32[1]{0:T(128)}) custom-call(s32[32]{0:T(128)} %keep_ref.1, f32[12,49]{1,0:T(8,128)} %bitcast.29, f32[5,12]{1,0:T(8,128)} %refs_3_.1, f32[1,48]{1,0:T(1,128)} %bitcast.33, f32[48,384]{1,0:T(8,128)} %bitcast.25, ...), custom_call_target="tpu_custom_call" | custom-call | tf_op jit(solution)/shard_map/pack/pallas_call | solution.py:835
  3.1 1.5 fusion.1
  4.6 1.3 collective-permute-start.6
  5.9 3.1 %collective-permute-start.5 = (bf16[12,3,24,384]{3,2,1,0:T(8,128)(2,1)S(1)}, bf16[12,3,24,384]{3,2,1,0:T(8,128)(2,1)S(1)}, u32[]{:S(2)}, u32[]{:S(2)}) collective-permute-start(bf16[12,3,24,384]{3,2,1,0:T(8,128)(2,1)S(1)} %get-tuple-element.193), channel_id=1, source_target_pairs={{0,1},{1,2},{2,3},{4,5},{5,6},{6,7},{8,9},{9,10},{10,11},{12,13},{... | collective-permute-start | bytes 1990664 | tf_op jit(solution)/shard_map/ppermute | solution.py:917
  9.0 7.3 %all-to-all-start = ((f32[32,8,128]{2,1,0:T(8,128)}), f32[32,8,128]{2,1,0:T(8,128)S(1)}, u32[]{:S(2)}, u32[]{:S(2)}) async-start(f32[32,8,128]{2,1,0:T(8,128)} %get-tuple-element.107), calls=%async_computation | async-start | bytes 262144 | tf_op jit(solution)/shard_map/all_to_all | solution.py:962
  16.3 3.7 %collective-permute-start.2 = (bf16[48,768]{1,0:T(8,128)(2,1)S(1)}, bf16[48,768]{1,0:T(8,128)(2,1)S(1)}, u32[]{:S(2)}, u32[]{:S(2)}) collective-permute-start(bf16[48,768]{1,0:T(8,128)(2,1)S(1)} %copy-done.21), channel_id=1, source_target_pairs={{0,24},{4,28},{8,16},{12,20},{16,8},{20,12},{24,0},{28,4},{1,25},{... | collective-permute-start | bytes 221192 | tf_op jit(solution)/shard_map/ppermute | solution.py:928
  20.0 0.8 collective-permute-start
  20.8 4.4 %collective-permute-done.2.refs_3_ = bf16[48,768]{1,0:T(8,128)(2,1)S(1)} collective-permute-done((bf16[48,768]{1,0:T(8,128)(2,1)S(1)}, bf16[48,768]{1,0:T(8,128)(2,1)S(1)}, u32[]{:S(2)}, u32[]{:S(2)}) %collective-permute-start.2) | collective-permute-done | bytes 73760 | tf_op jit(solution)/shard_map/ppermute | solution.py:928
  25.2 4.0 %collective-permute-done.1.refs_2_ = bf16[48,768]{1,0:T(8,128)(2,1)S(1)} collective-permute-done((bf16[48,768]{1,0:T(8,128)(2,1)S(1)}, bf16[48,768]{1,0:T(8,128)(2,1)S(1)}, u32[]{:S(2)}, u32[]{:S(2)}) %collective-permute-start.1) | collective-permute-done | bytes 73760 | tf_op jit(solution)/shard_map/ppermute | solution.py:928
  29.2 0.6 copy-done.23
  29.8 0.0 copy-done.24
  29.8 1.8 join.2
  31.7 3.8 %fusion = (bf16[20,3,24,384]{3,2,1,0:T(8,128)(2,1)}, bf16[20,3,24,384]{3,2,1,0:T(8,128)(2,1)}) fusion(bf16[32,6,24,384]{3,2,1,0:T(8,128)(2,1)} %image_ref.5), kind=kLoop, calls=%fused_computation.7 | loop fusion | bytes 4423680 | tf_op jit(solution)/shard_map/slice | solution.py:996
  35.5 1.3 collective-permute-start.10
  36.7 3.1 %collective-permute-start.9 = (bf16[20,3,24,384]{3,2,1,0:T(8,128)(2,1)}, bf16[20,3,24,384]{3,2,1,0:T(8,128)(2,1)S(1)}, u32[]{:S(2)}, u32[]{:S(2)}) collective-permute-start(bf16[20,3,24,384]{3,2,1,0:T(8,128)(2,1)} %get-tuple-element.191), channel_id=1, source_target_pairs={{0,1},{1,2},{2,3},{4,5},{5,6},{6,7},{8,9},{9,10},{10,11},{12,13},{... | collective-permute-start | bytes 3317768 | tf_op jit(solution)/shard_map/ppermute | solution.py:917
  39.9 1.5 collective-permute-start.3
  41.4 1.5 collective-permute-start.4
  42.9 2.0 unpack.1
  44.9 10.7 %conv_norm.3 = (f32[32,144,384]{2,1,0:T(8,128)}, f32[32,144,128]{2,1,0:T(8,128)}, bf16[32,6,24,384]{3,2,1,0:T(8,128)(2,1)}) custom-call(s32[32]{0:T(128)} %get-tuple-element.166.order_ref, s32[6,5]{1,0:T(8,128)} %get-tuple-element.116.range_ref, s32[32]{0:T(128)} %side_ref.13, bf16[12,3,24,384]{3,2,1,0:T(8,128)(2,1)} %copy-done.6, ...), custom_call_target="tpu_custom_call" | custom-call | tf_op jit(solution)/shard_map/conv_norm/pallas_call | solution.py:778
  55.6 0.1 collective-permute-done.4.refs_3_
  55.7 0.6 copy-done.17
  56.3 2.0 join.3
  58.3 0.5 collective-permute-start.7
  58.8 1.5 collective-permute-start.8
  60.4 1.5 collective-permute-start.11
  61.8 0.1 collective-permute-start.13
  61.9 0.9 copy-done.2
  62.8 0.4 copy-done.3
  63.2 9.7 %conv_norm.4 = (f32[32,144,384]{2,1,0:T(8,128)}, f32[32,144,128]{2,1,0:T(8,128)}, bf16[32,6,24,384]{3,2,1,0:T(8,128)(2,1)}) custom-call(s32[32]{0:T(128)} %get-tuple-element.166.order_ref, s32[6,5]{1,0:T(8,128)} %get-tuple-element.116.range_ref, s32[32]{0:T(128)} %side_ref.13, ...), custom_call_target="tpu_custom_call", output_to_operand_aliasing={{0}: (8, {}), {1}: (9, {}), {2}: (10, {})} | custom-call | tf_op jit(solution)/shard_map/conv_norm/pallas_call | solution.py:778
  72.9 0.2 collective-permute-start.12
  73.2 0.4 collective-permute-start.14
  73.5 8.7 %conv_norm.5 = (f32[32,144,384]{2,1,0:T(8,128)}, f32[32,144,128]{2,1,0:T(8,128)}, bf16[32,6,24,384]{3,2,1,0:T(8,128)(2,1)}) custom-call(s32[32]{0:T(128)} %get-tuple-element.166.order_ref, s32[6,5]{1,0:T(8,128)} %get-tuple-element.116.range_ref, s32[32]{0:T(128)} %side_ref.13, ...), custom_call_target="tpu_custom_call", output_to_operand_aliasing={{0}: (8, {}), {1}: (9, {}), {2}: (10, {})} | custom-call | tf_op jit(solution)/shard_map/conv_norm/pallas_call | solution.py:778
  82.3 0.7 copy-done.11
  83.0 0.1 copy-done.12
  83.1 0.1 copy-done.13
  83.2 0.1 copy-done.14
  83.3 43.7 %mlp.1 = (bf16[32,6,24,384]{3,2,1,0:T(8,128)(2,1)}, bf16[32,6,24,384]{3,2,1,0:T(8,128)(2,1)}, bf16[32,3,24,384]{3,2,1,0:T(8,128)(2,1)}, bf16[32,3,24,384]{3,2,1,...) custom-call(s32[1]{0:T(128)} %get-tuple-element.105.count_ref, ...), custom_call_target="tpu_custom_call" | custom-call | tf_op jit(solution)/shard_map/mlp/pallas_call | solution.py:669
  126.9 0.2 collective-permute-start.15
  127.1 2.4 %collective-permute-start.20 = (bf16[32,3,24,384]{3,2,1,0:T(8,128)(2,1)}, bf16[32,3,24,384]{3,2,1,0:T(8,128)(2,1)S(1)}, u32[]{:S(2)}, u32[]{:S(2)}) collective-permute-start(bf16[32,3,24,384]{3,2,1,0:T(8,128)(2,1)} %get-tuple-element.152), channel_id=1, source_target_pairs={{0,1},{1,2},{2,3},{4,5},{5,6},{6,7},{8,9},{9,10},{10,11},{12,13},{... | collective-permute-start | bytes 5308424 | tf_op jit(solution)/shard_map/ppermute | solution.py:917
  129.5 1.3 collective-permute-start.21
  130.8 1.1 copy-done.4
  131.9 2.0 add_convert_fusion
  133.9 2.3 %collective-permute-start.16 = (bf16[192,768]{1,0:T(8,128)(2,1)}, bf16[192,768]{1,0:T(8,128)(2,1)}, u32[]{:S(2)}, u32[]{:S(2)}) collective-permute-start(bf16[192,768]{1,0:T(8,128)(2,1)} %get-tuple-element.200), channel_id=1, source_target_pairs={{0,2},{1,3},{2,0},{3,1},{4,6},{5,7},{6,4},{7,5},{8,10},{9,11},{10,... | collective-permute-start | bytes 884744 | tf_op jit(solution)/shard_map/ppermute | solution.py:928
  136.2 13.8 %taps_grad.1.taps_ref = f32[49,384]{1,0:T(8,128)} custom-call(s32[32]{0:T(128)} %get-tuple-element.166.order_ref, s32[6,5]{1,0:T(8,128)} %get-tuple-element.116.range_ref, s32[32]{0:T(128)} %side_ref.13, bf16[12,3,24,384]{3,2,1,0:T(8,128)(2,1)} %copy-done.6, bf16[32,6,24,384]{3,2,1,0:T(8,128)(2,1)} %image_ref.5, bf16[12,3,24,384]{3,2,1,0:T(8,128)(2,1)} %copy-done.5, ...), custom_call_target="tpu_custom_call" | custom-call | tf_op jit(solution)/shard_map/taps_grad/pallas_call | solution.py:799
  150.0 2.1 pack_grads.1
  152.1 15.5 %all-to-all-start.1 = ((f32[32,8,128]{2,1,0:T(8,128)}), f32[32,8,128]{2,1,0:T(8,128)}, u32[]{:S(2)}, u32[]{:S(2)}) async-start(f32[32,8,128]{2,1,0:T(8,128)} %pack_grads.1), calls=%async_computation.1 | async-start | bytes 262144 | tf_op jit(solution)/shard_map/all_to_all | solution.py:962
  167.6 2.1 add_convert_fusion.2
  169.7 1.7 collective-permute-start.19
  171.4 1.5 collective-permute-start.18
  172.9 1.2 copy-done
  174.1 0.5 copy-done.1
  174.6 8.1 %finish.3 = (bf16[32,6,24,384]{3,2,1,0:T(8,128)(2,1)}, bf16[32,6,24,384]{3,2,1,0:T(8,128)(2,1)}) custom-call(s32[32]{0:T(128)} %get-tuple-element.166.order_ref, s32[6,5]{1,0:T(8,128)} %get-tuple-element.116.range_ref, s32[32]{0:T(128)} %side_ref.13, bf16[32,3,24,384]{3,2,1,0:T(8,128)(2,1)} %copy-done, bf16[32,6,24,384]{3,2,1,0:T(8,128)(2,1)} %get-tuple-element.146.gc_ref, ...), custom_call_target="tpu_custom_call" | custom-call | tf_op jit(solution)/shard_map/finish/pallas_call | solution.py:830
  182.7 1.4 add_convert_fusion.4
  184.1 4.7 %collective-permute-start.24 = (bf16[48,768]{1,0:T(8,128)(2,1)S(1)}, bf16[48,768]{1,0:T(8,128)(2,1)S(1)}, u32[]{:S(2)}, u32[]{:S(2)}) collective-permute-start(bf16[48,768]{1,0:T(8,128)(2,1)S(1)} %get-tuple-element.194), channel_id=1, source_target_pairs={{0,24},{4,28},{8,16},{12,20},{16,8},{20,12},{24,0},{28,4},{1,25},{... | collective-permute-start | bytes 221192 | tf_op jit(solution)/shard_map/ppermute | solution.py:928
  188.8 0.6 collective-permute-start.22
  189.4 7.4 %finish.4 = (bf16[32,6,24,384]{3,2,1,0:T(8,128)(2,1)}, bf16[32,6,24,384]{3,2,1,0:T(8,128)(2,1)}) custom-call(s32[32]{0:T(128)} %get-tuple-element.166.order_ref, s32[6,5]{1,0:T(8,128)} %get-tuple-element.116.range_ref, s32[32]{0:T(128)} %side_ref.13, bf16[32,3,24,384]{3,2,1,0:T(8,128)(2,1)} %copy-done, ...), custom_call_target="tpu_custom_call", output_to_operand_aliasing={{0}: (10, {}), {1}: (11, {})} | custom-call | tf_op jit(solution)/shard_map/finish/pallas_call | solution.py:830
  196.9 0.6 copy-done.18
  197.5 0.0 copy-done.19
  197.5 0.0 copy-done.20
  197.6 2.1 add_up.1
  199.7 4.8 %all-to-all-start.2 = ((f32[32,8,128]{2,1,0:T(8,128)}), f32[32,8,128]{2,1,0:T(8,128)S(1)}, u32[]{:S(2)}, u32[]{:S(2)}) async-start(f32[32,8,128]{2,1,0:T(8,128)} %get-tuple-element.165), calls=%async_computation.2 | async-start | bytes 262144 | tf_op jit(solution)/shard_map/all_to_all | solution.py:962
  204.5 12.0 %finish.5 = (bf16[32,6,24,384]{3,2,1,0:T(8,128)(2,1)}, bf16[32,6,24,384]{3,2,1,0:T(8,128)(2,1)}) custom-call(s32[32]{0:T(128)} %get-tuple-element.166.order_ref, s32[6,5]{1,0:T(8,128)} %get-tuple-element.116.range_ref, s32[32]{0:T(128)} %side_ref.13, bf16[32,3,24,384]{3,2,1,0:T(8,128)(2,1)} %copy-done, ...), custom_call_target="tpu_custom_call", output_to_operand_aliasing={{0}: (10, {}), {1}: (11, {})} | custom-call | tf_op jit(solution)/shard_map/finish/pallas_call | solution.py:830
  216.5 0.6 copy-done.8
  217.1 2.3 %update.1 = (f32[12,49]{1,0:T(8,128)}, f32[12,49]{1,0:T(8,128)}, f32[12,49]{1,0:T(8,128)}, f32[5,12]{1,0:T(8,128)}, f32[5,12]{1,0:T(8,128)}, /*index=5*/f32[5,12...) custom-call(f32[48,768]{1,0:T(8,128)} %get-tuple-element.171.own_ref, ...), custom_call_target="tpu_custom_call" | custom-call | tf_op jit(solution)/shard_map/update/pallas_call | solution.py:905
  (62 shorter events, 0.1 us)
Async XLA Ops:
  3.1 13.2 %copy-start.21 = (bf16[48,768]{1,0:T(8,128)(2,1)S(1)}, bf16[48,768]{1,0:T(8,128)(2,1)}, u32[]{:S(2)}) copy-start(bf16[48,768]{1,0:T(8,128)(2,1)} %get-tuple-element.109.refs_0_) | copy-start | bytes 221188
  4.6 27.0 %collective-permute-start.6 = (bf16[12,3,24,384]{3,2,1,0:T(8,128)(2,1)S(1)}, bf16[12,3,24,384]{3,2,1,0:T(8,128)(2,1)S(1)}, u32[]{:S(2)}, u32[]{:S(2)}) collective-permute-start(bf16[12,3,24,384]{3,2,1,0:T(8,128)(2,1)S(1)} %get-tuple-element.192), channel_id=1, source_target_pairs={{1,0},{2,1},{3,2},{5,4},{6,5},{7,6},{9,8},{10,9},{11,10},{13,12},{... | collective-permute-start | bytes 1990664 | tf_op jit(solution)/shard_map/ppermute | solution.py:918
  5.9 25.7 %collective-permute-start.5 = (bf16[12,3,24,384]{3,2,1,0:T(8,128)(2,1)S(1)}, bf16[12,3,24,384]{3,2,1,0:T(8,128)(2,1)S(1)}, u32[]{:S(2)}, u32[]{:S(2)}) collective-permute-start(bf16[12,3,24,384]{3,2,1,0:T(8,128)(2,1)S(1)} %get-tuple-element.193), channel_id=1, source_target_pairs={{0,1},{1,2},{2,3},{4,5},{5,6},{6,7},{8,9},{9,10},{10,11},{12,13},{... | collective-permute-start | bytes 1990664 | tf_op jit(solution)/shard_map/ppermute | solution.py:917
  9.0 20.2 %all-to-all-start = ((f32[32,8,128]{2,1,0:T(8,128)}), f32[32,8,128]{2,1,0:T(8,128)S(1)}, u32[]{:S(2)}, u32[]{:S(2)}) async-start(f32[32,8,128]{2,1,0:T(8,128)} %get-tuple-element.107), calls=%async_computation | async-start | bytes 262144 | tf_op jit(solution)/shard_map/all_to_all | solution.py:962
  16.3 8.9 %collective-permute-start.2 = (bf16[48,768]{1,0:T(8,128)(2,1)S(1)}, bf16[48,768]{1,0:T(8,128)(2,1)S(1)}, u32[]{:S(2)}, u32[]{:S(2)}) collective-permute-start(bf16[48,768]{1,0:T(8,128)(2,1)S(1)} %copy-done.21), channel_id=1, source_target_pairs={{0,24},{4,28},{8,16},{12,20},{16,8},{20,12},{24,0},{28,4},{1,25},{... | collective-permute-start | bytes 221192 | tf_op jit(solution)/shard_map/ppermute | solution.py:928
  20.0 9.2 %collective-permute-start.1 = (bf16[48,768]{1,0:T(8,128)(2,1)S(1)}, bf16[48,768]{1,0:T(8,128)(2,1)S(1)}, u32[]{:S(2)}, u32[]{:S(2)}) collective-permute-start(bf16[48,768]{1,0:T(8,128)(2,1)S(1)} %copy-done.21), channel_id=1, source_target_pairs={{0,16},{4,20},{8,24},{12,28},{16,0},{20,4},{24,8},{28,12},{1,17},{... | collective-permute-start | bytes 221192 | tf_op jit(solution)/shard_map/ppermute | solution.py:928
  20.0 9.2 %collective-permute-start = (bf16[48,768]{1,0:T(8,128)(2,1)S(1)}, bf16[48,768]{1,0:T(8,128)(2,1)S(1)}, u32[]{:S(2)}, u32[]{:S(2)}) collective-permute-start(bf16[48,768]{1,0:T(8,128)(2,1)S(1)} %copy-done.21), channel_id=1, source_target_pairs={{0,8},{4,12},{8,0},{12,4},{16,24},{20,28},{24,16},{28,20},{1,9},{5... | collective-permute-start | bytes 221192 | tf_op jit(solution)/shard_map/ppermute | solution.py:928
  25.2 4.0 %copy-start.22 = (bf16[48,768]{1,0:T(8,128)(2,1)}, bf16[48,768]{1,0:T(8,128)(2,1)S(1)}, u32[]{:S(2)}) copy-start(bf16[48,768]{1,0:T(8,128)(2,1)S(1)} %collective-permute-done.2.refs_3_) | copy-start | bytes 221188
  29.2 0.6 copy-start.23
  29.2 0.7 copy-start.24
  29.8 5.6 %copy-start.7 = (f32[32,8,128]{2,1,0:T(8,128)}, f32[32,8,128]{2,1,0:T(8,128)S(1)}, u32[]{:S(2)}) copy-start(f32[32,8,128]{2,1,0:T(8,128)S(1)} %all-to-all-done.small_ref) | copy-start | bytes 393220
  31.6 8.2 %copy-start.15 = (bf16[96,768]{1,0:T(8,128)(2,1)S(1)}, bf16[96,768]{1,0:T(8,128)(2,1)}, u32[]{:S(2)}) copy-start(bf16[96,768]{1,0:T(8,128)(2,1)} %get-tuple-element.113.refs_0_) | copy-start | bytes 442372
  31.6 9.8 %copy-start.16 = (bf16[96,768]{1,0:T(8,128)(2,1)S(1)}, bf16[96,768]{1,0:T(8,128)(2,1)}, u32[]{:S(2)}) copy-start(bf16[96,768]{1,0:T(8,128)(2,1)} %get-tuple-element.114.refs_2_) | copy-start | bytes 442372
  31.6 13.3 %copy-start.5 = (bf16[12,3,24,384]{3,2,1,0:T(8,128)(2,1)}, bf16[12,3,24,384]{3,2,1,0:T(8,128)(2,1)S(1)}, u32[]{:S(2)}) copy-start(bf16[12,3,24,384]{3,2,1,0:T(8,128)(2,1)S(1)} %collective-permute-done.6.below_ref) | copy-start | bytes 1990660
  31.7 13.3 %copy-start.6 = (bf16[12,3,24,384]{3,2,1,0:T(8,128)(2,1)}, bf16[12,3,24,384]{3,2,1,0:T(8,128)(2,1)S(1)}, u32[]{:S(2)}) copy-start(bf16[12,3,24,384]{3,2,1,0:T(8,128)(2,1)S(1)} %collective-permute-done.5.above_ref) | copy-start | bytes 1990660
  35.5 26.4 %collective-permute-start.10 = (bf16[20,3,24,384]{3,2,1,0:T(8,128)(2,1)}, bf16[20,3,24,384]{3,2,1,0:T(8,128)(2,1)S(1)}, u32[]{:S(2)}, u32[]{:S(2)}) collective-permute-start(bf16[20,3,24,384]{3,2,1,0:T(8,128)(2,1)} %get-tuple-element.190), channel_id=1, source_target_pairs={{1,0},{2,1},{3,2},{5,4},{6,5},{7,6},{9,8},{10,9},{11,10},{13,12},{... | collective-permute-start | bytes 3317768 | tf_op jit(solution)/shard_map/ppermute | solution.py:918
  36.7 25.2 %collective-permute-start.9 = (bf16[20,3,24,384]{3,2,1,0:T(8,128)(2,1)}, bf16[20,3,24,384]{3,2,1,0:T(8,128)(2,1)S(1)}, u32[]{:S(2)}, u32[]{:S(2)}) collective-permute-start(bf16[20,3,24,384]{3,2,1,0:T(8,128)(2,1)} %get-tuple-element.191), channel_id=1, source_target_pairs={{0,1},{1,2},{2,3},{4,5},{5,6},{6,7},{8,9},{9,10},{10,11},{12,13},{... | collective-permute-start | bytes 3317768 | tf_op jit(solution)/shard_map/ppermute | solution.py:917
  39.9 15.7 %collective-permute-start.3 = (bf16[96,768]{1,0:T(8,128)(2,1)S(1)}, bf16[96,768]{1,0:T(8,128)(2,1)S(1)}, u32[]{:S(2)}, u32[]{:S(2)}) collective-permute-start(bf16[96,768]{1,0:T(8,128)(2,1)S(1)} %copy-done.15), channel_id=1, source_target_pairs={{0,4},{4,0},{8,12},{12,8},{16,20},{20,16},{24,28},{28,24},{1,5},{5... | collective-permute-start | bytes 442376 | tf_op jit(solution)/shard_map/ppermute | solution.py:928
  41.4 14.3 %collective-permute-start.4 = (bf16[96,768]{1,0:T(8,128)(2,1)S(1)}, bf16[96,768]{1,0:T(8,128)(2,1)}, u32[]{:S(2)}, u32[]{:S(2)}) collective-permute-start(bf16[96,768]{1,0:T(8,128)(2,1)S(1)} %copy-done.16), channel_id=1, source_target_pairs={{0,2},{1,3},{2,0},{3,1},{4,6},{5,7},{6,4},{7,5},{8,10},{9,11},{10,... | collective-permute-start | bytes 442376 | tf_op jit(solution)/shard_map/ppermute | solution.py:928
  55.6 0.6 copy-start.17
  58.3 14.6 %collective-permute-start.7 = (bf16[192,768]{1,0:T(8,128)(2,1)}, bf16[192,768]{1,0:T(8,128)(2,1)S(1)}, u32[]{:S(2)}, u32[]{:S(2)}) collective-permute-start(bf16[192,768]{1,0:T(8,128)(2,1)} %get-tuple-element.123.refs_0_), channel_id=1, source_target_pairs={{0,2},{1,3},{2,0},{3,1},{4,6},{5,7},{6,4},{7,5},{8,10},{9,11},{10,... | collective-permute-start | bytes 884744 | tf_op jit(solution)/shard_map/ppermute | solution.py:928
  58.8 14.1 %collective-permute-start.8 = (bf16[192,768]{1,0:T(8,128)(2,1)}, bf16[192,768]{1,0:T(8,128)(2,1)S(1)}, u32[]{:S(2)}, u32[]{:S(2)}) collective-permute-start(bf16[192,768]{1,0:T(8,128)(2,1)} %get-tuple-element.124.refs_2_), channel_id=1, source_target_pairs={{0,4},{4,0},{8,12},{12,8},{16,20},{20,16},{24,28},{28,24},{1,5},{5... | collective-permute-start | bytes 884744 | tf_op jit(solution)/shard_map/ppermute | solution.py:928
  60.4 21.9 %collective-permute-start.11 = (bf16[192,768]{1,0:T(8,128)(2,1)}, bf16[192,768]{1,0:T(8,128)(2,1)S(1)}, u32[]{:S(2)}, u32[]{:S(2)}) collective-permute-start(bf16[192,768]{1,0:T(8,128)(2,1)} %get-tuple-element.123.refs_0_), channel_id=1, source_target_pairs={{0,1},{1,0},{2,3},{3,2},{4,5},{5,4},{6,7},{7,6},{8,9},{9,8},{10,11... | collective-permute-start | bytes 884744 | tf_op jit(solution)/shard_map/ppermute | solution.py:928
  61.8 1.0 copy-start.2
  61.8 20.5 %collective-permute-start.13 = (bf16[192,768]{1,0:T(8,128)(2,1)}, bf16[192,768]{1,0:T(8,128)(2,1)S(1)}, u32[]{:S(2)}, u32[]{:S(2)}) collective-permute-start(bf16[192,768]{1,0:T(8,128)(2,1)} %get-tuple-element.124.refs_2_), channel_id=1, source_target_pairs={{0,1},{1,0},{2,3},{3,2},{4,5},{5,4},{6,7},{7,6},{8,9},{9,8},{10,11... | collective-permute-start | bytes 884744 | tf_op jit(solution)/shard_map/ppermute | solution.py:928
  61.9 1.3 copy-start.3
  72.9 9.3 %copy-start.9 = (bf16[192,768]{1,0:T(8,128)(2,1)}, bf16[192,768]{1,0:T(8,128)(2,1)S(1)}, u32[]{:S(2)}) copy-start(bf16[192,768]{1,0:T(8,128)(2,1)S(1)} %collective-permute-done.7.refs_1_) | copy-start | bytes 884740
  72.9 9.3 %copy-start.10 = (bf16[192,768]{1,0:T(8,128)(2,1)}, bf16[192,768]{1,0:T(8,128)(2,1)S(1)}, u32[]{:S(2)}) copy-start(bf16[192,768]{1,0:T(8,128)(2,1)S(1)} %collective-permute-done.8.refs_3_) | copy-start | bytes 884740
  72.9 9.4 %collective-permute-start.12 = (bf16[192,768]{1,0:T(8,128)(2,1)S(1)}, bf16[192,768]{1,0:T(8,128)(2,1)S(1)}, u32[]{:S(2)}, u32[]{:S(2)}) collective-permute-start(bf16[192,768]{1,0:T(8,128)(2,1)S(1)} %collective-permute-done.7.refs_1_), channel_id=1, source_target_pairs={{0,1},{1,0},{2,3},{3,2},{4,5},{5,4},{6,7},{7,6},{8,9},{9,8},{10,11... | collective-permute-start | bytes 884744 | tf_op jit(solution)/shard_map/ppermute | solution.py:928
  73.2 9.2 %collective-permute-start.14 = (bf16[192,768]{1,0:T(8,128)(2,1)S(1)}, bf16[192,768]{1,0:T(8,128)(2,1)S(1)}, u32[]{:S(2)}, u32[]{:S(2)}) collective-permute-start(bf16[192,768]{1,0:T(8,128)(2,1)S(1)} %collective-permute-done.8.refs_3_), channel_id=1, source_target_pairs={{0,1},{1,0},{2,3},{3,2},{4,5},{5,4},{6,7},{7,6},{8,9},{9,8},{10,11... | collective-permute-start | bytes 884744 | tf_op jit(solution)/shard_map/ppermute | solution.py:928
  82.3 0.7 copy-start.11
  82.3 0.8 copy-start.12
  82.3 0.9 copy-start.13
  82.3 0.9 copy-start.14
  126.9 3.9 %collective-permute-start.15 = (bf16[768,768]{1,0:T(8,128)(2,1)}, bf16[768,768]{1,0:T(8,128)(2,1)S(1)}, u32[]{:S(2)}, u32[]{:S(2)}) collective-permute-start(bf16[768,768]{1,0:T(8,128)(2,1)} %get-tuple-element.144), channel_id=1, source_target_pairs={{0,1},{1,0},{2,3},{3,2},{4,5},{5,4},{6,7},{7,6},{8,9},{9,8},{10,11... | collective-permute-start | bytes 3538952 | tf_op jit(solution)/shard_map/ppermute | solution.py:928
  127.1 45.7 %collective-permute-start.20 = (bf16[32,3,24,384]{3,2,1,0:T(8,128)(2,1)}, bf16[32,3,24,384]{3,2,1,0:T(8,128)(2,1)S(1)}, u32[]{:S(2)}, u32[]{:S(2)}) collective-permute-start(bf16[32,3,24,384]{3,2,1,0:T(8,128)(2,1)} %get-tuple-element.152), channel_id=1, source_target_pairs={{0,1},{1,2},{2,3},{4,5},{5,6},{6,7},{8,9},{9,10},{10,11},{12,13},{... | collective-permute-start | bytes 5308424 | tf_op jit(solution)/shard_map/ppermute | solution.py:917
  129.5 43.3 %collective-permute-start.21 = (bf16[32,3,24,384]{3,2,1,0:T(8,128)(2,1)}, bf16[32,3,24,384]{3,2,1,0:T(8,128)(2,1)S(1)}, u32[]{:S(2)}, u32[]{:S(2)}) collective-permute-start(bf16[32,3,24,384]{3,2,1,0:T(8,128)(2,1)} %get-tuple-element.153), channel_id=1, source_target_pairs={{1,0},{2,1},{3,2},{5,4},{6,5},{7,6},{9,8},{10,9},{11,10},{13,12},{... | collective-permute-start | bytes 5308424 | tf_op jit(solution)/shard_map/ppermute | solution.py:918
  130.8 1.1 copy-start.4
  133.9 33.7 %collective-permute-start.17 = (bf16[192,768]{1,0:T(8,128)(2,1)}, bf16[192,768]{1,0:T(8,128)(2,1)}, u32[]{:S(2)}, u32[]{:S(2)}) collective-permute-start(bf16[192,768]{1,0:T(8,128)(2,1)} %get-tuple-element.199), channel_id=1, source_target_pairs={{0,4},{4,0},{8,12},{12,8},{16,20},{20,16},{24,28},{28,24},{1,5},{5... | collective-permute-start | bytes 884744 | tf_op jit(solution)/shard_map/ppermute | solution.py:928
  133.9 33.7 %collective-permute-start.16 = (bf16[192,768]{1,0:T(8,128)(2,1)}, bf16[192,768]{1,0:T(8,128)(2,1)}, u32[]{:S(2)}, u32[]{:S(2)}) collective-permute-start(bf16[192,768]{1,0:T(8,128)(2,1)} %get-tuple-element.200), channel_id=1, source_target_pairs={{0,2},{1,3},{2,0},{3,1},{4,6},{5,7},{6,4},{7,5},{8,10},{9,11},{10,... | collective-permute-start | bytes 884744 | tf_op jit(solution)/shard_map/ppermute | solution.py:928
  152.1 30.6 %all-to-all-start.1 = ((f32[32,8,128]{2,1,0:T(8,128)}), f32[32,8,128]{2,1,0:T(8,128)}, u32[]{:S(2)}, u32[]{:S(2)}) async-start(f32[32,8,128]{2,1,0:T(8,128)} %pack_grads.1), calls=%async_computation.1 | async-start | bytes 262144 | tf_op jit(solution)/shard_map/all_to_all | solution.py:962
  169.7 13.0 %collective-permute-start.19 = (bf16[96,768]{1,0:T(8,128)(2,1)}, bf16[96,768]{1,0:T(8,128)(2,1)}, u32[]{:S(2)}, u32[]{:S(2)}) collective-permute-start(bf16[96,768]{1,0:T(8,128)(2,1)} %get-tuple-element.197), channel_id=1, source_target_pairs={{0,2},{1,3},{2,0},{3,1},{4,6},{5,7},{6,4},{7,5},{8,10},{9,11},{10,... | collective-permute-start | bytes 442376 | tf_op jit(solution)/shard_map/ppermute | solution.py:928
  171.4 11.3 %collective-permute-start.18 = (bf16[96,768]{1,0:T(8,128)(2,1)}, bf16[96,768]{1,0:T(8,128)(2,1)}, u32[]{:S(2)}, u32[]{:S(2)}) collective-permute-start(bf16[96,768]{1,0:T(8,128)(2,1)} %get-tuple-element.198), channel_id=1, source_target_pairs={{0,4},{4,0},{8,12},{12,8},{16,20},{20,16},{24,28},{28,24},{1,5},{5... | collective-permute-start | bytes 442376 | tf_op jit(solution)/shard_map/ppermute | solution.py:928
  172.9 1.2 copy-start
  172.9 1.7 copy-start.1
  184.1 12.8 %collective-permute-start.24 = (bf16[48,768]{1,0:T(8,128)(2,1)S(1)}, bf16[48,768]{1,0:T(8,128)(2,1)S(1)}, u32[]{:S(2)}, u32[]{:S(2)}) collective-permute-start(bf16[48,768]{1,0:T(8,128)(2,1)S(1)} %get-tuple-element.194), channel_id=1, source_target_pairs={{0,24},{4,28},{8,16},{12,20},{16,8},{20,12},{24,0},{28,4},{1,25},{... | collective-permute-start | bytes 221192 | tf_op jit(solution)/shard_map/ppermute | solution.py:928
  188.8 8.1 %collective-permute-start.23 = (bf16[48,768]{1,0:T(8,128)(2,1)S(1)}, bf16[48,768]{1,0:T(8,128)(2,1)S(1)}, u32[]{:S(2)}, u32[]{:S(2)}) collective-permute-start(bf16[48,768]{1,0:T(8,128)(2,1)S(1)} %get-tuple-element.195), channel_id=1, source_target_pairs={{0,16},{4,20},{8,24},{12,28},{16,0},{20,4},{24,8},{28,12},{1,17},{... | collective-permute-start | bytes 221192 | tf_op jit(solution)/shard_map/ppermute | solution.py:928
  188.8 8.1 %collective-permute-start.22 = (bf16[48,768]{1,0:T(8,128)(2,1)S(1)}, bf16[48,768]{1,0:T(8,128)(2,1)S(1)}, u32[]{:S(2)}, u32[]{:S(2)}) collective-permute-start(bf16[48,768]{1,0:T(8,128)(2,1)S(1)} %get-tuple-element.196), channel_id=1, source_target_pairs={{0,8},{4,12},{8,0},{12,4},{16,24},{20,28},{24,16},{28,20},{1,9},{5... | collective-permute-start | bytes 221192 | tf_op jit(solution)/shard_map/ppermute | solution.py:928
  196.9 0.6 copy-start.18
  196.9 0.6 copy-start.19
  196.9 0.6 copy-start.20
  199.7 16.8 %all-to-all-start.2 = ((f32[32,8,128]{2,1,0:T(8,128)}), f32[32,8,128]{2,1,0:T(8,128)S(1)}, u32[]{:S(2)}, u32[]{:S(2)}) async-start(f32[32,8,128]{2,1,0:T(8,128)} %get-tuple-element.165), calls=%async_computation.2 | async-start | bytes 262144 | tf_op jit(solution)/shard_map/all_to_all | solution.py:962
  216.5 0.7 copy-start.8

commit v3 on v2

--- a/solution.py
+++ b/solution.py
@@ -27,9 +27,10 @@
 TAPS = 7
 VEC = TAPS * TAPS
 ROWS = 64
+NARROW = 16
 EDGE = 8
 MLP_SLOTS = 4
-VMEM_MIB = 60
+VMEM_MIB = 64
 DEPTH = 5
 AHEAD = DEPTH - 2
 MLP_COLS = 768
@@ -50,7 +51,7 @@
 
 
 def mlp_kernel(
-    count_ref, unit_ref, stat_ref, cot_ref, bias_ref, par_ref, *refs
+    at, table_ref, unit_ref, stat_ref, cot_ref, bias_ref, par_ref, *refs
 ):
     step = pl.program_id(0)
     rows, channels = unit_ref.shape
@@ -60,7 +61,7 @@
     hidden_size = both_ref.shape[0]
     half = hidden_size // 2
     pixels = rows // MLP_SLOTS
-    used = count_ref[0] * pixels
+    used = table_ref[at] * pixels
     gamma = par_ref[VEC + 4 : VEC + 5, :] * keep_scale
 
     @pl.when(step == 0)
@@ -200,26 +201,32 @@
     return lax.broadcasted_iota(jnp.int32, (cols, LANES), 0) < reach
 
 
-def fill_rows(pad_ref, win_ref, side=None, first_row=None):
+def fill_rows(pad_ref, win_ref, width, side, first_row):
     rows, cols, channels = win_ref.shape
     for row in range(rows):
-        inside = None if side is None else inside_cols(cols, first_row + row, side)
+        inside = inside_cols(width, first_row + row, side)
         for tile in range(channels // LANES):
-            line = win_ref[row, :, tile * LANES : (tile + 1) * LANES].astype(f32)
-            if side is not None:
-                line = jnp.where(inside, line, 0.0)
-            pad_ref[tile, row, EDGE : EDGE + cols, :] = line
-
-
-def conv_tile(pad_ref, tile, par_ref, out_rows, cols, flip):
+            line = win_ref[row, 0:width, tile * LANES : (tile + 1) * LANES].astype(f32)
+            pad_ref[tile, row, EDGE : EDGE + width, :] = jnp.where(inside, line, 0.0)
+            if width < cols:
+                pad_ref[tile, row, EDGE + width : EDGE + cols, :] = jnp.zeros((cols - width, LANES), f32)
+
+
+def by_width(cols, side, work):
+    if NARROW < cols:
+        pl.when(side <= NARROW)(lambda: work(NARROW))
+        pl.when(side > NARROW)(lambda: work(cols))
+    else:
+        work(cols)
+
+
+def conv_tile(pad_ref, tile, par_ref, out_rows, cols):
     lanes = slice(tile * LANES, (tile + 1) * LANES)
     sums = [None] * out_rows
     for col_off in range(TAPS):
         weights = []
         for row_off in range(TAPS):
             index = row_off * TAPS + col_off
-            if flip:
-                index = TAPS * TAPS - 1 - index
             weights.append(par_ref[index : index + 1, lanes])
         for row in range(out_rows + 2 * REACH):
             start = EDGE - REACH + col_off
@@ -233,15 +240,16 @@
 
 
 def conv_norm_kernel(
-    which, first, order_ref, range_ref, side_ref, above_ref, own_ref, below_ref, cot_ref, pars_ref, *rest
+    which, first, table_ref, above_ref, own_ref, below_ref, cot_ref, pars_ref, *rest
 ):
     (unit_ref, stat_ref, cots_ref, win_ref, unit_buf, stat_buf, cot_buf, pad_ref, conv_ref, par_ref,
      in_sems, out_sems, par_sem) = rest[-13:]
-    rows, cols, channels = own_ref.shape[1:]
-    low, high, start = range_ref[which, 0], range_ref[which, 1], range_ref[which, 2]
+    count, rows, cols, channels = own_ref.shape
+    at = 2 * count + 5 * which
+    low, high, start = table_ref[at], table_ref[at + 1], table_ref[at + 2]
 
     def fetch(i, buf):
-        image = order_ref[i]
+        image = table_ref[i]
         win = win_ref.at[buf]
         return copies(
             [
@@ -259,13 +267,20 @@
         return copies([(mine.at[buf], ref.at[i]) for mine, ref in pairs], out_sems, buf)
 
     def compute(i, buf):
-        side = side_ref[order_ref[i]]
-        fill_rows(pad_ref, win_ref.at[buf], side, start - REACH)
-        for tile in range(channels // LANES):
-            lanes = slice(tile * LANES, (tile + 1) * LANES)
-            sums = conv_tile(pad_ref, tile, par_ref, rows, cols, False)
-            for row in range(rows):
-                conv_ref[row * cols : (row + 1) * cols, lanes] = sums[row] + par_ref[VEC : VEC + 1, lanes]
+        side = table_ref[count + i]
+
+        def convolve(width):
+            fill_rows(pad_ref, win_ref.at[buf], width, side, start - REACH)
+            for tile in range(channels // LANES):
+                lanes = slice(tile * LANES, (tile + 1) * LANES)
+                sums = conv_tile(pad_ref, tile, par_ref, rows, width)
+                for row in range(rows):
+                    begin, end = row * cols, (row + 1) * cols
+                    conv_ref[begin : begin + width, lanes] = sums[row] + par_ref[VEC : VEC + 1, lanes]
+                    if width < cols:
+                        conv_ref[begin + width : end, lanes] = jnp.zeros((cols - width, LANES), f32)
+
+        by_width(cols, side, convolve)
 
         @pl.when(i < high)
         def _():
@@ -286,30 +301,31 @@
     walk(low, high, fetch, compute, store, load, lambda: clear_edges(pad_ref, cols))
 
 
-def fill_pairs(pair_ref, win_ref, side=None, first_row=None):
+def fill_pairs(pair_ref, win_ref, width, side=None, first_row=None):
     tiles, pairs = pair_ref.shape[:2]
-    rows, cols, channels = win_ref.shape
+    rows = win_ref.shape[0]
     apart = rows - pairs
     for row in range(rows):
         if side is not None:
-            mask = jnp.where(inside_cols(cols, first_row + row, side), 1.0, 0.0).astype(bf16)
+            mask = jnp.where(inside_cols(width, first_row + row, side), 1.0, 0.0).astype(bf16)
         for tile in range(tiles):
-            line = win_ref[row, :, tile * LANES : (tile + 1) * LANES]
+            line = win_ref[row, 0:width, tile * LANES : (tile + 1) * LANES]
             if side is not None:
                 line = line * mask
             if row < pairs:
-                pair_ref[tile, row, 0:cols, :] = line
+                pair_ref[tile, row, 0:width, :] = line
             if row >= apart:
-                pair_ref[tile, row - apart, cols : 2 * cols, :] = line
+                pair_ref[tile, row - apart, width : 2 * width, :] = line
 
 
 def taps_grad_kernel(
-    which, split, order_ref, range_ref, side_ref, above_ref, own_ref, below_ref, far_above_ref, far_below_ref, gc_ref,
-    out_ref, win_ref, gc_buf, pair_ref, acc_ref, grad_ref, in_sems,
+    which, split, table_ref, above_ref, own_ref, below_ref, far_above_ref, far_below_ref, gc_ref,
+    owner_ref, vec_ref, bias_ref, out_ref, win_ref, gc_buf, pair_ref, acc_ref, grad_ref, rows_ref, in_sems,
 ):
-    rows, cols, channels = own_ref.shape[1:]
+    count, rows, cols, channels = own_ref.shape
     half = rows // 2
-    low, high, start = range_ref[which, 0], range_ref[which, 1], range_ref[which, 2]
+    at = 2 * count + 5 * which
+    low, high, start = table_ref[at], table_ref[at + 1], table_ref[at + 2]
 
     def halo_copies(above, below, image, buf):
         win = win_ref.at[buf]
@@ -338,52 +354,60 @@
                 copy.wait()
 
     def fetch(i, buf):
-        image = order_ref[i]
+        image = table_ref[i]
         win = win_ref.at[buf]
         near = copies([(own_ref.at[image], win.at[REACH : REACH + rows]), (gc_ref.at[i], gc_buf.at[buf])], in_sems, buf)
         return near + [Halo(image, buf)]
 
     def compute(i, buf):
-        fill_pairs(pair_ref, win_ref.at[buf], side_ref[order_ref[i]], start - REACH)
-        for row in range(rows):
+        side = table_ref[count + i]
+
+        def multiply(width):
+            fill_pairs(pair_ref, win_ref.at[buf], width, side, start - REACH)
+            for row in range(rows):
+                for tile in range(channels // LANES):
+                    line = gc_buf[buf, row, :, tile * LANES : (tile + 1) * LANES]
+                    grad_ref[tile, row, EDGE : EDGE + cols, :] = line.astype(f32)
             for tile in range(channels // LANES):
-                line = gc_buf[buf, row, :, tile * LANES : (tile + 1) * LANES]
-                grad_ref[tile, row, EDGE : EDGE + cols, :] = line.astype(f32)
-        for tile in range(channels // LANES):
-            lanes = slice(tile * LANES, (tile + 1) * LANES)
-            for col_off in range(TAPS):
-                at = EDGE + REACH - col_off
-                grads = []
-                for row in range(half):
-                    two = [grad_ref[tile, row, at : at + cols, :], grad_ref[tile, row + half, at : at + cols, :]]
-                    grads.append(jnp.concatenate(two, axis=0).astype(bf16))
-                for row_off in range(TAPS):
-                    total = grads[0] * pair_ref[tile, row_off]
-                    for row in range(1, half):
-                        total = total + grads[row] * pair_ref[tile, row_off + row]
-                    total = total[0:16] + total[16:32] + total[32:48]
-                    acc_ref[row_off * TAPS + col_off, :, lanes] += fold(total.astype(f32))
+                lanes = slice(tile * LANES, (tile + 1) * LANES)
+                for col_off in range(TAPS):
+                    at = EDGE + REACH - col_off
+                    grads = []
+                    for row in range(half):
+                        two = [grad_ref[tile, r, at : at + width, :] for r in (row, row + half)]
+                        grads.append(jnp.concatenate(two, axis=0).astype(bf16))
+                    for row_off in range(TAPS):
+                        total = grads[0] * pair_ref[tile, row_off, 0 : 2 * width]
+                        for row in range(1, half):
+                            total = total + grads[row] * pair_ref[tile, row_off + row, 0 : 2 * width]
+                        short = total[0:16]
+                        for begin in range(16, 2 * width, 16):
+                            short = short + total[begin : begin + 16]
+                        acc_ref[row_off * TAPS + col_off, :, lanes] += fold(short.astype(f32))
+
+        by_width(cols, side, multiply)
 
     def prepare():
         acc_ref[...] = jnp.zeros_like(acc_ref)
         clear_edges(grad_ref, cols)
 
     walk(low, high, fetch, compute, lambda i, buf: [], None, prepare)
-    out_ref[...] = jnp.sum(acc_ref[...], axis=1)
+    pack_grads(owner_ref, jnp.sum(acc_ref[...], axis=1), vec_ref, bias_ref, out_ref, rows_ref)
 
 
 def finish_kernel(
-    which, order_ref, range_ref, side_ref, above_ref, gc_ref, below_ref, branch_ref, image_ref, cot_ref, pars_ref, *rest
+    which, table_ref, above_ref, gc_ref, below_ref, branch_ref, image_ref, cot_ref, pars_ref, *rest
 ):
     (out_ref, gim_ref, win_ref, branch_buf, image_buf, cot_buf, out_buf, gim_buf, pair_ref, part_ref, sum_ref, par_ref,
      in_sems, out_sems, par_sem) = rest[-15:]
-    rows, cols, channels = image_ref.shape[1:]
+    count, rows, cols, channels = image_ref.shape
     half = rows // 2
-    low, high, start = range_ref[which, 0], range_ref[which, 1], range_ref[which, 2]
-    plain_low, plain_high = range_ref[which, 3], range_ref[which, 4]
+    at = 2 * count + 5 * which
+    low, high, start = table_ref[at], table_ref[at + 1], table_ref[at + 2]
+    plain_low, plain_high = table_ref[at + 3], table_ref[at + 4]
 
     def fetch(i, buf):
-        image = order_ref[i]
+        image = table_ref[i]
         win = win_ref.at[buf]
         return copies(
             [
@@ -399,42 +423,48 @@
         )
 
     def store(i, buf):
-        image = order_ref[i]
+        image = table_ref[i]
         return copies([(out_buf.at[buf], out_ref.at[image]), (gim_buf.at[buf], gim_ref.at[image])], out_sems, buf)
 
     def pass_in(i, buf):
-        image = order_ref[i]
+        image = table_ref[i]
         return copies([(image_ref.at[image], image_buf.at[buf]), (cot_ref.at[image], cot_buf.at[buf])], in_sems, buf)
 
     def pass_out(i, buf):
-        image = order_ref[i]
+        image = table_ref[i]
         return copies([(image_buf.at[buf], out_ref.at[image]), (cot_buf.at[buf], gim_ref.at[image])], out_sems, buf)
 
     def compute(i, buf):
-        side = side_ref[order_ref[i]]
-        fill_pairs(pair_ref, win_ref.at[buf])
-        for tile in range(channels // LANES):
-            lanes = slice(tile * LANES, (tile + 1) * LANES)
-            for col_off in range(TAPS):
-                at = EDGE
-                weights = []
-                for row_off in range(TAPS):
-                    index = TAPS * TAPS - 1 - row_off * TAPS - col_off
-                    weights.append(par_ref[index : index + 1, lanes].astype(bf16))
-                for row in range(half):
-                    total = weights[0] * pair_ref[tile, row]
-                    for row_off in range(1, TAPS):
-                        total = total + weights[row_off] * pair_ref[tile, row + row_off]
-                    total = total.astype(f32)
-                    part_ref[col_off, row, at : at + cols, :] = total[0:cols]
-                    part_ref[col_off, row + half, at : at + cols, :] = total[cols : 2 * cols]
-            for row in range(rows):
-                total = part_ref[REACH, row, EDGE : EDGE + cols, :]
+        side = table_ref[count + i]
+
+        def convolve(width):
+            fill_pairs(pair_ref, win_ref.at[buf], width)
+            for tile in range(channels // LANES):
+                lanes = slice(tile * LANES, (tile + 1) * LANES)
                 for col_off in range(TAPS):
-                    if col_off != REACH:
-                        at = EDGE - REACH + col_off
-                        total = total + part_ref[col_off, row, at : at + cols, :]
-                sum_ref[row, :, lanes] = total
+                    at = EDGE
+                    weights = []
+                    for row_off in range(TAPS):
+                        index = TAPS * TAPS - 1 - row_off * TAPS - col_off
+                        weights.append(par_ref[index : index + 1, lanes].astype(bf16))
+                    for row in range(half):
+                        total = weights[0] * pair_ref[tile, row, 0 : 2 * width]
+                        for row_off in range(1, TAPS):
+                            total = total + weights[row_off] * pair_ref[tile, row + row_off, 0 : 2 * width]
+                        total = total.astype(f32)
+                        for line, begin in ((row, 0), (row + half, width)):
+                            part_ref[col_off, line, at : at + width, :] = total[begin : begin + width]
+                            if width < cols:
+                                part_ref[col_off, line, at + width : at + cols, :] = jnp.zeros((cols - width, LANES), f32)
+                for row in range(rows):
+                    total = part_ref[REACH, row, EDGE : EDGE + width, :]
+                    for col_off in range(TAPS):
+                        if col_off != REACH:
+                            at = EDGE - REACH + col_off
+                            total = total + part_ref[col_off, row, at : at + width, :]
+                    sum_ref[row, 0:width, lanes] = total
+
+        by_width(cols, side, convolve)
 
         @pl.when(i < high)
         def _():
@@ -460,8 +490,8 @@
 
 
 def pack_kernel(
-    spans, codes, space_size, rows, keep_ref, kernel_ref, vectors_ref, bias_ref, up_ref, down_ref,
-    small_ref, piece_ref, order_ref, range_ref, owner_ref, used_ref, rows_ref, seen_ref,
+    spans, codes, space_size, rows, keep_ref, side_ref, kernel_ref, vectors_ref, bias_ref, up_ref, down_ref,
+    small_ref, piece_ref, table_ref, owner_ref, rows_ref, seen_ref,
 ):
     part, channels = up_ref.shape
     width = kernel_ref.shape[0]
@@ -484,7 +514,9 @@
         keep = keep_ref[i] > 0
         upper, lower = at
         seen_ref[i] = upper
-        order_ref[jnp.where(keep, upper, lower)] = i
+        spot = jnp.where(keep, upper, lower)
+        table_ref[spot] = i
+        table_ref[count + spot] = side_ref[i]
         return jnp.where(keep, upper + 1, upper), jnp.where(keep, lower, lower + 1)
 
     kept = lax.fori_loop(0, count, lambda i, at: at + jnp.where(keep_ref[i] > 0, 1, 0), 0)
@@ -493,14 +525,14 @@
     me_space = lax.axis_index("space")
     me = lax.axis_index("dp") * space_size + me_space
     for which, (low, high, plain) in enumerate(spans):
-        range_ref[which, 0] = seen_ref[low]
-        range_ref[which, 1] = seen_ref[high]
-        range_ref[which, 2] = me_space * rows
-        range_ref[which, 3] = jnp.maximum(kept, plain)
-        range_ref[which, 4] = jnp.maximum(kept, count)
+        at = 2 * count + 5 * which
+        table_ref[at] = seen_ref[low]
+        table_ref[at + 1] = seen_ref[high]
+        table_ref[at + 2] = me_space * rows
+        table_ref[at + 3] = jnp.maximum(kept, plain)
+        table_ref[at + 4] = jnp.maximum(kept, count)
     for at, code in enumerate(codes):
         owner_ref[at] = code if space_size != 4 or len(codes) != 32 else me ^ code
-    used_ref[0] = kept
 
 
 def join_kernel(*refs):
@@ -544,13 +576,13 @@
                     bias_ref[0:1, lanes] = jnp.where(lane_mask(lower, upper), moved, kept)[0:1]
 
 
-def pack_grads_kernel(order_ref, taps_ref, vec_ref, bias_ref, out_ref, rows_ref):
+def pack_grads(owner_ref, taps, vec_ref, bias_ref, out_ref, rows_ref):
     devices = out_ref.shape[0]
-    channels = taps_ref.shape[1]
+    channels = taps.shape[1]
     width = channels // devices
     part = bias_ref.shape[1] // devices
     rows_ref[...] = jnp.zeros_like(rows_ref)
-    rows_ref[0:VEC, :] = taps_ref[...]
+    rows_ref[0:VEC, :] = taps
     rows_ref[VEC : VEC + 5, :] = vec_ref[0:5, :]
 
     def cut(row_slice, source, start, group):
@@ -575,7 +607,7 @@
             total = jnp.where(lane_mask(group * width, (group + 1) * width), moved, total)
         out_ref[device] = total
     for place in range(devices):
-        device = order_ref[place]
+        device = owner_ref[place]
         for at in range(part // width):
             row = VEC + 5 + at
             group, line = row // 8, row % 8
@@ -650,15 +682,16 @@
             ref[0:1, lanes] = value
 
 
-def mlp(kept, unit, stat, cots, pieces, bias, pars, dims):
+def mlp(which, table, unit, stat, cots, pieces, bias, pars, dims):
     count, rows, cols, channels = dims
     pixels = rows * cols
     total = count * pixels
     hidden_size = bias.shape[1]
     tall = MLP_SLOTS * pixels
+    at = 2 * count + 5 * which + 1
 
     def last(i, n):
-        return jnp.minimum(i, jnp.maximum((n[0] + MLP_SLOTS - 1) // MLP_SLOTS - 1, 0))
+        return jnp.minimum(i, jnp.maximum((n[at] + MLP_SLOTS - 1) // MLP_SLOTS - 1, 0))
 
     tile_map = lambda i, n: (last(i, n), 0)
     slot_map = lambda i, n: (last(i, n), 0, 0, 0)
@@ -667,7 +700,7 @@
     halo = (count, REACH, cols, channels)
     once = pl.Buffered(1)
     return pl.pallas_call(
-        mlp_kernel,
+        functools.partial(mlp_kernel, at),
         grid_spec=pltpu.PrefetchScalarGridSpec(
             num_scalar_prefetch=1,
             grid=(-(-count // MLP_SLOTS),),
@@ -710,7 +743,7 @@
         ],
         compiler_params=pltpu.CompilerParams(dimension_semantics=("arbitrary",), vmem_limit_bytes=VMEM_MIB * MIB),
         name="mlp",
-    )(kept, unit.reshape(total, channels), stat.reshape(total, LANES), cots.reshape(total, channels), bias, pars, *pieces)
+    )(table, unit.reshape(total, channels), stat.reshape(total, LANES), cots.reshape(total, channels), bias, pars, *pieces)
 
 
 IN_PLACE = pl.BlockSpec(memory_space=pltpu.HBM)
@@ -747,7 +780,7 @@
     return pltpu.VMEM((channels // LANES, rows // 2 + 2 * REACH, 2 * cols, LANES), bf16)
 
 
-def conv_norm(which, first, order, ranges, sides, above, own, below, cot, pars, earlier):
+def conv_norm(which, first, table, above, own, below, cot, pars, earlier):
     count, rows, cols, channels = own.shape
     pixels = rows * cols
     outs = [
@@ -757,7 +790,7 @@
     ]
     run = call(
         functools.partial(conv_norm_kernel, which, first),
-        [SCALARS] * 3 + [IN_PLACE] * (5 + len(earlier)),
+        [SCALARS] + [IN_PLACE] * (5 + len(earlier)),
         [IN_PLACE] * 3,
         outs,
         [
@@ -773,38 +806,38 @@
             pltpu.SemaphoreType.DMA,
         ],
         "conv_norm",
-        {8 + at: at for at in range(len(earlier))},
+        {6 + at: at for at in range(len(earlier))},
     )
-    return run(order, ranges, sides, above, own, below, cot, pars, *earlier)
-
-
-def taps_grad(which, order, ranges, sides, halos, own, gc):
+    return run(table, above, own, below, cot, pars, *earlier)
+
+
+def taps_grad(which, table, halos, own, gc, owners, vec, bias):
     count, rows, cols, channels = own.shape
-    pixels = rows * cols
     run = call(
         functools.partial(taps_grad_kernel, which, halos[0].shape[0]),
-        [SCALARS] * 3 + [IN_PLACE] * 6,
+        [SCALARS] + [IN_PLACE] * 6 + [SCALARS] + [LOADED] * 2,
         LOADED,
-        shape((TAPS * TAPS, channels), f32),
+        shape((owners.shape[0], 8, LANES), f32),
         [
             window(rows, cols, channels),
             pltpu.VMEM((DEPTH, rows, cols, channels), bf16),
             paired(rows, cols, channels),
             pltpu.VMEM((TAPS * TAPS, 8, channels), f32),
             pltpu.VMEM((channels // LANES, rows, cols + 2 * EDGE, LANES), f32),
+            pltpu.VMEM((ROWS, channels), f32),
             pltpu.SemaphoreType.DMA((DEPTH, 4)),
         ],
         "taps_grad",
     )
-    return run(order, ranges, sides, halos[0], own, halos[1], halos[2], halos[3], gc.reshape(own.shape))
-
-
-def finish(which, order, ranges, sides, above, gc, below, branch, images, cot, pars, earlier):
+    return run(table, halos[0], own, halos[1], halos[2], halos[3], gc, owners, vec, bias)
+
+
+def finish(which, table, above, gc, below, branch, images, cot, pars, earlier):
     count, rows, cols, channels = images.shape
     block = (DEPTH, rows, cols, channels)
     run = call(
         functools.partial(finish_kernel, which),
-        [SCALARS] * 3 + [IN_PLACE] * (7 + len(earlier)),
+        [SCALARS] + [IN_PLACE] * (7 + len(earlier)),
         [IN_PLACE] * 2,
         [shape(images.shape, bf16)] * 2,
         [
@@ -823,30 +856,28 @@
             pltpu.SemaphoreType.DMA,
         ],
         "finish",
-        {10 + at: at for at in range(len(earlier))},
+        {8 + at: at for at in range(len(earlier))},
     )
     maps = (value.reshape(images.shape) for value in (gc, branch))
     gc, branch = maps
-    return run(order, ranges, sides, above, gc, below, branch, images, cot, pars, *earlier)
-
-
-def pack(spans, codes, space_size, rows, keep, kernel, vectors, bias, up, down):
+    return run(table, above, gc, below, branch, images, cot, pars, *earlier)
+
+
+def pack(spans, codes, space_size, rows, keep, sides, kernel, vectors, bias, up, down):
     channels, part = up.shape
     return call(
         functools.partial(pack_kernel, spans, codes, space_size, rows),
-        [SCALARS] + [LOADED] * 5,
-        [LOADED] * 2 + [SCALARS] * 4,
+        [SCALARS] * 2 + [LOADED] * 5,
+        [LOADED] * 2 + [SCALARS] * 2,
         [
             shape((len(codes), 8, LANES), f32),
             shape((part, 2 * channels), bf16),
-            shape(keep.shape, jnp.int32),
-            shape((len(spans), 5), jnp.int32),
+            shape((2 * keep.shape[0] + 5 * len(spans),), jnp.int32),
             shape((len(codes),), jnp.int32),
-            shape((1,), jnp.int32),
         ],
         [pltpu.VMEM((LANES, LANES), f32), pltpu.SMEM((keep.shape[0] + 1,), jnp.int32)],
         "pack",
-    )(keep, kernel.T, vectors, bias.reshape(1, -1), up.T, down)
+    )(keep, sides, kernel.T, vectors, bias.reshape(1, -1), up.T, down)
 
 
 def join_two(*pieces):
@@ -865,17 +896,6 @@
         [],
         "unpack",
     )(order, small)
-
-
-def pack_grads(order, taps, vec, bias):
-    return call(
-        pack_grads_kernel,
-        [SCALARS] + [LOADED] * 3,
-        LOADED,
-        shape((order.shape[0], 8, LANES), f32),
-        [pltpu.VMEM((ROWS, taps.shape[1]), f32)],
-        "pack_grads",
-    )(order, taps, vec, bias)
 
 
 def add_up(small, parts, size):
@@ -973,8 +993,8 @@
     cut, mid = 3 * count // 8, 11 * count // 16
     spans = ((0, cut, count), (cut, mid, count), (mid, count, count), (mid, count, 0), (0, count, count), (0, count, 0))
     codes = tuple(cube_order()) if cube else tuple(range(devices))
-    small, piece, order, ranges, owners, kept = pack(
-        spans, codes, space_size, rows, keep_flags, depth_kernel, block_vectors, up_bias, up_weight, down_weight
+    small, piece, table, owners = pack(
+        spans, codes, space_size, rows, keep_flags, image_sides, depth_kernel, block_vectors, up_bias, up_weight, down_weight
     )
     small_all = exchange(small)
     piece, maps = after((piece, images), small) if cube else (piece, images)
@@ -985,7 +1005,7 @@
         above, below = halos[:2] if which == 0 else halos[2:]
         first = 0 if which == 0 else cut
         return conv_norm(
-            which, first, after(order, *waits), ranges, image_sides, above, images, below, cotangent, pars, earlier
+            which, first, after(table, *waits), above, images, below, cotangent, pars, earlier
         )
 
     later = images
@@ -1011,15 +1031,15 @@
         made = conv_part(1, made)
         unit, stat, cots = conv_part(2, made)
     branch, gc, top, low, grad_near, grad_far, bias_sum, vec_sum = mlp(
-        kept, unit, stat, cots, pieces, bias, pars, images.shape
+        4, table, unit, stat, cots, pieces, bias, pars, images.shape
     )
 
     def taps_part(which, *waits):
-        return taps_grad(which, after(order, *waits), ranges, image_sides, halos, images, gc)
+        return taps_grad(which, after(table, *waits), halos, images, gc, owners, vec_sum, bias_sum)
 
     def finish_part(which, earlier, *waits):
         return finish(
-            which, after(order, *waits), ranges, image_sides,
+            which, after(table, *waits),
             gc_above, gc, gc_below, branch, images, cotangent, pars, earlier,
         )
 
@@ -1037,7 +1057,7 @@
         two_a, two_b = swap(send[0], Y), swap(send[1], X)
         taps = taps_part(4, *send)
         two_a, two_b = behind((two_a, two_b), taps)
-        got = exchange(pack_grads(owners, taps, vec_sum, bias_sum))
+        got = exchange(taps)
         send = [kept_sum(0, eighth, quarter, two_a), kept_sum(1, eighth, quarter, two_b)]
         three_a, three_b = swap(send[0], X), swap(send[1], Y)
         made = finish_part(0, (), *send)
@@ -1058,7 +1078,7 @@
         gc_above, gc_below = pass_rows(top, low, space_size)
         grads = jnp.concatenate([grad_near, grad_far]).astype(f32)
         parts = [lax.psum_scatter(grads, AXES, scatter_dimension=0, tiled=True)]
-        got = exchange(pack_grads(owners, taps_part(4), vec_sum, bias_sum))
+        got = exchange(taps_part(4))
         own, sums, norm = add_up(got, parts, part)
         norms = exchange(norm)
         out_images, grad_images = finish_part(5, ())

time: 222 us -> 217 us (0.977)
  starting transfers between devices: 62.6 us -> 50.2 us
  Pallas kernels: 129 us -> 137 us
  waiting for transfers between devices: 8.56 us -> 14.6 us
  local copies, waits for them, and re-layouts: 12.8 us -> 7.46 us
    all_to_all x3, starting transfers between devices: 27.6 us -> 16.8 us  [exchange(): return lax.all_to_all(value, AXES, 0, 0, tiled=True)]
    pallas_call x9 -> x8, Pallas kernels: 116 us -> 125 us  [the longest x1 49.7 us: mlp(): pl.pallas_call(functools.partial(mlp_kernel, at), grid_spec=pltpu.Prefetc...]
    ppermute x19, waiting for transfers between devices: 8.54 us -> 14.5 us  [swap(): return lax.ppermute(value, axis, flip_perm(size, bit))]
    unnamed x50 -> x8, local copies, waits for them, and re-layouts: 7.54 us -> 1.66 us
    ppermute x19, starting transfers between devices: 22.7 us -> 18.5 us  [swap(): return lax.ppermute(value, axis, flip_perm(size, bit))]
    ppermute x3, starting transfers between devices: 8.54 us -> 11.2 us  [pass_rows(): above = lax.ppermute(low, 'space', [(i, i + 1) for i in range(places - 1)])]
  transfers between devices with their start and end apart: 28 -> 28, of which waited for: 3 -> 3; matrix products, arithmetic and copies ran while one was open for 2% -> 2% of each run, Pallas kernels for 36% -> 37%
where the time goes in v3:
time: 217 us
  Pallas kernels  137 us (63%)
  starting transfers between devices  50.2 us (23%)
  waiting for transfers between devices  14.6 us (7%)
  local copies, waits for them, and re-layouts  7.46 us (3%)
  other arithmetic  6.07 us (3%)
    pallas_call x1, Pallas kernels, mlp(): pl.pallas_call(functools.partial(mlp_kernel, at), grid_spec=pltpu.Prefetc...  49.7 us
    pallas_call x3, Pallas kernels, conv_norm(): return run(table, above, own, below, cot, pars, *earlier)  30.9 us
    pallas_call x3, Pallas kernels, finish(): return run(table, above, gc, below, branch, images, cot, pars, *earlier)  28.4 us
    ppermute x19, starting transfers between devices, swap(): return lax.ppermute(value, axis, flip_perm(size, bit))  18.5 us
    all_to_all x3, starting transfers between devices, exchange(): return lax.all_to_all(value, AXES, 0, 0, tiled=True)  16.8 us
    pallas_call x1, Pallas kernels, taps_grad(): run(table, halos[0], own, halos[1], halos[2], halos[3], gc, owners, vec,...  15.5 us
    ppermute x19, waiting for transfers between devices, swap(): return lax.ppermute(value, axis, flip_perm(size, bit))  14.5 us
    ppermute x3, starting transfers between devices, pass_rows(): above = lax.ppermute(low, 'space', [(i, i + 1) for i in range(places - 1)])  11.2 us
  transfers between devices with their start and end apart: 28, of which 3 were waited for; matrix products, arithmetic and copies ran while one was open for 2% of the time, Pallas kernels for 37%

profile of v3, /device:TPU:0, one launch (start us, length us, event | category | flops | bytes accessed | tf_op | source)
XLA Modules:
  0.0 216.8 jit_solution(2464532889852518320)
XLA Ops:
  0.7 2.5 %pack.1 = (f32[32,8,128]{2,1,0:T(8,128)}, bf16[48,768]{1,0:T(8,128)(2,1)}, s32[94]{0:T(128)}, s32[32]{0:T(128)}) custom-call(s32[32]{0:T(128)} %keep_ref.1, s32[32]{0:T(128)} %side_ref.1, f32[12,49]{1,0:T(8,128)} %bitcast.29, f32[5,12]{1,0:T(8,128)} %refs_3_.1, f32[1,48]{1,0:T(1,128)} %bitcast.33, f32[48,384]{1,0:T(8,128)} %bitcast.25, f32[48,384]{1,0:T(8,128)} %refs_12_.1), custom_call_target="tpu_custom_call" | custom-call | tf_op jit(solution)/shard_map/pack/pallas_call | solution.py:868
  3.1 0.0 copy-start.1
  3.1 2.5 %fusion.1 = (bf16[12,3,24,384]{3,2,1,0:T(8,128)(2,1)}, bf16[12,3,24,384]{3,2,1,0:T(8,128)(2,1)}) fusion(bf16[32,6,24,384]{3,2,1,0:T(8,128)(2,1)} %image_ref.5), kind=kLoop, calls=%fused_computation.8 | loop fusion | bytes 2654208 | tf_op jit(solution)/shard_map/slice | solution.py:1001
  5.6 1.3 collective-permute-start.6
  6.9 3.9 %collective-permute-start.5 = (bf16[12,3,24,384]{3,2,1,0:T(8,128)(2,1)}, bf16[12,3,24,384]{3,2,1,0:T(8,128)(2,1)}, u32[]{:S(2)}, u32[]{:S(2)}) collective-permute-start(bf16[12,3,24,384]{3,2,1,0:T(8,128)(2,1)} %get-tuple-element.189), channel_id=1, source_target_pairs={{0,1},{1,2},{2,3},{4,5},{5,6},{6,7},{8,9},{9,10},{10,11},{12,13},{... | collective-permute-start | bytes 1990664 | tf_op jit(solution)/shard_map/ppermute | solution.py:937
  10.8 7.4 %all-to-all-start = ((f32[32,8,128]{2,1,0:T(8,128)}), f32[32,8,128]{2,1,0:T(8,128)}, u32[]{:S(2)}, u32[]{:S(2)}) async-start(f32[32,8,128]{2,1,0:T(8,128)} %get-tuple-element.104), calls=%async_computation | async-start | bytes 262144 | tf_op jit(solution)/shard_map/all_to_all | solution.py:982
  18.3 3.6 %collective-permute-start.2 = (bf16[48,768]{1,0:T(8,128)(2,1)S(1)}, bf16[48,768]{1,0:T(8,128)(2,1)S(1)}, u32[]{:S(2)}, u32[]{:S(2)}) collective-permute-start(bf16[48,768]{1,0:T(8,128)(2,1)S(1)} %copy-done.1), channel_id=1, source_target_pairs={{0,24},{4,28},{8,16},{12,20},{16,8},{20,12},{24,0},{28,4},{1,25},{... | collective-permute-start | bytes 221192 | tf_op jit(solution)/shard_map/ppermute | solution.py:948
  21.9 0.8 collective-permute-start
  22.7 4.3 %collective-permute-done.2.refs_3_ = bf16[48,768]{1,0:T(8,128)(2,1)S(1)} collective-permute-done((bf16[48,768]{1,0:T(8,128)(2,1)S(1)}, bf16[48,768]{1,0:T(8,128)(2,1)S(1)}, u32[]{:S(2)}, u32[]{:S(2)}) %collective-permute-start.2) | collective-permute-done | bytes 73760 | tf_op jit(solution)/shard_map/ppermute | solution.py:948
  27.0 4.0 %collective-permute-done.1.refs_2_ = bf16[48,768]{1,0:T(8,128)(2,1)S(1)} collective-permute-done((bf16[48,768]{1,0:T(8,128)(2,1)S(1)}, bf16[48,768]{1,0:T(8,128)(2,1)S(1)}, u32[]{:S(2)}, u32[]{:S(2)}) %collective-permute-start.1) | collective-permute-done | bytes 73760 | tf_op jit(solution)/shard_map/ppermute | solution.py:948
  31.0 0.6 copy-done.3
  31.7 0.0 collective-permute-done.refs_1_
  31.7 0.0 all-to-all-done.small_ref
  31.7 1.7 join.2
  33.4 0.0 collective-permute-done.6.below_ref
  33.4 0.0 collective-permute-done.5.above_ref
  33.4 3.3 %fusion = (bf16[20,3,24,384]{3,2,1,0:T(8,128)(2,1)}, bf16[20,3,24,384]{3,2,1,0:T(8,128)(2,1)}) fusion(bf16[32,6,24,384]{3,2,1,0:T(8,128)(2,1)} %image_ref.5), kind=kLoop, calls=%fused_computation.7 | loop fusion | bytes 4423680 | tf_op jit(solution)/shard_map/slice | solution.py:1016
  36.7 1.3 collective-permute-start.10
  38.0 4.0 %collective-permute-start.9 = (bf16[20,3,24,384]{3,2,1,0:T(8,128)(2,1)}, bf16[20,3,24,384]{3,2,1,0:T(8,128)(2,1)}, u32[]{:S(2)}, u32[]{:S(2)}) collective-permute-start(bf16[20,3,24,384]{3,2,1,0:T(8,128)(2,1)} %get-tuple-element.187), channel_id=1, source_target_pairs={{0,1},{1,2},{2,3},{4,5},{5,6},{6,7},{8,9},{9,10},{10,11},{12,13},{... | collective-permute-start | bytes 3317768 | tf_op jit(solution)/shard_map/ppermute | solution.py:937
  42.0 1.5 collective-permute-start.3
  43.5 1.6 collective-permute-start.4
  45.1 2.0 unpack.1
  47.1 10.1 %conv_norm.3 = (f32[32,144,384]{2,1,0:T(8,128)}, f32[32,144,128]{2,1,0:T(8,128)}, bf16[32,6,24,384]{3,2,1,0:T(8,128)(2,1)}) custom-call(s32[94]{0:T(128)} %get-tuple-element.162.table_ref, bf16[12,3,24,384]{3,2,1,0:T(8,128)(2,1)} %collective-permute-done.5.above_ref, bf16[32,6,24,384]{3,2,1,0:T(8,128)(2,1)} %image_ref.5, ...), custom_call_target="tpu_custom_call" | custom-call | tf_op jit(solution)/shard_map/conv_norm/pallas_call | solution.py:811
  57.2 0.0 collective-permute-done.3.refs_1_
  57.2 2.0 join.3
  59.2 0.5 collective-permute-start.7
  59.7 2.3 %collective-permute-start.8 = (bf16[192,768]{1,0:T(8,128)(2,1)}, bf16[192,768]{1,0:T(8,128)(2,1)}, u32[]{:S(2)}, u32[]{:S(2)}) collective-permute-start(bf16[192,768]{1,0:T(8,128)(2,1)} %get-tuple-element.120.refs_2_), channel_id=1, source_target_pairs={{0,4},{4,0},{8,12},{12,8},{16,20},{20,16},{24,28},{28,24},{1,5},{5... | collective-permute-start | bytes 884744 | tf_op jit(solution)/shard_map/ppermute | solution.py:948
  62.0 1.0 collective-permute-start.11
  63.0 0.0 collective-permute-done.10.below_ref.far_below_ref
  63.0 0.0 collective-permute-start.13
  63.0 0.0 collective-permute-done.9.above_ref.far_above_ref
  63.0 8.9 %conv_norm.4 = (f32[32,144,384]{2,1,0:T(8,128)}, f32[32,144,128]{2,1,0:T(8,128)}, bf16[32,6,24,384]{3,2,1,0:T(8,128)(2,1)}) custom-call(s32[94]{0:T(128)} %get-tuple-element.162.table_ref, bf16[20,3,24,384]{3,2,1,0:T(8,128)(2,1)} %collective-permute-done.9.above_ref.far_above_ref, ...), custom_call_target="tpu_custom_call", output_to_operand_aliasing={{0}: (6, {}), {1}: (7, {}), {2}: (8, {})} | custom-call | tf_op jit(solution)/shard_map/conv_norm/pallas_call | solution.py:811
  71.9 0.0 collective-permute-done.7.refs_1_
  72.0 0.6 collective-permute-start.12
  72.5 0.1 collective-permute-start.14
  72.6 11.9 %conv_norm.5 = (f32[32,144,384]{2,1,0:T(8,128)}, f32[32,144,128]{2,1,0:T(8,128)}, bf16[32,6,24,384]{3,2,1,0:T(8,128)(2,1)}) custom-call(s32[94]{0:T(128)} %get-tuple-element.162.table_ref, bf16[20,3,24,384]{3,2,1,0:T(8,128)(2,1)} %collective-permute-done.9.above_ref.far_above_ref, ...), custom_call_target="tpu_custom_call", output_to_operand_aliasing={{0}: (6, {}), {1}: (7, {}), {2}: (8, {})} | custom-call | tf_op jit(solution)/shard_map/conv_norm/pallas_call | solution.py:811
  84.5 0.0 collective-permute-done.11.refs_4_
  84.5 0.0 collective-permute-done.14.refs_7_
  84.5 49.7 %mlp.1 = (bf16[32,6,24,384]{3,2,1,0:T(8,128)(2,1)}, bf16[32,6,24,384]{3,2,1,0:T(8,128)(2,1)}, bf16[32,3,24,384]{3,2,1,0:T(8,128)(2,1)}, bf16[32,3,24,384]{3,2,1,...) custom-call(s32[94]{0:T(128)} %get-tuple-element.162.table_ref, ...), custom_call_target="tpu_custom_call" | custom-call | tf_op jit(solution)/shard_map/mlp/pallas_call | solution.py:702
  134.3 0.5 collective-permute-start.15
  134.8 3.2 %collective-permute-start.20 = (bf16[32,3,24,384]{3,2,1,0:T(8,128)(2,1)}, bf16[32,3,24,384]{3,2,1,0:T(8,128)(2,1)}, u32[]{:S(2)}, u32[]{:S(2)}) collective-permute-start(bf16[32,3,24,384]{3,2,1,0:T(8,128)(2,1)} %get-tuple-element.148), channel_id=1, source_target_pairs={{0,1},{1,2},{2,3},{4,5},{5,6},{6,7},{8,9},{9,10},{10,11},{12,13},{... | collective-permute-start | bytes 5308424 | tf_op jit(solution)/shard_map/ppermute | solution.py:937
  138.0 1.3 collective-permute-start.21
  139.3 1.0 copy-done
  140.3 2.0 add_convert_fusion
  142.3 0.0 collective-permute-start.17
  142.3 1.6 collective-permute-start.16
  144.0 15.5 %taps_grad.1 = f32[32,8,128]{2,1,0:T(8,128)} custom-call(s32[94]{0:T(128)} %get-tuple-element.162.table_ref, bf16[12,3,24,384]{3,2,1,0:T(8,128)(2,1)} %collective-permute-done.5.above_ref, bf16[32,6,24,384]{3,2,1,0:T(8,128)(2,1)} %image_ref.5, bf16[12,3,24,384]{3,2,1,0:T(8,128)(2,1)} %collective-permute-done.6.below_ref, ...), custom_call_target="tpu_custom_call" | custom-call | tf_op jit(solution)/shard_map/taps_grad/pallas_call | solution.py:832
  159.5 3.3 %all-to-all-start.1 = ((f32[32,8,128]{2,1,0:T(8,128)}), f32[32,8,128]{2,1,0:T(8,128)}, u32[]{:S(2)}, u32[]{:S(2)}) async-start(f32[32,8,128]{2,1,0:T(8,128)} %taps_grad.1), calls=%async_computation.1 | async-start | bytes 262144 | tf_op jit(solution)/shard_map/all_to_all | solution.py:982
  162.8 6.2 %collective-permute-done.16.refs_2_ = bf16[192,768]{1,0:T(8,128)(2,1)} collective-permute-done((bf16[192,768]{1,0:T(8,128)(2,1)}, bf16[192,768]{1,0:T(8,128)(2,1)}, u32[]{:S(2)}, u32[]{:S(2)}) %collective-permute-start.16) | collective-permute-done | bytes 294944 | tf_op jit(solution)/shard_map/ppermute | solution.py:948
  169.0 2.1 add_convert_fusion.2
  171.1 0.0 collective-permute-start.19
  171.1 0.0 collective-permute-start.18
  171.1 0.0 collective-permute-done.20.above_ref
  171.1 8.0 %finish.3 = (bf16[32,6,24,384]{3,2,1,0:T(8,128)(2,1)}, bf16[32,6,24,384]{3,2,1,0:T(8,128)(2,1)}) custom-call(s32[94]{0:T(128)} %get-tuple-element.162.table_ref, bf16[32,3,24,384]{3,2,1,0:T(8,128)(2,1)} %collective-permute-done.20.above_ref, bf16[32,6,24,384]{3,2,1,0:T(8,128)(2,1)} %get-tuple-element.142.gc_ref, ...), custom_call_target="tpu_custom_call" | custom-call | tf_op jit(solution)/shard_map/finish/pallas_call | solution.py:863
  179.2 0.0 collective-permute-done.18.refs_3_
  179.2 2.0 add_convert_fusion.4
  181.2 2.2 collective-permute-start.24
  183.3 0.0 collective-permute-start.23
  183.3 2.2 %collective-permute-start.22 = (bf16[48,768]{1,0:T(8,128)(2,1)}, bf16[48,768]{1,0:T(8,128)(2,1)}, u32[]{:S(2)}, u32[]{:S(2)}) collective-permute-start(bf16[48,768]{1,0:T(8,128)(2,1)} %get-tuple-element.192), channel_id=1, source_target_pairs={{0,8},{4,12},{8,0},{12,4},{16,24},{20,28},{24,16},{28,20},{1,9},{5... | collective-permute-start | bytes 221192 | tf_op jit(solution)/shard_map/ppermute | solution.py:948
  185.6 7.2 %finish.4 = (bf16[32,6,24,384]{3,2,1,0:T(8,128)(2,1)}, bf16[32,6,24,384]{3,2,1,0:T(8,128)(2,1)}) custom-call(s32[94]{0:T(128)} %get-tuple-element.162.table_ref, bf16[32,3,24,384]{3,2,1,0:T(8,128)(2,1)} %collective-permute-done.20.above_ref, bf16[32,6,24,384]{3,2,1,0:T(8,128)(2,1)} %get-tuple-element.142.gc_ref, ...), custom_call_target="tpu_custom_call", output_to_operand_aliasing={{0}: (8, {}), {1}: (9, {})} | custom-call | tf_op jit(solution)/shard_map/finish/pallas_call | solution.py:863
  192.8 2.1 add_up.1
  195.0 6.1 %all-to-all-start.2 = ((f32[32,8,128]{2,1,0:T(8,128)}), f32[32,8,128]{2,1,0:T(8,128)}, u32[]{:S(2)}, u32[]{:S(2)}) async-start(f32[32,8,128]{2,1,0:T(8,128)} %get-tuple-element.161), calls=%async_computation.2 | async-start | bytes 262144 | tf_op jit(solution)/shard_map/all_to_all | solution.py:982
  201.0 13.2 %finish.5 = (bf16[32,6,24,384]{3,2,1,0:T(8,128)(2,1)}, bf16[32,6,24,384]{3,2,1,0:T(8,128)(2,1)}) custom-call(s32[94]{0:T(128)} %get-tuple-element.162.table_ref, bf16[32,3,24,384]{3,2,1,0:T(8,128)(2,1)} %collective-permute-done.20.above_ref, bf16[32,6,24,384]{3,2,1,0:T(8,128)(2,1)} %get-tuple-element.142.gc_ref, ...), custom_call_target="tpu_custom_call", output_to_operand_aliasing={{0}: (8, {}), {1}: (9, {})} | custom-call | tf_op jit(solution)/shard_map/finish/pallas_call | solution.py:863
  214.2 2.4 %update.1 = (f32[12,49]{1,0:T(8,128)}, f32[12,49]{1,0:T(8,128)}, f32[12,49]{1,0:T(8,128)}, f32[5,12]{1,0:T(8,128)}, f32[5,12]{1,0:T(8,128)}, /*index=5*/f32[5,12...) custom-call(f32[48,768]{1,0:T(8,128)} %get-tuple-element.167.own_ref, ...), custom_call_target="tpu_custom_call" | custom-call | tf_op jit(solution)/shard_map/update/pallas_call | solution.py:925
  (19 shorter events, 0.0 us)
Async XLA Ops:
  3.1 15.1 %copy-start.1 = (bf16[48,768]{1,0:T(8,128)(2,1)S(1)}, bf16[48,768]{1,0:T(8,128)(2,1)}, u32[]{:S(2)}) copy-start(bf16[48,768]{1,0:T(8,128)(2,1)} %get-tuple-element.106.refs_0_) | copy-start | bytes 221188
  5.6 27.7 %collective-permute-start.6 = (bf16[12,3,24,384]{3,2,1,0:T(8,128)(2,1)}, bf16[12,3,24,384]{3,2,1,0:T(8,128)(2,1)}, u32[]{:S(2)}, u32[]{:S(2)}) collective-permute-start(bf16[12,3,24,384]{3,2,1,0:T(8,128)(2,1)} %get-tuple-element.188), channel_id=1, source_target_pairs={{1,0},{2,1},{3,2},{5,4},{6,5},{7,6},{9,8},{10,9},{11,10},{13,12},{... | collective-permute-start | bytes 1990664 | tf_op jit(solution)/shard_map/ppermute | solution.py:938
  6.9 26.5 %collective-permute-start.5 = (bf16[12,3,24,384]{3,2,1,0:T(8,128)(2,1)}, bf16[12,3,24,384]{3,2,1,0:T(8,128)(2,1)}, u32[]{:S(2)}, u32[]{:S(2)}) collective-permute-start(bf16[12,3,24,384]{3,2,1,0:T(8,128)(2,1)} %get-tuple-element.189), channel_id=1, source_target_pairs={{0,1},{1,2},{2,3},{4,5},{5,6},{6,7},{8,9},{9,10},{10,11},{12,13},{... | collective-permute-start | bytes 1990664 | tf_op jit(solution)/shard_map/ppermute | solution.py:937
  10.8 20.8 %all-to-all-start = ((f32[32,8,128]{2,1,0:T(8,128)}), f32[32,8,128]{2,1,0:T(8,128)}, u32[]{:S(2)}, u32[]{:S(2)}) async-start(f32[32,8,128]{2,1,0:T(8,128)} %get-tuple-element.104), calls=%async_computation | async-start | bytes 262144 | tf_op jit(solution)/shard_map/all_to_all | solution.py:982
  18.3 8.7 %collective-permute-start.2 = (bf16[48,768]{1,0:T(8,128)(2,1)S(1)}, bf16[48,768]{1,0:T(8,128)(2,1)S(1)}, u32[]{:S(2)}, u32[]{:S(2)}) collective-permute-start(bf16[48,768]{1,0:T(8,128)(2,1)S(1)} %copy-done.1), channel_id=1, source_target_pairs={{0,24},{4,28},{8,16},{12,20},{16,8},{20,12},{24,0},{28,4},{1,25},{... | collective-permute-start | bytes 221192 | tf_op jit(solution)/shard_map/ppermute | solution.py:948
  21.9 9.1 %collective-permute-start.1 = (bf16[48,768]{1,0:T(8,128)(2,1)S(1)}, bf16[48,768]{1,0:T(8,128)(2,1)S(1)}, u32[]{:S(2)}, u32[]{:S(2)}) collective-permute-start(bf16[48,768]{1,0:T(8,128)(2,1)S(1)} %copy-done.1), channel_id=1, source_target_pairs={{0,16},{4,20},{8,24},{12,28},{16,0},{20,4},{24,8},{28,12},{1,17},{... | collective-permute-start | bytes 221192 | tf_op jit(solution)/shard_map/ppermute | solution.py:948
  21.9 9.8 %collective-permute-start = (bf16[48,768]{1,0:T(8,128)(2,1)S(1)}, bf16[48,768]{1,0:T(8,128)(2,1)}, u32[]{:S(2)}, u32[]{:S(2)}) collective-permute-start(bf16[48,768]{1,0:T(8,128)(2,1)S(1)} %copy-done.1), channel_id=1, source_target_pairs={{0,8},{4,12},{8,0},{12,4},{16,24},{20,28},{24,16},{28,20},{1,9},{5... | collective-permute-start | bytes 221192 | tf_op jit(solution)/shard_map/ppermute | solution.py:948
  27.0 4.0 %copy-start.2 = (bf16[48,768]{1,0:T(8,128)(2,1)}, bf16[48,768]{1,0:T(8,128)(2,1)S(1)}, u32[]{:S(2)}) copy-start(bf16[48,768]{1,0:T(8,128)(2,1)S(1)} %collective-permute-done.2.refs_3_) | copy-start | bytes 221188
  31.0 0.6 copy-start.3
  36.7 26.3 %collective-permute-start.10 = (bf16[20,3,24,384]{3,2,1,0:T(8,128)(2,1)}, bf16[20,3,24,384]{3,2,1,0:T(8,128)(2,1)}, u32[]{:S(2)}, u32[]{:S(2)}) collective-permute-start(bf16[20,3,24,384]{3,2,1,0:T(8,128)(2,1)} %get-tuple-element.186), channel_id=1, source_target_pairs={{1,0},{2,1},{3,2},{5,4},{6,5},{7,6},{9,8},{10,9},{11,10},{13,12},{... | collective-permute-start | bytes 3317768 | tf_op jit(solution)/shard_map/ppermute | solution.py:938
  38.0 25.0 %collective-permute-start.9 = (bf16[20,3,24,384]{3,2,1,0:T(8,128)(2,1)}, bf16[20,3,24,384]{3,2,1,0:T(8,128)(2,1)}, u32[]{:S(2)}, u32[]{:S(2)}) collective-permute-start(bf16[20,3,24,384]{3,2,1,0:T(8,128)(2,1)} %get-tuple-element.187), channel_id=1, source_target_pairs={{0,1},{1,2},{2,3},{4,5},{5,6},{6,7},{8,9},{9,10},{10,11},{12,13},{... | collective-permute-start | bytes 3317768 | tf_op jit(solution)/shard_map/ppermute | solution.py:937
  42.0 15.2 %collective-permute-start.3 = (bf16[96,768]{1,0:T(8,128)(2,1)}, bf16[96,768]{1,0:T(8,128)(2,1)}, u32[]{:S(2)}, u32[]{:S(2)}) collective-permute-start(bf16[96,768]{1,0:T(8,128)(2,1)} %get-tuple-element.110.refs_0_), channel_id=1, source_target_pairs={{0,4},{4,0},{8,12},{12,8},{16,20},{20,16},{24,28},{28,24},{1,5},{5... | collective-permute-start | bytes 442376 | tf_op jit(solution)/shard_map/ppermute | solution.py:948
  43.5 13.8 %collective-permute-start.4 = (bf16[96,768]{1,0:T(8,128)(2,1)}, bf16[96,768]{1,0:T(8,128)(2,1)}, u32[]{:S(2)}, u32[]{:S(2)}) collective-permute-start(bf16[96,768]{1,0:T(8,128)(2,1)} %get-tuple-element.111.refs_2_), channel_id=1, source_target_pairs={{0,2},{1,3},{2,0},{3,1},{4,6},{5,7},{6,4},{7,5},{8,10},{9,11},{10,... | collective-permute-start | bytes 442376 | tf_op jit(solution)/shard_map/ppermute | solution.py:948
  59.2 12.7 %collective-permute-start.7 = (bf16[192,768]{1,0:T(8,128)(2,1)}, bf16[192,768]{1,0:T(8,128)(2,1)}, u32[]{:S(2)}, u32[]{:S(2)}) collective-permute-start(bf16[192,768]{1,0:T(8,128)(2,1)} %get-tuple-element.119.refs_0_), channel_id=1, source_target_pairs={{0,2},{1,3},{2,0},{3,1},{4,6},{5,7},{6,4},{7,5},{8,10},{9,11},{10,... | collective-permute-start | bytes 884744 | tf_op jit(solution)/shard_map/ppermute | solution.py:948
  59.7 12.3 %collective-permute-start.8 = (bf16[192,768]{1,0:T(8,128)(2,1)}, bf16[192,768]{1,0:T(8,128)(2,1)}, u32[]{:S(2)}, u32[]{:S(2)}) collective-permute-start(bf16[192,768]{1,0:T(8,128)(2,1)} %get-tuple-element.120.refs_2_), channel_id=1, source_target_pairs={{0,4},{4,0},{8,12},{12,8},{16,20},{20,16},{24,28},{28,24},{1,5},{5... | collective-permute-start | bytes 884744 | tf_op jit(solution)/shard_map/ppermute | solution.py:948
  62.0 22.5 %collective-permute-start.11 = (bf16[192,768]{1,0:T(8,128)(2,1)}, bf16[192,768]{1,0:T(8,128)(2,1)}, u32[]{:S(2)}, u32[]{:S(2)}) collective-permute-start(bf16[192,768]{1,0:T(8,128)(2,1)} %get-tuple-element.119.refs_0_), channel_id=1, source_target_pairs={{0,1},{1,0},{2,3},{3,2},{4,5},{5,4},{6,7},{7,6},{8,9},{9,8},{10,11... | collective-permute-start | bytes 884744 | tf_op jit(solution)/shard_map/ppermute | solution.py:948
  63.0 21.5 %collective-permute-start.13 = (bf16[192,768]{1,0:T(8,128)(2,1)}, bf16[192,768]{1,0:T(8,128)(2,1)}, u32[]{:S(2)}, u32[]{:S(2)}) collective-permute-start(bf16[192,768]{1,0:T(8,128)(2,1)} %get-tuple-element.120.refs_2_), channel_id=1, source_target_pairs={{0,1},{1,0},{2,3},{3,2},{4,5},{5,4},{6,7},{7,6},{8,9},{9,8},{10,11... | collective-permute-start | bytes 884744 | tf_op jit(solution)/shard_map/ppermute | solution.py:948
  72.0 12.6 %collective-permute-start.12 = (bf16[192,768]{1,0:T(8,128)(2,1)}, bf16[192,768]{1,0:T(8,128)(2,1)}, u32[]{:S(2)}, u32[]{:S(2)}) collective-permute-start(bf16[192,768]{1,0:T(8,128)(2,1)} %collective-permute-done.7.refs_1_), channel_id=1, source_target_pairs={{0,1},{1,0},{2,3},{3,2},{4,5},{5,4},{6,7},{7,6},{8,9},{9,8},{10,11... | collective-permute-start | bytes 884744 | tf_op jit(solution)/shard_map/ppermute | solution.py:948
  72.5 12.0 %collective-permute-start.14 = (bf16[192,768]{1,0:T(8,128)(2,1)}, bf16[192,768]{1,0:T(8,128)(2,1)}, u32[]{:S(2)}, u32[]{:S(2)}) collective-permute-start(bf16[192,768]{1,0:T(8,128)(2,1)} %collective-permute-done.8.refs_3_), channel_id=1, source_target_pairs={{0,1},{1,0},{2,3},{3,2},{4,5},{5,4},{6,7},{7,6},{8,9},{9,8},{10,11... | collective-permute-start | bytes 884744 | tf_op jit(solution)/shard_map/ppermute | solution.py:948
  134.3 5.0 %collective-permute-start.15 = (bf16[768,768]{1,0:T(8,128)(2,1)}, bf16[768,768]{1,0:T(8,128)(2,1)S(1)}, u32[]{:S(2)}, u32[]{:S(2)}) collective-permute-start(bf16[768,768]{1,0:T(8,128)(2,1)} %get-tuple-element.140), channel_id=1, source_target_pairs={{0,1},{1,0},{2,3},{3,2},{4,5},{5,4},{6,7},{7,6},{8,9},{9,8},{10,11... | collective-permute-start | bytes 3538952 | tf_op jit(solution)/shard_map/ppermute | solution.py:948
  134.8 36.3 %collective-permute-start.20 = (bf16[32,3,24,384]{3,2,1,0:T(8,128)(2,1)}, bf16[32,3,24,384]{3,2,1,0:T(8,128)(2,1)}, u32[]{:S(2)}, u32[]{:S(2)}) collective-permute-start(bf16[32,3,24,384]{3,2,1,0:T(8,128)(2,1)} %get-tuple-element.148), channel_id=1, source_target_pairs={{0,1},{1,2},{2,3},{4,5},{5,6},{6,7},{8,9},{9,10},{10,11},{12,13},{... | collective-permute-start | bytes 5308424 | tf_op jit(solution)/shard_map/ppermute | solution.py:937
  138.0 33.1 %collective-permute-start.21 = (bf16[32,3,24,384]{3,2,1,0:T(8,128)(2,1)}, bf16[32,3,24,384]{3,2,1,0:T(8,128)(2,1)}, u32[]{:S(2)}, u32[]{:S(2)}) collective-permute-start(bf16[32,3,24,384]{3,2,1,0:T(8,128)(2,1)} %get-tuple-element.149), channel_id=1, source_target_pairs={{1,0},{2,1},{3,2},{5,4},{6,5},{7,6},{9,8},{10,9},{11,10},{13,12},{... | collective-permute-start | bytes 5308424 | tf_op jit(solution)/shard_map/ppermute | solution.py:938
  139.3 1.0 copy-start
  142.3 20.5 %collective-permute-start.17 = (bf16[192,768]{1,0:T(8,128)(2,1)}, bf16[192,768]{1,0:T(8,128)(2,1)}, u32[]{:S(2)}, u32[]{:S(2)}) collective-permute-start(bf16[192,768]{1,0:T(8,128)(2,1)} %get-tuple-element.195), channel_id=1, source_target_pairs={{0,4},{4,0},{8,12},{12,8},{16,20},{20,16},{24,28},{28,24},{1,5},{5... | collective-permute-start | bytes 884744 | tf_op jit(solution)/shard_map/ppermute | solution.py:948
  142.3 26.7 %collective-permute-start.16 = (bf16[192,768]{1,0:T(8,128)(2,1)}, bf16[192,768]{1,0:T(8,128)(2,1)}, u32[]{:S(2)}, u32[]{:S(2)}) collective-permute-start(bf16[192,768]{1,0:T(8,128)(2,1)} %get-tuple-element.196), channel_id=1, source_target_pairs={{0,2},{1,3},{2,0},{3,1},{4,6},{5,7},{6,4},{7,5},{8,10},{9,11},{10,... | collective-permute-start | bytes 884744 | tf_op jit(solution)/shard_map/ppermute | solution.py:948
  159.5 19.6 %all-to-all-start.1 = ((f32[32,8,128]{2,1,0:T(8,128)}), f32[32,8,128]{2,1,0:T(8,128)}, u32[]{:S(2)}, u32[]{:S(2)}) async-start(f32[32,8,128]{2,1,0:T(8,128)} %taps_grad.1), calls=%async_computation.1 | async-start | bytes 262144 | tf_op jit(solution)/shard_map/all_to_all | solution.py:982
  171.1 8.1 %collective-permute-start.19 = (bf16[96,768]{1,0:T(8,128)(2,1)}, bf16[96,768]{1,0:T(8,128)(2,1)}, u32[]{:S(2)}, u32[]{:S(2)}) collective-permute-start(bf16[96,768]{1,0:T(8,128)(2,1)} %get-tuple-element.193), channel_id=1, source_target_pairs={{0,2},{1,3},{2,0},{3,1},{4,6},{5,7},{6,4},{7,5},{8,10},{9,11},{10,... | collective-permute-start | bytes 442376 | tf_op jit(solution)/shard_map/ppermute | solution.py:948
  171.1 8.1 %collective-permute-start.18 = (bf16[96,768]{1,0:T(8,128)(2,1)}, bf16[96,768]{1,0:T(8,128)(2,1)}, u32[]{:S(2)}, u32[]{:S(2)}) collective-permute-start(bf16[96,768]{1,0:T(8,128)(2,1)} %get-tuple-element.194), channel_id=1, source_target_pairs={{0,4},{4,0},{8,12},{12,8},{16,20},{20,16},{24,28},{28,24},{1,5},{5... | collective-permute-start | bytes 442376 | tf_op jit(solution)/shard_map/ppermute | solution.py:948
  181.2 11.6 %collective-permute-start.24 = (bf16[48,768]{1,0:T(8,128)(2,1)}, bf16[48,768]{1,0:T(8,128)(2,1)}, u32[]{:S(2)}, u32[]{:S(2)}) collective-permute-start(bf16[48,768]{1,0:T(8,128)(2,1)} %get-tuple-element.190), channel_id=1, source_target_pairs={{0,24},{4,28},{8,16},{12,20},{16,8},{20,12},{24,0},{28,4},{1,25},{... | collective-permute-start | bytes 221192 | tf_op jit(solution)/shard_map/ppermute | solution.py:948
  183.3 9.5 %collective-permute-start.23 = (bf16[48,768]{1,0:T(8,128)(2,1)}, bf16[48,768]{1,0:T(8,128)(2,1)}, u32[]{:S(2)}, u32[]{:S(2)}) collective-permute-start(bf16[48,768]{1,0:T(8,128)(2,1)} %get-tuple-element.191), channel_id=1, source_target_pairs={{0,16},{4,20},{8,24},{12,28},{16,0},{20,4},{24,8},{28,12},{1,17},{... | collective-permute-start | bytes 221192 | tf_op jit(solution)/shard_map/ppermute | solution.py:948
  183.3 9.5 %collective-permute-start.22 = (bf16[48,768]{1,0:T(8,128)(2,1)}, bf16[48,768]{1,0:T(8,128)(2,1)}, u32[]{:S(2)}, u32[]{:S(2)}) collective-permute-start(bf16[48,768]{1,0:T(8,128)(2,1)} %get-tuple-element.192), channel_id=1, source_target_pairs={{0,8},{4,12},{8,0},{12,4},{16,24},{20,28},{24,16},{28,20},{1,9},{5... | collective-permute-start | bytes 221192 | tf_op jit(solution)/shard_map/ppermute | solution.py:948
  195.0 19.2 %all-to-all-start.2 = ((f32[32,8,128]{2,1,0:T(8,128)}), f32[32,8,128]{2,1,0:T(8,128)}, u32[]{:S(2)}, u32[]{:S(2)}) async-start(f32[32,8,128]{2,1,0:T(8,128)} %get-tuple-element.161), calls=%async_computation.2 | async-start | bytes 262144 | tf_op jit(solution)/shard_map/all_to_all | solution.py:982
